TPU v7x, 32 devices: a whole 2x2x4 slice. The times are simulated.
32 devices in a mesh: dp: 4 (over y, core), fsdp: 8 (over z, x).
Axes of the slice: x: 2, y: 2, z: 4, core: 2. Of those that a mesh axis runs over, the one named last changes fastest.
Arguments:
- hidden_in: bfloat16 [2, 32, 128, 1024], P(None, ('dp', 'fsdp')), may hold values from -6 to 6
- memory: bfloat16 [2, 32, 588, 1024], P(None, ('dp', 'fsdp')), may hold values from -6 to 6
- cotangent: bfloat16 [2, 32, 128, 1024], P(None, ('dp', 'fsdp')), may hold values from -6 to 6
- lengths: int32 [2, 32], P(None, ('dp', 'fsdp')), may hold values from 32 to 128, as said below
- memory_count: int32 [2, 32], P(None, ('dp', 'fsdp')), may hold values from 147 to 588, as said below
- causal_gain: bfloat16 [1024], P(('dp', 'fsdp')), may hold values from 0.5 to 1.5
- causal_query: bfloat16 [1024, 1024], P(('dp', 'fsdp')), may hold values from -0.1875 to 0.1875
- causal_key: bfloat16 [1024, 1024], P(('dp', 'fsdp')), may hold values from -0.1875 to 0.1875
- causal_value: bfloat16 [1024, 1024], P(('dp', 'fsdp')), may hold values from -0.1875 to 0.1875
- causal_output: bfloat16 [1024, 1024], P(('dp', 'fsdp')), may hold values from -1.5 to 1.5
- source_gain: bfloat16 [1024], P(('dp', 'fsdp')), may hold values from 0.5 to 1.5
- source_query: bfloat16 [1024, 1024], P(('dp', 'fsdp')), may hold values from -0.1875 to 0.1875
- source_key: bfloat16 [1024, 1024], P(('dp', 'fsdp')), may hold values from -0.1875 to 0.1875
- source_value: bfloat16 [1024, 1024], P(('dp', 'fsdp')), may hold values from -0.1875 to 0.1875
- source_output: bfloat16 [1024, 1024], P(('dp', 'fsdp')), may hold values from -1.5 to 1.5
- dense_gain: bfloat16 [1024], P(('dp', 'fsdp')), may hold values from 0.5 to 1.5
- dense_expand: bfloat16 [1024, 4096], P(('dp', 'fsdp')), may hold values from -0.1875 to 0.1875
- dense_reduce: bfloat16 [4096, 1024], P(('dp', 'fsdp')), may hold values from -0.09375 to 0.09375
Outputs:
- hidden_out: bfloat16 [2, 32, 128, 1024], P(None, ('dp', 'fsdp'))
- input_gradient: float32 [2, 32, 128, 1024], P(None, ('dp', 'fsdp'))
- memory_gradient: float32 [2, 32, 588, 1024], P(None, ('dp', 'fsdp'))
- causal_gain_gradient: float32 [1024], P(('dp', 'fsdp'))
- causal_query_gradient: float32 [1024, 1024], P(('dp', 'fsdp'))
- causal_key_gradient: float32 [1024, 1024], P(('dp', 'fsdp'))
- causal_value_gradient: float32 [1024, 1024], P(('dp', 'fsdp'))
- causal_output_gradient: float32 [1024, 1024], P(('dp', 'fsdp'))
- source_gain_gradient: float32 [1024], P(('dp', 'fsdp'))
- source_query_gradient: float32 [1024, 1024], P(('dp', 'fsdp'))
- source_key_gradient: float32 [1024, 1024], P(('dp', 'fsdp'))
- source_value_gradient: float32 [1024, 1024], P(('dp', 'fsdp'))
- source_output_gradient: float32 [1024, 1024], P(('dp', 'fsdp'))
- dense_gain_gradient: float32 [1024], P(('dp', 'fsdp'))
- dense_expand_gradient: float32 [1024, 4096], P(('dp', 'fsdp'))
- dense_reduce_gradient: float32 [4096, 1024], P(('dp', 'fsdp'))
Inputs may be any that keep to these rules, and one draw needn't show every extreme that they name: `lengths`: each micro-batch has a page of exactly 128 tokens. `memory_count`: each value is 147 or 588; both occur in every draw.
All inputs are finite; a program needn't handle non-finite values.
Results may differ from a plain program's by a relative error of at most 0.019.
Values may be sent and summed in bfloat16 or wider, within the bound.
A program may use at most 384 MiB of HBM per device.

v0:
```python
import jax
import jax.numpy as jnp
from jax import lax
from jax.sharding import PartitionSpec as P

HD = 64


EPS = 1e-05


def split_heads(value):
    return value.reshape(value.shape[0], value.shape[1], -1, HD)


def project(left, weight):
    return jnp.einsum("bld,de->ble", left, weight, preferred_element_type=jnp.float32)


def project_back(grad, weight):
    return jnp.einsum("ble,de->bld", grad, weight, preferred_element_type=jnp.float32)


def outer_sum(left, grad):
    return jnp.einsum("bld,ble->de", left, grad, preferred_element_type=jnp.float32)


def normalize(value, gain):
    centred = value - jnp.mean(value, axis=-1, keepdims=True)
    spread = jnp.mean(centred * centred, axis=-1, keepdims=True)
    scale_row = lax.rsqrt(spread + EPS)
    unit = centred * scale_row
    return (unit * gain, unit, scale_row)


def normalize_back(grad, unit, scale_row, gain):
    grad_unit = grad * gain
    grad_gain = jnp.sum(grad * unit, axis=(0, 1))
    centred = grad_unit - jnp.mean(grad_unit, axis=-1, keepdims=True)
    grad_input = scale_row * (centred - unit * jnp.mean(grad_unit * unit, axis=-1, keepdims=True))
    return (grad_input, grad_gain)


def masked_scores(queries, keys, allowed):
    scores = jnp.einsum(
        "bqhd,bkhd->bhqk",
        split_heads(queries),
        split_heads(keys),
        preferred_element_type=jnp.float32,
    ) * HD ** (-0.5)
    return jnp.where(allowed[:, None], scores, -1000000000.0)


def attend(queries, keys, values, allowed):
    scores = masked_scores(queries, keys, allowed)
    top = jnp.max(scores, axis=-1, keepdims=True)
    expos = jnp.exp(scores - top)
    total = jnp.sum(expos, axis=-1, keepdims=True)
    probs = (expos / total).astype(jnp.bfloat16)
    context = jnp.einsum(
        "bhqk,bkhd->bqhd", probs, split_heads(values), preferred_element_type=jnp.float32
    )
    return (context.reshape(queries.shape).astype(jnp.bfloat16), top + jnp.log(total))


def attend_back(queries, keys, values, allowed, logsum, grad_context):
    probs = jnp.exp(masked_scores(queries, keys, allowed) - logsum)
    grad_heads = split_heads(grad_context)
    grad_values = jnp.einsum(
        "bhqk,bqhd->bkhd",
        probs.astype(jnp.bfloat16),
        grad_heads,
        preferred_element_type=jnp.float32,
    )
    grad_probs = jnp.einsum(
        "bqhd,bkhd->bhqk", grad_heads, split_heads(values), preferred_element_type=jnp.float32
    )
    inner = jnp.sum(probs * grad_probs, axis=-1, keepdims=True)
    grad_scores = (probs * (grad_probs - inner)).astype(jnp.bfloat16)
    scale = HD ** (-0.5)
    grad_queries = (
        jnp.einsum(
            "bhqk,bkhd->bqhd", grad_scores, split_heads(keys), preferred_element_type=jnp.float32
        )
        * scale
    )
    grad_keys = (
        jnp.einsum(
            "bhqk,bqhd->bkhd", grad_scores, split_heads(queries), preferred_element_type=jnp.float32
        )
        * scale
    )
    return (
        grad_queries.reshape(queries.shape).astype(jnp.bfloat16),
        grad_keys.reshape(keys.shape).astype(jnp.bfloat16),
        grad_values.reshape(values.shape).astype(jnp.bfloat16),
    )


def sum_gradients(block):
    owners = lax.axis_size("dp") * lax.axis_size("fsdp")
    shapes = [member.shape for member in block]
    flats = [member.reshape(owners, -1) for member in block]
    widths = [flat.shape[1] for flat in flats]
    joined = jnp.concatenate(flats, axis=1)
    summed = lax.psum_scatter(joined, ("dp", "fsdp"), scatter_dimension=0, tiled=True)
    pieces = []
    offset = 0
    for shape, width in zip(shapes, widths):
        piece = summed[0, offset : offset + width]
        pieces.append(piece.reshape((shape[0] // owners,) + tuple(shape[1:])))
        offset = offset + width
    return pieces


def per_device(
    hidden_in,
    memory,
    cotangent,
    lengths,
    memory_count,
    causal_gain,
    causal_query,
    causal_key,
    causal_value,
    causal_output,
    source_gain,
    source_query,
    source_key,
    source_value,
    source_output,
    dense_gain,
    dense_expand,
    dense_reduce,
):
    inputs = hidden_in[:, 0].astype(jnp.float32)
    source = memory[:, 0]
    page_length = lengths[:, 0]
    page_count = memory_count[:, 0]
    rows = inputs.shape[1]
    slots = source.shape[1]
    places = jnp.arange(rows)
    causal_mask = (places[None, None, :] <= places[None, :, None]) & (
        places[None, None, :] < page_length[:, None, None]
    )
    source_mask = jnp.arange(slots)[None, None, :] < page_count[:, None, None]
    causal_block = (
        lax.all_gather(causal_gain, ("dp", "fsdp"), axis=0, tiled=True),
        lax.all_gather(causal_query, ("dp", "fsdp"), axis=0, tiled=True),
        lax.all_gather(causal_key, ("dp", "fsdp"), axis=0, tiled=True),
        lax.all_gather(causal_value, ("dp", "fsdp"), axis=0, tiled=True),
        lax.all_gather(causal_output, ("dp", "fsdp"), axis=0, tiled=True),
    )
    gain_one = causal_block[0].astype(jnp.float32)
    normed, unit_one, scale_one = normalize(inputs, gain_one)
    first = normed.astype(jnp.bfloat16)
    queries = project(first, causal_block[1]).astype(jnp.bfloat16)
    keys = project(first, causal_block[2]).astype(jnp.bfloat16)
    values = project(first, causal_block[3]).astype(jnp.bfloat16)
    context, logsum_self = attend(queries, keys, values, causal_mask)
    after_self = inputs + project(context, causal_block[4])
    source_block = (
        lax.all_gather(source_gain, ("dp", "fsdp"), axis=0, tiled=True),
        lax.all_gather(source_query, ("dp", "fsdp"), axis=0, tiled=True),
        lax.all_gather(source_key, ("dp", "fsdp"), axis=0, tiled=True),
        lax.all_gather(source_value, ("dp", "fsdp"), axis=0, tiled=True),
        lax.all_gather(source_output, ("dp", "fsdp"), axis=0, tiled=True),
    )
    gain_two = source_block[0].astype(jnp.float32)
    normed, unit_two, scale_two = normalize(after_self, gain_two)
    second = normed.astype(jnp.bfloat16)
    cross_queries = project(second, source_block[1]).astype(jnp.bfloat16)
    memory_keys = project(source, source_block[2]).astype(jnp.bfloat16)
    memory_values = project(source, source_block[3]).astype(jnp.bfloat16)
    cross_context, logsum_cross = attend(cross_queries, memory_keys, memory_values, source_mask)
    after_cross = after_self + project(cross_context, source_block[4])
    dense_block = (
        lax.all_gather(dense_gain, ("dp", "fsdp"), axis=0, tiled=True),
        lax.all_gather(dense_expand, ("dp", "fsdp"), axis=0, tiled=True),
        lax.all_gather(dense_reduce, ("dp", "fsdp"), axis=0, tiled=True),
    )
    gain_three = dense_block[0].astype(jnp.float32)
    normed, unit_three, scale_three = normalize(after_cross, gain_three)
    third = normed.astype(jnp.bfloat16)
    hidden_pre = project(third, dense_block[1])
    hidden = jax.nn.gelu(hidden_pre, approximate=False).astype(jnp.bfloat16)
    result = after_cross + project(hidden, dense_block[2])
    grad_out = cotangent[:, 0].astype(jnp.float32)
    dense_block = (
        lax.all_gather(dense_gain, ("dp", "fsdp"), axis=0, tiled=True),
        lax.all_gather(dense_expand, ("dp", "fsdp"), axis=0, tiled=True),
        lax.all_gather(dense_reduce, ("dp", "fsdp"), axis=0, tiled=True),
    )
    grad_branch = grad_out.astype(jnp.bfloat16)
    grad_reduce = outer_sum(hidden, grad_branch)
    grad_hidden = project_back(grad_branch, dense_block[2])
    gelu_value, gelu_pull = jax.vjp(lambda v: jax.nn.gelu(v, approximate=False), hidden_pre)
    grad_pre = gelu_pull(grad_hidden)[0].astype(jnp.bfloat16)
    grad_expand = outer_sum(third, grad_pre)
    grad_norm, grad_gain_three = normalize_back(
        project_back(grad_pre, dense_block[1]),
        unit_three,
        scale_three,
        dense_block[0].astype(jnp.float32),
    )
    grad_cross = grad_out + grad_norm
    dense_sums = sum_gradients((grad_gain_three, grad_expand, grad_reduce))
    source_block = (
        lax.all_gather(source_gain, ("dp", "fsdp"), axis=0, tiled=True),
        lax.all_gather(source_query, ("dp", "fsdp"), axis=0, tiled=True),
        lax.all_gather(source_key, ("dp", "fsdp"), axis=0, tiled=True),
        lax.all_gather(source_value, ("dp", "fsdp"), axis=0, tiled=True),
        lax.all_gather(source_output, ("dp", "fsdp"), axis=0, tiled=True),
    )
    grad_branch = grad_cross.astype(jnp.bfloat16)
    grad_source_output = outer_sum(cross_context, grad_branch)
    grad_context = project_back(grad_branch, source_block[4]).astype(jnp.bfloat16)
    grad_cq, grad_mk, grad_mv = attend_back(
        cross_queries, memory_keys, memory_values, source_mask, logsum_cross, grad_context
    )
    grad_source_query = outer_sum(second, grad_cq)
    grad_source_key = outer_sum(source, grad_mk)
    grad_source_value = outer_sum(source, grad_mv)
    grad_memory = project_back(grad_mk, source_block[2]) + project_back(grad_mv, source_block[3])
    grad_norm, grad_gain_two = normalize_back(
        project_back(grad_cq, source_block[1]),
        unit_two,
        scale_two,
        source_block[0].astype(jnp.float32),
    )
    grad_self = grad_cross + grad_norm
    source_sums = sum_gradients(
        (grad_gain_two, grad_source_query, grad_source_key, grad_source_value, grad_source_output)
    )
    causal_block = (
        lax.all_gather(causal_gain, ("dp", "fsdp"), axis=0, tiled=True),
        lax.all_gather(causal_query, ("dp", "fsdp"), axis=0, tiled=True),
        lax.all_gather(causal_key, ("dp", "fsdp"), axis=0, tiled=True),
        lax.all_gather(causal_value, ("dp", "fsdp"), axis=0, tiled=True),
        lax.all_gather(causal_output, ("dp", "fsdp"), axis=0, tiled=True),
    )
    grad_branch = grad_self.astype(jnp.bfloat16)
    grad_causal_output = outer_sum(context, grad_branch)
    grad_context = project_back(grad_branch, causal_block[4]).astype(jnp.bfloat16)
    grad_q, grad_k, grad_v = attend_back(
        queries, keys, values, causal_mask, logsum_self, grad_context
    )
    grad_causal_query = outer_sum(first, grad_q)
    grad_causal_key = outer_sum(first, grad_k)
    grad_causal_value = outer_sum(first, grad_v)
    grad_first = (
        project_back(grad_q, causal_block[1])
        + project_back(grad_k, causal_block[2])
        + project_back(grad_v, causal_block[3])
    )
    grad_norm, grad_gain_one = normalize_back(
        grad_first, unit_one, scale_one, causal_block[0].astype(jnp.float32)
    )
    grad_inputs = grad_self + grad_norm
    causal_sums = sum_gradients(
        (grad_gain_one, grad_causal_query, grad_causal_key, grad_causal_value, grad_causal_output)
    )
    return (
        result.astype(jnp.bfloat16)[:, None],
        grad_inputs[:, None],
        grad_memory[:, None],
        causal_sums[0],
        causal_sums[1],
        causal_sums[2],
        causal_sums[3],
        causal_sums[4],
        source_sums[0],
        source_sums[1],
        source_sums[2],
        source_sums[3],
        source_sums[4],
        dense_sums[0],
        dense_sums[1],
        dense_sums[2],
    )


def solution(mesh):
    return jax.shard_map(
        per_device,
        mesh=mesh,
        in_specs=(
            P(None, ("dp", "fsdp"), None, None),
            P(None, ("dp", "fsdp"), None, None),
            P(None, ("dp", "fsdp"), None, None),
            P(None, ("dp", "fsdp")),
            P(None, ("dp", "fsdp")),
            P(("dp", "fsdp")),
            P(("dp", "fsdp"), None),
            P(("dp", "fsdp"), None),
            P(("dp", "fsdp"), None),
            P(("dp", "fsdp"), None),
            P(("dp", "fsdp")),
            P(("dp", "fsdp"), None),
            P(("dp", "fsdp"), None),
            P(("dp", "fsdp"), None),
            P(("dp", "fsdp"), None),
            P(("dp", "fsdp")),
            P(("dp", "fsdp"), None),
            P(("dp", "fsdp"), None),
        ),
        out_specs=(
            P(None, ("dp", "fsdp"), None, None),
            P(None, ("dp", "fsdp"), None, None),
            P(None, ("dp", "fsdp"), None, None),
            P(("dp", "fsdp")),
            P(("dp", "fsdp"), None),
            P(("dp", "fsdp"), None),
            P(("dp", "fsdp"), None),
            P(("dp", "fsdp"), None),
            P(("dp", "fsdp")),
            P(("dp", "fsdp"), None),
            P(("dp", "fsdp"), None),
            P(("dp", "fsdp"), None),
            P(("dp", "fsdp"), None),
            P(("dp", "fsdp")),
            P(("dp", "fsdp"), None),
            P(("dp", "fsdp"), None),
        ),
        check_vma=False,
    )
```

profile of v0, /device:TPU:0, one launch (start us, length us, event | category | flops | bytes accessed | tf_op | source)
XLA Modules:
  0.0 2044.8 jit_solution(11670728679138672342)
XLA Ops:
  16.6 42.2 %all-reduce.7 = (bf16[1024]{0:T(1024)(128)(2,1)S(1)}, bf16[1024]{0:T(1024)(128)(2,1)S(1)}, bf16[1024]{0:T(1024)(128)(2,1)S(1)}) all-reduce(bf16[1024]{0:T(1024)(128)(2,1)S(1)} %dynamic-update-slice, bf16[1024]{0:T(1024)(128)(2,1)S(1)} %dynamic-update-slice.1, ...), channel_id=1, replica_groups=mesh['dp'=4,'fsdp'=8] {'dp','fsdp'}, use_global_device_ids=true, to_apply=%add | all-reduce | flops 3072 | bytes 12288
  62.9 7.4 all-gather.11.cloned.1.call-done
  73.8 55.0 %all-gather.13.cloned.1.call-done = bf16[1024,1024]{1,0:T(8,128)(2,1)} async-done(((bf16[32,1024]{1,0:T(8,128)(2,1)}), bf16[1024,1024]{1,0:T(8,128)(2,1)}) %all-gather.13.cloned.1.call-update) | async-done | bytes 2097168 | tf_op jit(solution)/shard_map/all_gather | solution.py:149
  131.5 55.7 %all-gather.15.cloned.1.call-done = bf16[1024,1024]{1,0:T(8,128)(2,1)} async-done(((bf16[32,1024]{1,0:T(8,128)(2,1)}), bf16[1024,1024]{1,0:T(8,128)(2,1)}) %all-gather.15.cloned.1.call-update) | async-done | bytes 2097168 | tf_op jit(solution)/shard_map/all_gather | solution.py:150
  189.8 55.6 %all-gather.19.cloned.1.call-done = bf16[1024,1024]{1,0:T(8,128)(2,1)} async-done(((bf16[32,1024]{1,0:T(8,128)(2,1)}), bf16[1024,1024]{1,0:T(8,128)(2,1)}) %all-gather.19.cloned.1.call-update) | async-done | bytes 2097168 | tf_op jit(solution)/shard_map/all_gather | solution.py:166
  258.6 45.1 %all-gather.17.cloned.1.call-done = bf16[1024,1024]{1,0:T(8,128)(2,1)} async-done(((bf16[32,1024]{1,0:T(8,128)(2,1)}), bf16[1024,1024]{1,0:T(8,128)(2,1)}) %all-gather.17.cloned.1.call-update) | async-done | bytes 2097168 | tf_op jit(solution)/shard_map/all_gather | solution.py:152
  306.6 55.3 %all-gather.21.cloned.1.call-done = bf16[1024,1024]{1,0:T(8,128)(2,1)} async-done(((bf16[32,1024]{1,0:T(8,128)(2,1)}), bf16[1024,1024]{1,0:T(8,128)(2,1)}) %all-gather.21.cloned.1.call-update) | async-done | bytes 2097168 | tf_op jit(solution)/shard_map/all_gather | solution.py:164
  367.1 53.2 %all-gather.23.cloned.1.call-done = bf16[1024,1024]{1,0:T(8,128)(2,1)} async-done(((bf16[32,1024]{1,0:T(8,128)(2,1)}), bf16[1024,1024]{1,0:T(8,128)(2,1)}) %all-gather.23.cloned.1.call-update) | async-done | bytes 2097168 | tf_op jit(solution)/shard_map/all_gather | solution.py:165
  443.9 34.9 %all-gather.25.cloned.1.call-done = bf16[1024,1024]{1,0:T(8,128)(2,1)} async-done(((bf16[32,1024]{1,0:T(8,128)(2,1)}), bf16[1024,1024]{1,0:T(8,128)(2,1)}) %all-gather.25.cloned.1.call-update) | async-done | bytes 2097168 | tf_op jit(solution)/shard_map/all_gather | solution.py:167
  482.6 75.4 %all-gather.27.cloned.1.call-done = bf16[1024,4096]{1,0:T(8,128)(2,1)} async-done(((bf16[32,4096]{1,0:T(8,128)(2,1)}), bf16[1024,4096]{1,0:T(8,128)(2,1)}) %all-gather.27.cloned.1.call-update) | async-done | bytes 8388624 | tf_op jit(solution)/shard_map/all_gather | solution.py:179
  558.1 7.4 fusion.136
  567.5 11.0 multiply_convert_fusion.2
  578.5 58.5 %all-gather.29.cloned.1.call-done = bf16[4096,1024]{1,0:T(8,128)(2,1)} async-done(((bf16[128,1024]{1,0:T(8,128)(2,1)}), bf16[4096,1024]{1,0:T(8,128)(2,1)}) %all-gather.29.cloned.1.call-update) | async-done | bytes 8388624 | tf_op jit(solution)/shard_map/all_gather | solution.py:180
  636.9 9.5 add_convert_fusion
  658.5 8.4 multiply_reduce_fusion
  699.9 8.3 convolution_bitcast_fusion.1
  785.7 12.2 reshape.293
  797.9 9.7 convolution_bitcast_fusion
  807.6 12.1 reshape.294
  822.4 14.9 dynamic-update-slice.12
  837.3 14.9 dynamic-update-slice.7
  852.1 14.8 dynamic-update-slice.13
  867.0 14.8 dynamic-update-slice.8
  881.8 14.8 dynamic-update-slice.14
  896.7 14.8 dynamic-update-slice.9
  911.5 14.2 dynamic-update-slice.15
  925.7 14.2 dynamic-update-slice.10
  941.3 48.2 %dynamic-update-slice.4 = f32[32,262176]{1,0:T(8,128)} dynamic-update-slice(f32[32,262176]{1,0:T(8,128)} %dynamic-update-slice.3, f32[32,131072]{1,0:T(8,128)} %reshape.293, s32[]{} %constant.134, s32[]{} %constant.135) | dynamic-update-slice | bytes 33554436
  989.5 47.5 %dynamic-update-slice.5 = f32[32,262176]{1,0:T(8,128)} dynamic-update-slice(f32[32,262176]{1,0:T(8,128)} %dynamic-update-slice.4, f32[32,131072]{1,0:T(8,128)} %reshape.294, s32[]{} %constant.134, s32[]{} %constant.136) | dynamic-update-slice | bytes 33554436 | tf_op jit(solution)/shard_map/concatenate | solution.py:105
  1047.8 9.8 copy.165
  1060.2 7.4 fusion.119
  1067.7 945.0 %all-reduce.10.cloned.1.call-done = (f32[32,131104]{1,0:T(8,128)}, f32[32,131104]{1,0:T(8,128)}, f32[32,262176]{1,0:T(8,128)}) async-done(((f32[32,131104]{1,0:T(8,128)}, f32[32,131104]{1,0:T(8,128)}, f32[32,262176]{1,0:T(8,128)}), (f32[32,131104]{1,0:T(8,128)}, f32[32,131104]{1,0:T(8,128)}, f32[32,262176]{1,0:T(8,128)})) %all-reduce.10.cloned.1.call-update) | async-done | bytes 67121168
  (237 shorter events, 237.3 us)
Async XLA Ops:
  7.2 121.6 %copy-start.2 = (bf16[2,1,128,1024]{3,2,1,0:T(8,128)(2,1)S(1)}, bf16[2,1,128,1024]{3,2,1,0:T(8,128)(2,1)}, u32[]{:S(2)}) copy-start(bf16[2,1,128,1024]{3,2,1,0:T(8,128)(2,1)} %param.18) | copy-start | bytes 1572868
  7.2 63.1 %all-gather.11.cloned.1.call-start = ((), (), s32[]{:S(2)}) async-start(), calls=%async_computation | async-start | bytes 2162688 | tf_op jit(solution)/shard_map/all_gather | solution.py:151
  7.9 120.9 %all-gather.13.cloned.1.call-start = ((), (), s32[]{:S(2)}) async-start(), calls=%async_computation.1 | async-start | bytes 2162688 | tf_op jit(solution)/shard_map/all_gather | solution.py:149
  8.7 178.5 %all-gather.15.cloned.1.call-start = ((), (), s32[]{:S(2)}) async-start(), calls=%async_computation.2 | async-start | bytes 2162688 | tf_op jit(solution)/shard_map/all_gather | solution.py:150
  9.4 236.0 %all-gather.19.cloned.1.call-start = ((), (), s32[]{:S(2)}) async-start(), calls=%async_computation.4 | async-start | bytes 2162688 | tf_op jit(solution)/shard_map/all_gather | solution.py:166
  10.0 293.7 %all-gather.17.cloned.1.call-start = ((), (), s32[]{:S(2)}) async-start(), calls=%async_computation.3 | async-start | bytes 2162688 | tf_op jit(solution)/shard_map/all_gather | solution.py:152
  10.6 351.4 %all-gather.21.cloned.1.call-start = ((), (), s32[]{:S(2)}) async-start(), calls=%async_computation.5 | async-start | bytes 2162688 | tf_op jit(solution)/shard_map/all_gather | solution.py:164
  11.2 409.2 %all-gather.23.cloned.1.call-start = ((), (), s32[]{:S(2)}) async-start(), calls=%async_computation.6 | async-start | bytes 2162688 | tf_op jit(solution)/shard_map/all_gather | solution.py:165
  11.9 466.9 %all-gather.25.cloned.1.call-start = ((), (), s32[]{:S(2)}) async-start(), calls=%async_computation.7 | async-start | bytes 2162688 | tf_op jit(solution)/shard_map/all_gather | solution.py:167
  12.6 545.4 %all-gather.27.cloned.1.call-start = ((), (), s32[]{:S(2)}) async-start(), calls=%async_computation.8 | async-start | bytes 8650752 | tf_op jit(solution)/shard_map/all_gather | solution.py:179
  13.4 623.5 %all-gather.29.cloned.1.call-start = ((), (), s32[]{:S(2)}) async-start(), calls=%async_computation.9 | async-start | bytes 8650752 | tf_op jit(solution)/shard_map/all_gather | solution.py:180
  14.0 1998.7 %all-reduce.10.cloned.1.call-start = ((), (), s32[]{:S(2)}) async-start(), calls=%async_computation.10 | async-start | bytes 134316032
  131.4 124.8 %copy-start.18 = (bf16[2,128,1024]{1,2,0:T(8,128)(2,1)}, bf16[2,128,1024]{1,2,0:T(8,128)(2,1)S(1)}, u32[]{:S(2)}) copy-start(bf16[2,128,1024]{1,2,0:T(8,128)(2,1)S(1)} %copy.126) | copy-start | bytes 1572868
  189.8 66.5 %copy-start.20 = (bf16[2,128,1024]{1,2,0:T(8,128)(2,1)}, bf16[2,128,1024]{1,2,0:T(8,128)(2,1)S(1)}, u32[]{:S(2)}) copy-start(bf16[2,128,1024]{1,2,0:T(8,128)(2,1)S(1)} %copy.127) | copy-start | bytes 1572868
  636.9 9.5 copy-start.6
  646.5 6.9 copy-start.26
  646.5 6.9 copy-start.28
  646.5 8.3 copy-start.16
  658.5 8.4 slice-start
  658.5 8.4 slice-start.1
  658.5 8.4 slice-start.2
  670.0 4.2 copy-start.1
  679.3 4.8 slice-start.6
  681.3 6.1 slice-start.3
  682.0 5.4 slice-start.4
  687.5 4.2 copy-start.9
  699.9 8.3 copy-start.3
  711.1 5.8 copy-start.30
  785.7 12.2 copy-start.29
  1037.0 5.6 copy-start.25
  1037.0 5.6 copy-start.37
  1047.8 9.8 copy-start.10
  (27 other events, 70.5 us)
Sparse Core Ops, SparseCore 0:
  11.0 59.2 all-gather.10
  73.3 55.4 all-gather.12
  131.8 55.3 all-gather.14
  190.0 55.3 all-gather.18
  248.3 55.3 all-gather.16
  306.5 55.3 all-gather.20
  364.9 55.3 all-gather.22
  423.3 55.4 all-gather.24
  481.7 76.2 all-gather.26
  560.9 75.9 all-gather.28
  1037.1 975.5 all-reduce.9
where the time goes:
time: 2060 us; the launch traced here: 2040 us
  waiting for transfers between devices  1450 us (70%)
  local copies, waits for them, and re-layouts  355 us (17%)
  matrix products  159 us (8%)
  blocking collectives  42.2 us (2%)
  other arithmetic  25.4 us (1%)
    unnamed x12, waiting for transfers between devices  951 us
    unnamed x113, local copies, waits for them, and re-layouts  163 us
    concatenate x3, local copies, waits for them, and re-layouts, sum_gradients(): joined = jnp.concatenate(flats, axis=1)  76 us
    all_gather x1, waiting for transfers between devices, per_device(): lax.all_gather(dense_expand, ('dp', 'fsdp'), axis=0, tiled=True)  75.4 us
    reshape x13, local copies, waits for them, and re-layouts, sum_gradients(): flats = [member.reshape(owners, -1) for member in block]  64.3 us
    all_gather x1, waiting for transfers between devices, per_device(): lax.all_gather(dense_reduce, ('dp', 'fsdp'), axis=0, tiled=True)  58.5 us
    all_gather x1, waiting for transfers between devices, per_device(): lax.all_gather(causal_key, ('dp', 'fsdp'), axis=0, tiled=True)  55.7 us
    all_gather x1, waiting for transfers between devices, per_device(): lax.all_gather(source_value, ('dp', 'fsdp'), axis=0, tiled=True)  55.6 us
  transfers between devices with their start and end apart: 11, of which 11 were waited for; matrix products, arithmetic and copies ran while one was open for 5% of the time, Pallas kernels for 0%

commit v1 on v0

v1 whole, which is shorter than its diff:
```python
import jax
import jax.numpy as jnp
from jax import lax
from jax.sharding import PartitionSpec as P

HD = 64
EPS = 1e-05
AXES = ("dp", "fsdp")
CORES = 2


class Grid:
    def __init__(self, dp, fsdp):
        self.y = dp // CORES
        self.x = self.y
        self.z = fsdp // self.x
        self.fsdp = fsdp
        self.devices = dp * fsdp
        d, f = lax.axis_index("dp"), lax.axis_index("fsdp")
        self.at = (d // CORES, d % CORES, f // self.x, f % self.x)

    def index(self, y, c, z, x):
        return (y * CORES + c) * self.fsdp + z * self.x + x

    def send(self, value, move):
        pairs = []
        for y in range(self.y):
            for c in range(CORES):
                for z in range(self.z):
                    for x in range(self.x):
                        pairs.append((self.index(y, c, z, x), self.index(*move(y, c, z, x))))
        return lax.ppermute(value, AXES, pairs)

    def send_core(self, value):
        return self.send(value, lambda y, c, z, x: (y, 1 - c, z, x))

    def send_z(self, value, k):
        return self.send(value, lambda y, c, z, x: (y, c, (z + k) % self.z, x))

    def send_plane(self, value, k, swap):
        def move(y, c, z, x):
            if (c + swap) % 2 == 0:
                return (y, c, z, (x + k) % self.x)
            return ((y + k) % self.y, c, z, x)

        return self.send(value, move)

    def place(self, a, b, core):
        y, _, _, x = self.at
        x_first = core == 0
        ky = jnp.where(x_first, b, a)
        kx = jnp.where(x_first, a, b)
        return (y + ky) % self.y, (x + kx) % self.x


def gather(grid, shard):
    r, cols = shard.shape
    z, n = grid.z, grid.x
    core = grid.at[1]
    line = [shard] + [grid.send_z(shard, k) for k in range(1, z)]
    order = [line[k] for k in range(z - 1, -1, -1)] + [line[k] for k in range(z - 1, 0, -1)]
    column = lax.dynamic_slice_in_dim(jnp.stack(order), z - 1 - grid.at[2], z, axis=0)
    pieces = {(0, 0): column}
    for a in range(1, n):
        pieces[(a, 0)] = grid.send_plane(column, a, 0)
    for a in range(n):
        for b in range(1, n):
            pieces[(a, b)] = grid.send_plane(pieces[(a, 0)], b, 1)
    out = jnp.zeros((grid.y, CORES, z, n, r, cols), shard.dtype)
    for (a, b), piece in pieces.items():
        other = grid.send_core(piece)
        for part, c in ((piece, core), (other, 1 - core)):
            yy, xx = grid.place((n - a) % n, (n - b) % n, c)
            out = lax.dynamic_update_slice(out, part[None, None, :, None], (yy, c, 0, xx, 0, 0))
    return out.reshape(grid.devices * r, cols)


def outer(left, grad):
    return lax.dot_general(left, grad, (((0,), (0,)), ((), ())), preferred_element_type=jnp.float32)


def core_columns(grid, left, c):
    width = left.shape[1] // (grid.y * CORES)
    return jnp.concatenate(
        [
            lax.dynamic_slice_in_dim(left, (y * CORES + c) * width, width, axis=1)
            for y in range(grid.y)
        ],
        axis=1,
    )


def reduce_outer(grid, left, grad):
    z, n = grid.z, grid.x
    _, core, at_z, _ = grid.at
    rows, cols = left.shape[1], grad.shape[1]
    r = rows // grid.devices
    sent = outer(core_columns(grid, left, 1 - core), grad).astype(jnp.bfloat16)
    got = grid.send_core(sent)
    mine = (outer(core_columns(grid, left, core), grad) + got.astype(jnp.float32)).astype(jnp.bfloat16)
    mine = mine.reshape(grid.y, z, n, r, cols)

    def piece(a, b):
        yy, xx = grid.place(a, b, core)
        return lax.dynamic_slice(mine, (yy, 0, xx, 0, 0), (1, z, 1, r, cols)).reshape(z, r, cols)

    kept = []
    for b in range(n):
        total = piece(0, b).astype(jnp.float32)
        for a in range(1, n):
            total = total + grid.send_plane(piece(a, b), a, 0).astype(jnp.float32)
        kept.append(total.astype(jnp.bfloat16))
    total = kept[0].astype(jnp.float32)
    for b in range(1, n):
        total = total + grid.send_plane(kept[b], b, 1).astype(jnp.float32)
    column = total.astype(jnp.bfloat16)

    def block(k):
        return lax.dynamic_index_in_dim(column, (at_z + k) % z, axis=0, keepdims=False)

    total = block(0).astype(jnp.float32)
    for k in range(1, z):
        total = total + grid.send_z(block(k), k).astype(jnp.float32)
    return total


def reduce_gains(grid, gains):
    z, n = grid.z, grid.x
    total = gains + grid.send_core(gains)
    for swap in (0, 1):
        total = sum((grid.send_plane(total, a, swap) for a in range(1, n)), total)
    total = sum((grid.send_z(total, k) for k in range(1, z)), total)
    width = gains.shape[1] // grid.devices
    y, c, zz, x = grid.at
    return lax.dynamic_slice_in_dim(total, grid.index(y, c, zz, x) * width, width, axis=1)


def split_heads(value):
    return value.reshape(value.shape[0], value.shape[1], -1, HD)


def project(left, weight):
    return jnp.einsum("bld,de->ble", left, weight, preferred_element_type=jnp.float32)


def project_back(grad, weight):
    return jnp.einsum("ble,de->bld", grad, weight, preferred_element_type=jnp.float32)


def normalize(value, gain):
    centred = value - jnp.mean(value, axis=-1, keepdims=True)
    spread = jnp.mean(centred * centred, axis=-1, keepdims=True)
    scale_row = lax.rsqrt(spread + EPS)
    unit = centred * scale_row
    return (unit * gain, unit, scale_row)


def normalize_back(grad, unit, scale_row, gain):
    grad_unit = grad * gain
    grad_gain = jnp.sum(grad * unit, axis=(0, 1))
    centred = grad_unit - jnp.mean(grad_unit, axis=-1, keepdims=True)
    grad_input = scale_row * (centred - unit * jnp.mean(grad_unit * unit, axis=-1, keepdims=True))
    return (grad_input, grad_gain)


def masked_scores(queries, keys, allowed):
    scores = jnp.einsum(
        "bqhd,bkhd->bhqk",
        split_heads(queries),
        split_heads(keys),
        preferred_element_type=jnp.float32,
    ) * HD ** (-0.5)
    return jnp.where(allowed[:, None], scores, -1000000000.0)


def attend(queries, keys, values, allowed):
    scores = masked_scores(queries, keys, allowed)
    top = jnp.max(scores, axis=-1, keepdims=True)
    expos = jnp.exp(scores - top)
    total = jnp.sum(expos, axis=-1, keepdims=True)
    probs = (expos / total).astype(jnp.bfloat16)
    context = jnp.einsum(
        "bhqk,bkhd->bqhd", probs, split_heads(values), preferred_element_type=jnp.float32
    )
    return (context.reshape(queries.shape).astype(jnp.bfloat16), top + jnp.log(total))


def attend_back(queries, keys, values, allowed, logsum, grad_context):
    probs = jnp.exp(masked_scores(queries, keys, allowed) - logsum)
    grad_heads = split_heads(grad_context)
    grad_values = jnp.einsum(
        "bhqk,bqhd->bkhd",
        probs.astype(jnp.bfloat16),
        grad_heads,
        preferred_element_type=jnp.float32,
    )
    grad_probs = jnp.einsum(
        "bqhd,bkhd->bhqk", grad_heads, split_heads(values), preferred_element_type=jnp.float32
    )
    inner = jnp.sum(probs * grad_probs, axis=-1, keepdims=True)
    grad_scores = (probs * (grad_probs - inner)).astype(jnp.bfloat16)
    scale = HD ** (-0.5)
    grad_queries = (
        jnp.einsum(
            "bhqk,bkhd->bqhd", grad_scores, split_heads(keys), preferred_element_type=jnp.float32
        )
        * scale
    )
    grad_keys = (
        jnp.einsum(
            "bhqk,bqhd->bkhd", grad_scores, split_heads(queries), preferred_element_type=jnp.float32
        )
        * scale
    )
    return (
        grad_queries.reshape(queries.shape).astype(jnp.bfloat16),
        grad_keys.reshape(keys.shape).astype(jnp.bfloat16),
        grad_values.reshape(values.shape).astype(jnp.bfloat16),
    )


def per_device(
    hidden_in,
    memory,
    cotangent,
    lengths,
    memory_count,
    causal_gain,
    causal_query,
    causal_key,
    causal_value,
    causal_output,
    source_gain,
    source_query,
    source_key,
    source_value,
    source_output,
    dense_gain,
    dense_expand,
    dense_reduce,
):
    grid = Grid(lax.axis_size("dp"), lax.axis_size("fsdp"))
    inputs = hidden_in[:, 0].astype(jnp.float32)
    source = memory[:, 0]
    page_length = lengths[:, 0]
    page_count = memory_count[:, 0]
    pages, rows, width = inputs.shape
    slots = source.shape[1]
    places = jnp.arange(rows)
    causal_mask = (places[None, None, :] <= places[None, :, None]) & (
        places[None, None, :] < page_length[:, None, None]
    )
    source_mask = jnp.arange(slots)[None, None, :] < page_count[:, None, None]

    def flat(value):
        return value.reshape(pages * value.shape[1], value.shape[2])

    gains = jnp.stack([causal_gain, source_gain, dense_gain], axis=1)
    gains = jnp.pad(gains, ((0, 0), (0, 125)))
    kv_weight = gather(grid, jnp.concatenate([source_key, source_value], axis=1))
    self_weight = gather(
        grid,
        jnp.concatenate([causal_query, causal_key, causal_value, causal_output, gains], axis=1),
    )
    qo_weight = gather(grid, jnp.concatenate([source_query, source_output], axis=1))
    expand_weight = gather(grid, dense_expand)
    reduce_weight = gather(grid, dense_reduce)
    gain_rows = self_weight[:, 4 * width : 4 * width + 3].T.astype(jnp.float32)
    gain_one, gain_two, gain_three = gain_rows[0], gain_rows[1], gain_rows[2]
    qkv_weight = self_weight[:, : 3 * width]
    out_weight = self_weight[:, 3 * width : 4 * width]
    source_query_weight, source_out_weight = qo_weight[:, :width], qo_weight[:, width:]

    memory_both = project(source, kv_weight).astype(jnp.bfloat16)
    memory_keys, memory_values = memory_both[..., :width], memory_both[..., width:]
    normed, unit_one, scale_one = normalize(inputs, gain_one)
    first = normed.astype(jnp.bfloat16)
    qkv = project(first, qkv_weight).astype(jnp.bfloat16)
    queries, keys, values = (qkv[..., i * width : (i + 1) * width] for i in range(3))
    context, logsum_self = attend(queries, keys, values, causal_mask)
    after_self = inputs + project(context, out_weight)
    normed, unit_two, scale_two = normalize(after_self, gain_two)
    second = normed.astype(jnp.bfloat16)
    cross_queries = project(second, source_query_weight).astype(jnp.bfloat16)
    cross_context, logsum_cross = attend(cross_queries, memory_keys, memory_values, source_mask)
    after_cross = after_self + project(cross_context, source_out_weight)
    normed, unit_three, scale_three = normalize(after_cross, gain_three)
    third = normed.astype(jnp.bfloat16)
    hidden_pre = project(third, expand_weight)
    hidden = jax.nn.gelu(hidden_pre, approximate=False).astype(jnp.bfloat16)
    result = after_cross + project(hidden, reduce_weight)

    grad_out = cotangent[:, 0].astype(jnp.float32)
    grad_branch = grad_out.astype(jnp.bfloat16)
    grad_reduce = reduce_outer(grid, flat(hidden), flat(grad_branch))
    grad_hidden = project_back(grad_branch, reduce_weight)
    _, gelu_pull = jax.vjp(lambda v: jax.nn.gelu(v, approximate=False), hidden_pre)
    grad_pre = gelu_pull(grad_hidden)[0].astype(jnp.bfloat16)
    grad_expand = reduce_outer(grid, flat(third), flat(grad_pre))
    grad_norm, grad_gain_three = normalize_back(
        project_back(grad_pre, expand_weight), unit_three, scale_three, gain_three
    )
    grad_cross = grad_out + grad_norm

    grad_branch = grad_cross.astype(jnp.bfloat16)
    grad_source_output = reduce_outer(grid, flat(cross_context), flat(grad_branch))
    grad_context = project_back(grad_branch, source_out_weight).astype(jnp.bfloat16)
    grad_cq, grad_mk, grad_mv = attend_back(
        cross_queries, memory_keys, memory_values, source_mask, logsum_cross, grad_context
    )
    grad_both = jnp.concatenate([grad_mk, grad_mv], axis=-1)
    grad_source_query = reduce_outer(grid, flat(second), flat(grad_cq))
    grad_source_both = reduce_outer(grid, flat(source), flat(grad_both))
    grad_memory = project_back(grad_both, kv_weight)
    grad_norm, grad_gain_two = normalize_back(
        project_back(grad_cq, source_query_weight), unit_two, scale_two, gain_two
    )
    grad_self = grad_cross + grad_norm

    grad_branch = grad_self.astype(jnp.bfloat16)
    grad_causal_output = reduce_outer(grid, flat(context), flat(grad_branch))
    grad_context = project_back(grad_branch, out_weight).astype(jnp.bfloat16)
    grad_q, grad_k, grad_v = attend_back(
        queries, keys, values, causal_mask, logsum_self, grad_context
    )
    grad_qkv = jnp.concatenate([grad_q, grad_k, grad_v], axis=-1)
    grad_causal = reduce_outer(grid, flat(first), flat(grad_qkv))
    grad_norm, grad_gain_one = normalize_back(
        project_back(grad_qkv, qkv_weight), unit_one, scale_one, gain_one
    )
    grad_inputs = grad_self + grad_norm
    grad_gains = reduce_gains(grid, jnp.stack([grad_gain_one, grad_gain_two, grad_gain_three]))
    return (
        result.astype(jnp.bfloat16)[:, None],
        grad_inputs[:, None],
        grad_memory[:, None],
        grad_gains[0],
        grad_causal[:, :width],
        grad_causal[:, width : 2 * width],
        grad_causal[:, 2 * width :],
        grad_causal_output,
        grad_gains[1],
        grad_source_query,
        grad_source_both[:, :width],
        grad_source_both[:, width:],
        grad_source_output,
        grad_gains[2],
        grad_expand,
        grad_reduce,
    )


def solution(mesh):
    pages = P(None, AXES, None, None)
    counts = P(None, AXES)
    gain = P(AXES)
    weight = P(AXES, None)
    return jax.shard_map(
        per_device,
        mesh=mesh,
        in_specs=(pages, pages, pages, counts, counts)
        + (gain, weight, weight, weight, weight)
        + (gain, weight, weight, weight, weight)
        + (gain, weight, weight),
        out_specs=(pages, pages, pages)
        + (gain, weight, weight, weight, weight)
        + (gain, weight, weight, weight, weight)
        + (gain, weight, weight),
        check_vma=False,
    )
```

time: 2060 us -> 701 us (0.34)
  waiting for transfers between devices: 1450 us -> 205 us
  local copies, waits for them, and re-layouts: 355 us -> 186 us
  starting transfers between devices: 0.42 us -> 136 us
  blocking collectives: 42.2 us -> 0 us
  matrix products: 159 us -> 126 us
    unnamed x12 -> x0, waiting for transfers between devices: 951 us -> none
    all_gather x10 -> x0, waiting for transfers between devices: 496 us -> none  [the longest x1 75.4 us: per_device(): lax.all_gather(dense_expand, ('dp', 'fsdp'), axis=0, tiled=True)]
    ppermute x0 -> x105, waiting for transfers between devices: none -> 205 us  [send(): return lax.ppermute(value, AXES, pairs)]
    ppermute x0 -> x105, starting transfers between devices: none -> 136 us  [send(): return lax.ppermute(value, AXES, pairs)]
    unnamed x113 -> x258, local copies, waits for them, and re-layouts: 163 us -> 42.6 us
    concatenate x3 -> x5, local copies, waits for them, and re-layouts: 76 us -> 2.57 us  [the longest x1 1.47 us: per_device(): jnp.concatenate([source_query, source_output], axis=1)]
    dynamic_update_slice x0 -> x42, local copies, waits for them, and re-layouts: none -> 65.3 us  [gather(): lax.dynamic_update_slice(out, part[None, None, :, None], (yy, c, 0, xx, 0...]
    reshape x13 -> x7, local copies, waits for them, and re-layouts: 64.3 us -> 0.72 us  [piece(): lax.dynamic_slice(mine, (yy, 0, xx, 0, 0), (1, z, 1, r, cols))]
  transfers between devices with their start and end apart: 11 -> 105, of which waited for: 11 -> 35; matrix products, arithmetic and copies ran while one was open for 5% -> 33% of each run, Pallas kernels for 0% -> 0%
where the time goes in v1:
time: 701 us; the launch traced here: 694 us
  waiting for transfers between devices  205 us (29%)
  local copies, waits for them, and re-layouts  186 us (27%)
  starting transfers between devices  136 us (19%)
  matrix products  126 us (18%)
  other arithmetic  37.8 us (5%)
    ppermute x105, waiting for transfers between devices, send(): return lax.ppermute(value, AXES, pairs)  205 us
    ppermute x105, starting transfers between devices, send(): return lax.ppermute(value, AXES, pairs)  136 us
    dynamic_update_slice x42, local copies, waits for them, and re-layouts, gather(): lax.dynamic_update_slice(out, part[None, None, :, None], (yy, c, 0, xx, 0...  65.3 us
    unnamed x258, local copies, waits for them, and re-layouts  42.6 us
    dot_general x7, matrix products, project_back(): jnp.einsum('ble,de->bld', grad, weight, preferred_element_type=jnp.float32)  34.4 us
    dot_general x14, matrix products, outer(): lax.dot_general(left, grad, (((0,), (0,)), ((), ())), preferred_element_t...  32.4 us
    dot_general x7, matrix products, project(): jnp.einsum('bld,de->ble', left, weight, preferred_element_type=jnp.float32)  24.5 us
    convert_element_type x5, local copies, waits for them, and re-layouts, attend_back(): grad_values.reshape(values.shape).astype(jnp.bfloat16)  16.2 us
  transfers between devices with their start and end apart: 105, of which 35 were waited for; matrix products, arithmetic and copies ran while one was open for 33% of the time, Pallas kernels for 0%

profile of v1, /device:TPU:0, one launch (start us, length us, event | category | flops | bytes accessed | tf_op | source)
XLA Modules:
  0.0 694.4 jit_solution(9317003712899830756)
XLA Ops:
  33.5 6.3 collective-permute-done.21
  52.8 7.4 %collective-permute-done.30 = bf16[32,4096]{1,0:T(8,128)(2,1)S(1)} collective-permute-done((bf16[32,4096]{1,0:T(8,128)(2,1)}, bf16[32,4096]{1,0:T(8,128)(2,1)S(1)}, u32[]{:S(2)}, u32[]{:S(2)}) %collective-permute-start.30) | collective-permute-done | bytes 262176 | tf_op jit(solution)/shard_map/ppermute | solution.py:32
  60.2 17.9 %collective-permute-start.42 = (bf16[128,1024]{1,0:T(8,128)(2,1)}, bf16[128,1024]{1,0:T(8,128)(2,1)S(1)}, u32[]{:S(2)}, u32[]{:S(2)}) collective-permute-start(bf16[128,1024]{1,0:T(8,128)(2,1)} %param.35), channel_id=1, source_target_pairs={{0,2},{1,3},{2,4},{3,5},{4,6},{5,7},{6,0},{7,1},{8,10},{9,11},{10,... | collective-permute-start | bytes 786440 | tf_op jit(solution)/shard_map/ppermute | solution.py:32
  78.2 12.4 %collective-permute-start.1 = (bf16[32,4224]{1,0:T(8,128)(2,1)S(1)}, bf16[32,4224]{1,0:T(8,128)(2,1)S(1)}, u32[]{:S(2)}, u32[]{:S(2)}) collective-permute-start(bf16[32,4224]{1,0:T(8,128)(2,1)S(1)} %constant_dynamic-update-slice_fusion), channel_id=1, source_target_pairs={{0,4},{1,5},{2,6},{3,7},{4,0},{5,1},{6,2},{7,3},{8,12},{9,13},{10,... | collective-permute-start | bytes 811016 | tf_op jit(solution)/shard_map/ppermute | solution.py:32
  141.9 6.9 collective-permute-done.18
  149.2 5.2 collective-permute-done.28
  157.9 22.8 %collective-permute-done.44 = bf16[4,128,1024]{2,1,0:T(8,128)(2,1)} collective-permute-done((bf16[4,128,1024]{2,1,0:T(8,128)(2,1)}, bf16[4,128,1024]{2,1,0:T(8,128)(2,1)}, u32[]{:S(2)}, u32[]{:S(2)}) %collective-permute-start.44) | collective-permute-done | bytes 1048608 | tf_op jit(solution)/shard_map/ppermute | solution.py:32
  188.9 15.0 %collective-permute-done.4 = bf16[4,32,4224]{2,1,0:T(8,128)(2,1)S(1)} collective-permute-done((bf16[4,32,4224]{2,1,0:T(8,128)(2,1)}, bf16[4,32,4224]{2,1,0:T(8,128)(2,1)S(1)}, u32[]{:S(2)}, u32[]{:S(2)}) %collective-permute-start.4) | collective-permute-done | bytes 1081376 | tf_op jit(solution)/shard_map/ppermute | solution.py:32
  205.5 5.6 convert_bitcast_fusion
  233.0 7.8 %copy.144 = bf16[2,2,4,2,32,4096]{5,4,3,2,1,0:T(8,128)(2,1)} copy(bf16[2,2,4,2,32,4096]{5,4,2,3,1,0:T(8,128)(2,1)} %bitcast_dynamic-update-slice_fusion.19) | data formatting | bytes 16777216 | tf_op jit(solution)/shard_map/dynamic_update_slice | solution.py:74
  240.9 8.3 %copy.148 = bf16[2,2,4,2,128,1024]{5,4,3,2,1,0:T(8,128)(2,1)} copy(bf16[2,2,4,2,128,1024]{5,4,2,3,1,0:T(8,128)(2,1)} %bitcast_dynamic-update-slice_fusion.14) | data formatting | bytes 16777216 | tf_op jit(solution)/shard_map/dynamic_update_slice | solution.py:74
  255.5 8.8 %collective-permute-done.8 = bf16[4,32,4224]{2,1,0:T(8,128)(2,1)S(1)} collective-permute-done((bf16[4,32,4224]{2,1,0:T(8,128)(2,1)S(1)}, bf16[4,32,4224]{2,1,0:T(8,128)(2,1)S(1)}, u32[]{:S(2)}, u32[]{:S(2)}) %collective-permute-start.8) | collective-permute-done | bytes 1081376 | tf_op jit(solution)/shard_map/ppermute | solution.py:32
  310.7 10.8 %multiply_convert_fusion.2 = (bf16[2,128,4096]{2,1,0:T(8,128)(2,1)}, f32[2,128,4096]{2,1,0:T(8,128)}) fusion(f32[2,128,4096]{2,1,0:T(8,128)S(1)} %get-tuple-element.164, u8[128,4096]{1,0:T(8,128)(4,1)S(1)} %get-tuple-element.49, u8[128,4096]{1,0:T(8,128)(4,1)S(1)} %get-tuple-element.48), kind=kLoop, calls=%fused_computation.35 | loop fusion | flops 73400320 | bytes 11534336 | tf_op jit(solution)/shard_map/convert_element_type | solution.py:290
  321.6 5.9 add_convert_fusion.4
  337.2 8.0 %fusion.28 = bf16[2,16,64,588]{3,2,1,0:T(8,128)(2,1)} fusion(bf16[2,128,16,64]{1,3,2,0:T(8,128)(2,1)} %bitcast.669, f32[2,16,128]{2,1,0:T(8,128)S(1)} %log_add_fusion.1, f32[2,16,128,588]{2,3,1,0:T(8,128)} %copy-done, pred[2,588]{1,0:T(4,128)(4,1)S(1)} %iota_compare_fusion.1), kind=kOutput, calls=%fused_computation.76 | convolution fusion | flops 319119360 | bytes 12584088 | tf_op jit(solution)/shard_map/bhqk,bqhd->bkhd/dot_general | solution.py:191
  345.3 6.0 multiply_reduce_fusion
  393.2 6.6 convert_element_type.713
  411.0 6.8 fusion.93
  426.8 5.3 convert_element_type.712
  435.2 10.0 %fusion.21 = f32[2,1,588,1024]{3,2,0,1:T(8,128)} fusion(bf16[1024,2048,1]{1,0,2:T(8,128)(2,1)S(1)} %bitcast.694, bf16[2,588,1024]{2,1,0:T(8,128)(2,1)} %copy.162, bf16[2,588,1024]{2,1,0:T(8,128)(2,1)} %copy.161), kind=kOutput, calls=%fused_computation.53 | convolution fusion | flops 4942135296 | bytes 13828096 | tf_op jit(solution)/shard_map/ble,de->bld/dot_general | solution.py:147
  475.3 9.6 %copy.188 = f32[2,1,588,1024]{3,1,2,0:T(1,128)} copy(f32[2,1,588,1024]{3,2,0,1:T(8,128)} %fusion.21) | data formatting | bytes 9633792
  508.5 6.4 collective-permute-done.71
  518.9 6.5 add_convert_fusion.3
  535.8 5.3 collective-permute-done.74
  574.4 9.1 %collective-permute-done.58 = bf16[4,32,3072]{2,1,0:T(8,128)(2,1)S(1)} collective-permute-done((bf16[4,32,3072]{2,1,0:T(8,128)(2,1)S(1)}, bf16[4,32,3072]{2,1,0:T(8,128)(2,1)S(1)}, u32[]{:S(2)}, u32[]{:S(2)}) %collective-permute-start.58) | collective-permute-done | bytes 786464 | tf_op jit(solution)/shard_map/ppermute | solution.py:32
  591.3 5.4 collective-permute-done.57
  596.7 7.6 %collective-permute-done.59 = bf16[4,32,3072]{2,1,0:T(8,128)(2,1)S(1)} collective-permute-done((bf16[4,32,3072]{2,1,0:T(8,128)(2,1)S(1)}, bf16[4,32,3072]{2,1,0:T(8,128)(2,1)S(1)}, u32[]{:S(2)}, u32[]{:S(2)}) %collective-permute-start.59) | collective-permute-done | bytes 786464 | tf_op jit(solution)/shard_map/ppermute | solution.py:32
  608.7 10.4 %collective-permute-done.100 = bf16[4,128,1024]{2,1,0:T(8,128)(2,1)S(1)} collective-permute-done((bf16[4,128,1024]{2,1,0:T(8,128)(2,1)S(1)}, bf16[4,128,1024]{2,1,0:T(8,128)(2,1)S(1)}, u32[]{:S(2)}, u32[]{:S(2)}) %collective-permute-start.100) | collective-permute-done | bytes 1048608 | tf_op jit(solution)/shard_map/ppermute | solution.py:32
  622.7 11.6 %collective-permute-done.93 = bf16[4,32,4096]{2,1,0:T(8,128)(2,1)S(1)} collective-permute-done((bf16[4,32,4096]{2,1,0:T(8,128)(2,1)S(1)}, bf16[4,32,4096]{2,1,0:T(8,128)(2,1)S(1)}, u32[]{:S(2)}, u32[]{:S(2)}) %collective-permute-start.93) | collective-permute-done | bytes 1048608 | tf_op jit(solution)/shard_map/ppermute | solution.py:32
  639.1 11.5 %collective-permute-done.101 = bf16[4,128,1024]{2,1,0:T(8,128)(2,1)S(1)} collective-permute-done((bf16[4,128,1024]{2,1,0:T(8,128)(2,1)S(1)}, bf16[4,128,1024]{2,1,0:T(8,128)(2,1)S(1)}, u32[]{:S(2)}, u32[]{:S(2)}) %collective-permute-start.101) | collective-permute-done | bytes 1048608 | tf_op jit(solution)/shard_map/ppermute | solution.py:32
  670.7 8.9 %collective-permute-done.103 = bf16[128,1024]{1,0:T(8,128)(2,1)S(1)} collective-permute-done((bf16[128,1024]{1,0:T(8,128)(2,1)S(1)}, bf16[128,1024]{1,0:T(8,128)(2,1)S(1)}, u32[]{:S(2)}, u32[]{:S(2)}) %collective-permute-start.103) | collective-permute-done | bytes 262176 | tf_op jit(solution)/shard_map/ppermute | solution.py:32
  681.8 11.3 %collective-permute-done.96 = bf16[32,4096]{1,0:T(8,128)(2,1)S(1)} collective-permute-done((bf16[32,4096]{1,0:T(8,128)(2,1)S(1)}, bf16[32,4096]{1,0:T(8,128)(2,1)S(1)}, u32[]{:S(2)}, u32[]{:S(2)}) %collective-permute-start.96) | collective-permute-done | bytes 262176 | tf_op jit(solution)/shard_map/ppermute | solution.py:32
  (646 shorter events, 403.2 us)
Async XLA Ops:
  2.3 43.6 %collective-permute-start.12 = (bf16[32,2048]{1,0:T(8,128)(2,1)S(1)}, bf16[32,2048]{1,0:T(8,128)(2,1)S(1)}, u32[]{:S(2)}, u32[]{:S(2)}) collective-permute-start(bf16[32,2048]{1,0:T(8,128)(2,1)S(1)} %constant_dynamic-update-slice_fusion.5), channel_id=1, source_target_pairs={{0,2},{1,3},{2,4},{3,5},{4,6},{5,7},{6,0},{7,1},{8,10},{9,11},{10,... | collective-permute-start | bytes 393224 | tf_op jit(solution)/shard_map/ppermute | solution.py:32
  5.4 37.8 %collective-permute-start.11 = (bf16[32,2048]{1,0:T(8,128)(2,1)S(1)}, bf16[32,2048]{1,0:T(8,128)(2,1)S(1)}, u32[]{:S(2)}, u32[]{:S(2)}) collective-permute-start(bf16[32,2048]{1,0:T(8,128)(2,1)S(1)} %constant_dynamic-update-slice_fusion.5), channel_id=1, source_target_pairs={{0,4},{1,5},{2,6},{3,7},{4,0},{5,1},{6,2},{7,3},{8,12},{9,13},{10,... | collective-permute-start | bytes 393224 | tf_op jit(solution)/shard_map/ppermute | solution.py:32
  7.9 34.5 %collective-permute-start.10 = (bf16[32,2048]{1,0:T(8,128)(2,1)S(1)}, bf16[32,2048]{1,0:T(8,128)(2,1)S(1)}, u32[]{:S(2)}, u32[]{:S(2)}) collective-permute-start(bf16[32,2048]{1,0:T(8,128)(2,1)S(1)} %constant_dynamic-update-slice_fusion.5), channel_id=1, source_target_pairs={{0,6},{1,7},{2,0},{3,1},{4,2},{5,3},{6,4},{7,5},{8,14},{9,15},{10,... | collective-permute-start | bytes 393224 | tf_op jit(solution)/shard_map/ppermute | solution.py:32
  12.2 27.6 %collective-permute-start.22 = (bf16[32,2048]{1,0:T(8,128)(2,1)}, bf16[32,2048]{1,0:T(8,128)(2,1)S(1)}, u32[]{:S(2)}, u32[]{:S(2)}) collective-permute-start(bf16[32,2048]{1,0:T(8,128)(2,1)} %constant_dynamic-update-slice_fusion.7), channel_id=1, source_target_pairs={{0,2},{1,3},{2,4},{3,5},{4,6},{5,7},{6,0},{7,1},{8,10},{9,11},{10,... | collective-permute-start | bytes 393224 | tf_op jit(solution)/shard_map/ppermute | solution.py:32
  39.8 38.3 %collective-permute-start.31 = (bf16[32,4096]{1,0:T(8,128)(2,1)}, bf16[32,4096]{1,0:T(8,128)(2,1)S(1)}, u32[]{:S(2)}, u32[]{:S(2)}) collective-permute-start(bf16[32,4096]{1,0:T(8,128)(2,1)} %param.34), channel_id=1, source_target_pairs={{0,4},{1,5},{2,6},{3,7},{4,0},{5,1},{6,2},{7,3},{8,12},{9,13},{10,... | collective-permute-start | bytes 786440 | tf_op jit(solution)/shard_map/ppermute | solution.py:32
  42.5 57.0 %collective-permute-start.32 = (bf16[32,4096]{1,0:T(8,128)(2,1)}, bf16[32,4096]{1,0:T(8,128)(2,1)S(1)}, u32[]{:S(2)}, u32[]{:S(2)}) collective-permute-start(bf16[32,4096]{1,0:T(8,128)(2,1)} %param.34), channel_id=1, source_target_pairs={{0,2},{1,3},{2,4},{3,5},{4,6},{5,7},{6,0},{7,1},{8,10},{9,11},{10,... | collective-permute-start | bytes 786440 | tf_op jit(solution)/shard_map/ppermute | solution.py:32
  43.2 48.2 %collective-permute-start.41 = (bf16[128,1024]{1,0:T(8,128)(2,1)}, bf16[128,1024]{1,0:T(8,128)(2,1)S(1)}, u32[]{:S(2)}, u32[]{:S(2)}) collective-permute-start(bf16[128,1024]{1,0:T(8,128)(2,1)} %param.35), channel_id=1, source_target_pairs={{0,4},{1,5},{2,6},{3,7},{4,0},{5,1},{6,2},{7,3},{8,12},{9,13},{10,... | collective-permute-start | bytes 786440 | tf_op jit(solution)/shard_map/ppermute | solution.py:32
  45.9 32.3 %collective-permute-start.40 = (bf16[128,1024]{1,0:T(8,128)(2,1)}, bf16[128,1024]{1,0:T(8,128)(2,1)S(1)}, u32[]{:S(2)}, u32[]{:S(2)}) collective-permute-start(bf16[128,1024]{1,0:T(8,128)(2,1)} %param.35), channel_id=1, source_target_pairs={{0,6},{1,7},{2,0},{3,1},{4,2},{5,3},{6,4},{7,5},{8,14},{9,15},{10,... | collective-permute-start | bytes 786440 | tf_op jit(solution)/shard_map/ppermute | solution.py:32
  60.2 35.4 %collective-permute-start.42 = (bf16[128,1024]{1,0:T(8,128)(2,1)}, bf16[128,1024]{1,0:T(8,128)(2,1)S(1)}, u32[]{:S(2)}, u32[]{:S(2)}) collective-permute-start(bf16[128,1024]{1,0:T(8,128)(2,1)} %param.35), channel_id=1, source_target_pairs={{0,2},{1,3},{2,4},{3,5},{4,6},{5,7},{6,0},{7,1},{8,10},{9,11},{10,... | collective-permute-start | bytes 786440 | tf_op jit(solution)/shard_map/ppermute | solution.py:32
  78.1 33.8 %collective-permute-start.2 = (bf16[32,4224]{1,0:T(8,128)(2,1)S(1)}, bf16[32,4224]{1,0:T(8,128)(2,1)S(1)}, u32[]{:S(2)}, u32[]{:S(2)}) collective-permute-start(bf16[32,4224]{1,0:T(8,128)(2,1)S(1)} %constant_dynamic-update-slice_fusion), channel_id=1, source_target_pairs={{0,2},{1,3},{2,4},{3,5},{4,6},{5,7},{6,0},{7,1},{8,10},{9,11},{10,... | collective-permute-start | bytes 811016 | tf_op jit(solution)/shard_map/ppermute | solution.py:32
  78.2 32.5 %collective-permute-start.1 = (bf16[32,4224]{1,0:T(8,128)(2,1)S(1)}, bf16[32,4224]{1,0:T(8,128)(2,1)S(1)}, u32[]{:S(2)}, u32[]{:S(2)}) collective-permute-start(bf16[32,4224]{1,0:T(8,128)(2,1)S(1)} %constant_dynamic-update-slice_fusion), channel_id=1, source_target_pairs={{0,4},{1,5},{2,6},{3,7},{4,0},{5,1},{6,2},{7,3},{8,12},{9,13},{10,... | collective-permute-start | bytes 811016 | tf_op jit(solution)/shard_map/ppermute | solution.py:32
  95.6 28.4 %collective-permute-start.14 = (bf16[4,32,2048]{2,1,0:T(8,128)(2,1)}, bf16[4,32,2048]{2,1,0:T(8,128)(2,1)S(1)}, u32[]{:S(2)}, u32[]{:S(2)}) collective-permute-start(bf16[4,32,2048]{2,1,0:T(8,128)(2,1)} %get-tuple-element.73), channel_id=1, source_target_pairs={{0,1},{1,0},{2,3},{3,2},{4,5},{5,4},{6,7},{7,6},{8,24},{9,25},{10,... | collective-permute-start | bytes 1572872 | tf_op jit(solution)/shard_map/ppermute | solution.py:32
  124.0 58.1 %collective-permute-start.34 = (bf16[4,32,4096]{2,1,0:T(8,128)(2,1)}, bf16[4,32,4096]{2,1,0:T(8,128)(2,1)}, u32[]{:S(2)}, u32[]{:S(2)}) collective-permute-start(bf16[4,32,4096]{2,1,0:T(8,128)(2,1)} %get-tuple-element.69), channel_id=1, source_target_pairs={{0,1},{1,0},{2,3},{3,2},{4,5},{5,4},{6,7},{7,6},{8,24},{9,25},{10,... | collective-permute-start | bytes 3145736 | tf_op jit(solution)/shard_map/ppermute | solution.py:32
  130.0 27.5 %collective-permute-start.33 = (bf16[4,32,4096]{2,1,0:T(8,128)(2,1)}, bf16[4,32,4096]{2,1,0:T(8,128)(2,1)S(1)}, u32[]{:S(2)}, u32[]{:S(2)}) collective-permute-start(bf16[4,32,4096]{2,1,0:T(8,128)(2,1)} %get-tuple-element.69), channel_id=1, source_target_pairs={{0,8},{1,9},{2,10},{3,11},{4,12},{5,13},{6,14},{7,15},{8,0},{9,1},... | collective-permute-start | bytes 3145736 | tf_op jit(solution)/shard_map/ppermute | solution.py:32
  148.8 75.2 %collective-permute-start.36 = (bf16[4,32,4096]{2,1,0:T(8,128)(2,1)}, bf16[4,32,4096]{2,1,0:T(8,128)(2,1)}, u32[]{:S(2)}, u32[]{:S(2)}) collective-permute-start(bf16[4,32,4096]{2,1,0:T(8,128)(2,1)} %get-tuple-element.69), channel_id=1, source_target_pairs={{0,16},{1,17},{2,18},{3,19},{4,20},{5,21},{6,22},{7,23},{8,9},{9,8... | collective-permute-start | bytes 3145736 | tf_op jit(solution)/shard_map/ppermute | solution.py:32
  156.8 68.8 %collective-permute-start.46 = (bf16[4,128,1024]{2,1,0:T(8,128)(2,1)}, bf16[4,128,1024]{2,1,0:T(8,128)(2,1)}, u32[]{:S(2)}, u32[]{:S(2)}) collective-permute-start(bf16[4,128,1024]{2,1,0:T(8,128)(2,1)} %get-tuple-element.65), channel_id=1, source_target_pairs={{0,16},{1,17},{2,18},{3,19},{4,20},{5,21},{6,22},{7,23},{8,9},{9,8... | collective-permute-start | bytes 3145736 | tf_op jit(solution)/shard_map/ppermute | solution.py:32
  157.5 46.4 %collective-permute-start.4 = (bf16[4,32,4224]{2,1,0:T(8,128)(2,1)}, bf16[4,32,4224]{2,1,0:T(8,128)(2,1)S(1)}, u32[]{:S(2)}, u32[]{:S(2)}) collective-permute-start(bf16[4,32,4224]{2,1,0:T(8,128)(2,1)} %get-tuple-element.75), channel_id=1, source_target_pairs={{0,1},{1,0},{2,3},{3,2},{4,5},{5,4},{6,7},{7,6},{8,24},{9,25},{10,... | collective-permute-start | bytes 3244040 | tf_op jit(solution)/shard_map/ppermute | solution.py:32
  182.2 68.5 %collective-permute-start.6 = (bf16[4,32,4224]{2,1,0:T(8,128)(2,1)}, bf16[4,32,4224]{2,1,0:T(8,128)(2,1)}, u32[]{:S(2)}, u32[]{:S(2)}) collective-permute-start(bf16[4,32,4224]{2,1,0:T(8,128)(2,1)} %get-tuple-element.75), channel_id=1, source_target_pairs={{0,16},{1,17},{2,18},{3,19},{4,20},{5,21},{6,22},{7,23},{8,9},{9,8... | collective-permute-start | bytes 3244040 | tf_op jit(solution)/shard_map/ppermute | solution.py:32
  221.2 30.5 %collective-permute-start.38 = (bf16[4,32,4096]{2,1,0:T(8,128)(2,1)}, bf16[4,32,4096]{2,1,0:T(8,128)(2,1)S(1)}, u32[]{:S(2)}, u32[]{:S(2)}) collective-permute-start(bf16[4,32,4096]{2,1,0:T(8,128)(2,1)} %collective-permute-done.34), channel_id=1, source_target_pairs={{0,16},{1,17},{2,18},{3,19},{4,20},{5,21},{6,22},{7,23},{8,9},{9,8... | collective-permute-start | bytes 3145736 | tf_op jit(solution)/shard_map/ppermute | solution.py:32
  224.0 27.8 %collective-permute-start.48 = (bf16[4,128,1024]{2,1,0:T(8,128)(2,1)}, bf16[4,128,1024]{2,1,0:T(8,128)(2,1)S(1)}, u32[]{:S(2)}, u32[]{:S(2)}) collective-permute-start(bf16[4,128,1024]{2,1,0:T(8,128)(2,1)} %collective-permute-done.44), channel_id=1, source_target_pairs={{0,16},{1,17},{2,18},{3,19},{4,20},{5,21},{6,22},{7,23},{8,9},{9,8... | collective-permute-start | bytes 3145736 | tf_op jit(solution)/shard_map/ppermute | solution.py:32
  385.4 101.5 %collective-permute-start.84 = (bf16[512,1024]{1,0:T(8,128)(2,1)}, bf16[512,1024]{1,0:T(8,128)(2,1)}, u32[]{:S(2)}, u32[]{:S(2)}) collective-permute-start(bf16[512,1024]{1,0:T(8,128)(2,1)} %convolution_convert_fusion.4), channel_id=1, source_target_pairs={{0,8},{1,9},{2,10},{3,11},{4,12},{5,13},{6,14},{7,15},{8,0},{9,1},... | collective-permute-start | bytes 3145736 | tf_op jit(solution)/shard_map/ppermute | solution.py:32
  406.2 83.4 %collective-permute-start.70 = (bf16[512,1024]{1,0:T(8,128)(2,1)}, bf16[512,1024]{1,0:T(8,128)(2,1)}, u32[]{:S(2)}, u32[]{:S(2)}) collective-permute-start(bf16[512,1024]{1,0:T(8,128)(2,1)} %convolution_convert_fusion.5), channel_id=1, source_target_pairs={{0,8},{1,9},{2,10},{3,11},{4,12},{5,13},{6,14},{7,15},{8,0},{9,1},... | collective-permute-start | bytes 3145736 | tf_op jit(solution)/shard_map/ppermute | solution.py:32
  418.4 44.6 %collective-permute-start.50 = (f32[3,1024]{1,0:T(4,128)}, f32[3,1024]{1,0:T(4,128)S(1)}, u32[]{:S(2)}, u32[]{:S(2)}) collective-permute-start(f32[3,1024]{1,0:T(4,128)} %pad_maximum_fusion), channel_id=1, source_target_pairs={{0,8},{1,9},{2,10},{3,11},{4,12},{5,13},{6,14},{7,15},{8,0},{9,1},... | collective-permute-start | bytes 36872 | tf_op jit(solution)/shard_map/ppermute | solution.py:32
  484.9 99.3 %collective-permute-start.98 = (bf16[2048,1024]{1,0:T(8,128)(2,1)}, bf16[2048,1024]{1,0:T(8,128)(2,1)S(1)}, u32[]{:S(2)}, u32[]{:S(2)}) collective-permute-start(bf16[2048,1024]{1,0:T(8,128)(2,1)} %convolution_convert_fusion.2), channel_id=1, source_target_pairs={{0,8},{1,9},{2,10},{3,11},{4,12},{5,13},{6,14},{7,15},{8,0},{9,1},... | collective-permute-start | bytes 12582920 | tf_op jit(solution)/shard_map/ppermute | solution.py:32
  485.5 30.4 %collective-permute-start.77 = (bf16[512,2048]{1,0:T(8,128)(2,1)}, bf16[512,2048]{1,0:T(8,128)(2,1)S(1)}, u32[]{:S(2)}, u32[]{:S(2)}) collective-permute-start(bf16[512,2048]{1,0:T(8,128)(2,1)} %convolution_convert_fusion.3), channel_id=1, source_target_pairs={{0,8},{1,9},{2,10},{3,11},{4,12},{5,13},{6,14},{7,15},{8,0},{9,1},... | collective-permute-start | bytes 6291464 | tf_op jit(solution)/shard_map/ppermute | solution.py:32
  505.9 42.4 %collective-permute-start.56 = (bf16[512,3072]{1,0:T(8,128)(2,1)S(1)}, bf16[512,3072]{1,0:T(8,128)(2,1)S(1)}, u32[]{:S(2)}, u32[]{:S(2)}) collective-permute-start(bf16[512,3072]{1,0:T(8,128)(2,1)S(1)} %copy-done.22), channel_id=1, source_target_pairs={{0,8},{1,9},{2,10},{3,11},{4,12},{5,13},{6,14},{7,15},{8,0},{9,1},... | collective-permute-start | bytes 9437192 | tf_op jit(solution)/shard_map/ppermute | solution.py:32
  530.6 57.2 %collective-permute-start.91 = (bf16[512,4096]{1,0:T(8,128)(2,1)S(1)}, bf16[512,4096]{1,0:T(8,128)(2,1)S(1)}, u32[]{:S(2)}, u32[]{:S(2)}) collective-permute-start(bf16[512,4096]{1,0:T(8,128)(2,1)S(1)} %copy-done.41), channel_id=1, source_target_pairs={{0,8},{1,9},{2,10},{3,11},{4,12},{5,13},{6,14},{7,15},{8,0},{9,1},... | collective-permute-start | bytes 12582920 | tf_op jit(solution)/shard_map/ppermute | solution.py:32
  585.8 53.3 %collective-permute-start.99 = (bf16[4,128,1024]{2,1,0:T(8,128)(2,1)S(1)}, bf16[4,128,1024]{2,1,0:T(8,128)(2,1)S(1)}, u32[]{:S(2)}, u32[]{:S(2)}) collective-permute-start(bf16[4,128,1024]{2,1,0:T(8,128)(2,1)S(1)} %get-tuple-element.78), channel_id=1, source_target_pairs={{0,1},{1,0},{2,3},{3,2},{4,5},{5,4},{6,7},{7,6},{8,24},{9,25},{10,... | collective-permute-start | bytes 3145736 | tf_op jit(solution)/shard_map/ppermute | solution.py:32
  587.7 31.5 %collective-permute-start.100 = (bf16[4,128,1024]{2,1,0:T(8,128)(2,1)S(1)}, bf16[4,128,1024]{2,1,0:T(8,128)(2,1)S(1)}, u32[]{:S(2)}, u32[]{:S(2)}) collective-permute-start(bf16[4,128,1024]{2,1,0:T(8,128)(2,1)S(1)} %get-tuple-element.79), channel_id=1, source_target_pairs={{0,1},{1,0},{2,3},{3,2},{4,5},{5,4},{6,7},{7,6},{8,24},{9,25},{10,... | collective-permute-start | bytes 3145736 | tf_op jit(solution)/shard_map/ppermute | solution.py:32
  589.3 45.0 %collective-permute-start.93 = (bf16[4,32,4096]{2,1,0:T(8,128)(2,1)S(1)}, bf16[4,32,4096]{2,1,0:T(8,128)(2,1)S(1)}, u32[]{:S(2)}, u32[]{:S(2)}) collective-permute-start(bf16[4,32,4096]{2,1,0:T(8,128)(2,1)S(1)} %get-tuple-element.81), channel_id=1, source_target_pairs={{0,1},{1,0},{2,3},{3,2},{4,5},{5,4},{6,7},{7,6},{8,24},{9,25},{10,... | collective-permute-start | bytes 3145736 | tf_op jit(solution)/shard_map/ppermute | solution.py:32
  604.7 30.4 %collective-permute-start.60 = (bf16[32,3072]{1,0:T(8,128)(2,1)S(1)}, bf16[32,3072]{1,0:T(8,128)(2,1)S(1)}, u32[]{:S(2)}, u32[]{:S(2)}) collective-permute-start(bf16[32,3072]{1,0:T(8,128)(2,1)S(1)} %get-tuple-element.109), channel_id=1, source_target_pairs={{0,2},{1,3},{2,4},{3,5},{4,6},{5,7},{6,0},{7,1},{8,10},{9,11},{10,... | collective-permute-start | bytes 589832 | tf_op jit(solution)/shard_map/ppermute | solution.py:32
  608.7 28.2 %collective-permute-start.62 = (bf16[32,3072]{1,0:T(8,128)(2,1)S(1)}, bf16[32,3072]{1,0:T(8,128)(2,1)S(1)}, u32[]{:S(2)}, u32[]{:S(2)}) collective-permute-start(bf16[32,3072]{1,0:T(8,128)(2,1)S(1)} %get-tuple-element.110), channel_id=1, source_target_pairs={{0,6},{1,7},{2,0},{3,1},{4,2},{5,3},{6,4},{7,5},{8,14},{9,15},{10,... | collective-permute-start | bytes 589832 | tf_op jit(solution)/shard_map/ppermute | solution.py:32
  (180 other events, 2714.6 us)

commit v2 on v1

v2 whole, which is shorter than its diff:
```python
import functools

import jax
import jax.numpy as jnp
from jax import lax
from jax.experimental import pallas as pl
from jax.experimental.pallas import tpu as pltpu
from jax.sharding import PartitionSpec as P

HD = 64
EPS = 1e-05
AXES = ("dp", "fsdp")
CORES = 2
WIDTH = 1024
MESH = pl.DeviceIdType.MESH


class Grid:
    def __init__(self):
        dp, fsdp = lax.axis_size("dp"), lax.axis_size("fsdp")
        self.n = dp // CORES
        self.depth = fsdp // self.n
        self.devices = dp * fsdp
        d, f = lax.axis_index("dp"), lax.axis_index("fsdp")
        self.at = (d // CORES, d % CORES, f // self.n, f % self.n)

    def device(self, y, c, z, x):
        return (y * CORES + c, z * self.n + x)

    def step_z(self, k):
        y, c, z, x = self.at
        return self.device(y, c, lax.rem(z + k, self.depth), x)

    def step_plane(self, k, swap):
        y, c, z, x = self.at
        odd = lax.rem(c + swap, 2)
        return self.device(
            lax.rem(y + k * odd, self.n), c, z, lax.rem(x + k * (1 - odd), self.n)
        )

    def partner(self):
        y, c, z, x = self.at
        return self.device(y, 1 - c, z, x)

    def place(self, a, b):
        y, c, z, x = self.at
        ky = a * c + b * (1 - c)
        kx = a * (1 - c) + b * c
        return lax.rem(y + ky, self.n), lax.rem(x + kx, self.n)

    def peers(self):
        line = [self.step_z(k) for k in range(1, self.depth)]
        plane = [self.step_plane(k, s) for s in (0, 1) for k in range(1, self.n)]
        return line + plane + [self.partner()]

    def meet(self):
        barrier = pltpu.get_barrier_semaphore()
        peers = self.peers()
        for peer in peers:
            pl.semaphore_signal(barrier, inc=1, device_id=peer, device_id_type=MESH)
        pl.semaphore_wait(barrier, len(peers))


def remote(src, dst, send_sem, recv_sem, device):
    return pltpu.make_async_remote_copy(
        src_ref=src,
        dst_ref=dst,
        send_sem=send_sem,
        recv_sem=recv_sem,
        device_id=device,
        device_id_type=MESH,
    )


def started(*copy):
    made = remote(*copy)
    made.start()
    return made


class Plan:
    def __init__(self):
        self.calls = {}

    def add(self, tick, rank, call, *args):
        self.calls.setdefault((tick, rank), []).append((call, args))

    def run(self):
        for key in sorted(self.calls):
            for call, args in self.calls[key]:
                call(*args)


def gather_kernel(chunks, count, *refs):
    grid = Grid()
    n, depth = grid.n, grid.depth
    shards, outs = refs[:count], refs[count : 2 * count]
    local, zs, zr, ps, pr, qs, qr, cs, cr, us, ur, ds, dr = refs[2 * count :]
    y, c, z, x = grid.at
    grid.meet()
    pending = []

    def send(*copy):
        made = started(*copy)
        pending.append(made)
        return made

    def window(i):
        _, r0, nr, c0, nc, _ = chunks[i]
        return pl.ds(r0, nr), pl.ds(c0, nc)

    def shard(i):
        return shards[chunks[i][0]].at[window(i)]

    def block(i, yy, zz, xx):
        return outs[chunks[i][0]].at[(yy, c, zz, xx) + window(i)]

    def back(a, b):
        return grid.place((n - a) % n, (n - b) % n)

    def column(i, a, b):
        yy, xx = back(a, b)
        return outs[chunks[i][0]].at[(yy, c, slice(None), xx) + window(i)]

    def share(i, a, b):
        piece = column(i, a, b)
        slot = a * n + b
        return send(piece, piece, cs.at[i, slot], cr.at[i, slot], grid.partner())

    zc, pc, qc, cc, lc = {}, {}, {}, {}, {}

    def keep_own(i):
        lc[i] = pltpu.make_async_copy(shard(i), block(i, y, z, x), local.at[i])
        lc[i].start()

    def stage_z(i):
        zc[i] = [
            send(shard(i), block(i, y, z, x), zs.at[i, k - 1], zr.at[i, k - 1], grid.step_z(k))
            for k in range(1, depth)
        ]
        keep_own(i)

    def stage_p(i):
        for copy in zc[i]:
            copy.wait_recv()
        lc[i].wait()
        piece = column(i, 0, 0)
        pc[i] = [
            send(piece, piece, ps.at[i, a - 1], pr.at[i, a - 1], grid.step_plane(a, 0))
            for a in range(1, n)
        ]
        qc[i] = [
            send(piece, piece, qs.at[i, b - 1], qr.at[i, b - 1], grid.step_plane(b, 1))
            for b in range(1, n)
        ]
        cc[i] = [share(i, 0, 0)]

    def stage_q(i):
        for a in range(1, n):
            pc[i][a - 1].wait_recv()
            piece = column(i, a, 0)
            for b in range(1, n):
                j = a * (n - 1) + b - 1
                qc[i].append(
                    send(piece, piece, qs.at[i, j], qr.at[i, j], grid.step_plane(b, 1))
                )
            cc[i].append(share(i, a, 0))

    def stage_c(i):
        j = 0
        for a in range(n):
            for b in range(1, n):
                qc[i][j].wait_recv()
                j += 1
                cc[i].append(share(i, a, b))

    def tall_p(i):
        keep_own(i)
        pc[i] = [
            send(shard(i), block(i, y, z, x), ps.at[i, a - 1], pr.at[i, a - 1], grid.step_plane(a, 0))
            for a in range(1, n)
        ]

    def tall_q(i):
        lc[i].wait()
        qc[i] = []
        for a in range(n):
            if a:
                pc[i][a - 1].wait_recv()
            yy, xx = back(a, 0)
            piece = block(i, yy, z, xx)
            for b in range(1, n):
                j = a * (n - 1) + b - 1
                qc[i].append(
                    send(piece, piece, qs.at[i, j], qr.at[i, j], grid.step_plane(b, 1))
                )

    def layer(i, k, j):
        zz = lax.rem(z + (depth - j if k == 0 else j), depth)
        return outs[chunks[i][0]].at[(slice(None), c, zz, slice(None)) + window(i)]

    def hop(i, k, j):
        piece = layer(i, k, j)
        send_sem, recv_sem = ((us, ur), (ds, dr))[k]
        to = grid.device(y, c, lax.rem(z + (1 if k == 0 else depth - 1), depth), x)
        return remote(piece, piece, send_sem.at[i, j], recv_sem.at[i, j], to)

    def share_layer(i, k, j):
        piece = layer(i, k, j)
        slot = k * (depth - 1) + j
        return remote(piece, piece, cs.at[i, slot], cr.at[i, slot], grid.partner())

    def level(k):
        return z if k == 0 else depth - 1 - z

    def climb(i, j):
        if j == 0:
            for copy in qc[i]:
                copy.wait_recv()
            share_layer(i, 0, 0).start()
        for k in (0, 1):
            if j:

                @pl.when(level(k) >= j)
                def _():
                    hop(i, k, j - 1).wait_recv()
                    share_layer(i, k, j).start()

            if j < depth - 1:

                @pl.when((level(k) >= j) & (level(k) < depth - 1))
                def _():
                    hop(i, k, j).start()

    def finish_tall(i):
        share_layer(i, 0, 0).wait()
        for k in (0, 1):
            for j in range(depth - 1):

                @pl.when((level(k) >= j) & (level(k) < depth - 1))
                def _():
                    hop(i, k, j).wait_send()

                @pl.when(level(k) >= j + 1)
                def _():
                    share_layer(i, k, j + 1).wait()

    plan = Plan()
    flat = [i for i, chunk in enumerate(chunks) if not chunk[5]]
    tall = [i for i, chunk in enumerate(chunks) if chunk[5]]
    for t, i in enumerate(flat):
        plan.add(t - 2, 0, stage_z, i)
        plan.add(t, 2, stage_p, i)
        plan.add(t + 1, 4, stage_q, i)
        plan.add(t + 2, 6, stage_c, i)
    for t, i in enumerate(tall):
        t = 3 * t - 1
        plan.add(t, 1, tall_p, i)
        plan.add(t + 2, 3, tall_q, i)
        for h in range(depth):
            plan.add(t + 4 + 2 * h, 5, climb, i, h)
    plan.run()
    for i in flat:
        for copy in cc[i]:
            copy.wait_recv()
    for i in tall:
        finish_tall(i)
    for copy in pending:
        copy.wait_send()


def gather_all(shards, tall):
    dp, fsdp = lax.axis_size("dp"), lax.axis_size("fsdp")
    n = dp // CORES
    depth = fsdp // n
    rows = shards[0].shape[0]
    chunks = []
    for m, shard in enumerate(shards):
        r, cols = shard.shape
        for r0 in range(0, r, rows):
            for c0 in range(0, cols // WIDTH * WIDTH, WIDTH):
                nc = WIDTH if c0 + 2 * WIDTH <= cols else cols - c0
                chunks.append((m, r0, rows, c0, nc, len(chunks) in tall))
    t = len(chunks)
    slots = max(n * n, 2 * depth - 1)
    shapes = (1, depth - 1, depth - 1, n - 1, n - 1, n * (n - 1), n * (n - 1), slots, slots)
    shapes += (depth - 1,) * 4
    dma = pltpu.SemaphoreType.DMA
    outs = pl.pallas_call(
        functools.partial(gather_kernel, chunks, len(shards)),
        out_shape=[
            jax.ShapeDtypeStruct((n, CORES, depth, n) + s.shape, s.dtype) for s in shards
        ],
        in_specs=[pl.BlockSpec(memory_space=pltpu.VMEM)] * len(shards),
        out_specs=[pl.BlockSpec(memory_space=pltpu.HBM)] * len(shards),
        scratch_shapes=[dma((t,))] + [dma((t, k)) for k in shapes[1:]],
        compiler_params=pltpu.CompilerParams(collective_id=0, has_side_effects=True),
    )(*shards)
    return [o.reshape(dp * fsdp * s.shape[0], s.shape[1]) for o, s in zip(outs, shards)]


RING = 4


def reduce_kernel(chunks, count, *refs):
    grid = Grid()
    n, depth = grid.n, grid.depth
    y, c, z, x = grid.at
    parts, gain_in = refs[:count], refs[count]
    outs, gain_out = refs[count + 1 : 2 * count + 1], refs[2 * count + 1]
    (own, got0, send1, got1, keep1, send2, got2, keep2, line, got3, gain_sum, gain_got) = refs[
        2 * count + 2 : 2 * count + 14
    ]
    local, s0, r0, s1, r1, s2, r2, s3, r3, gs, gr = refs[2 * count + 14 :]
    rows, width = own.shape[-2:]
    total = len(chunks)
    f32, bf16 = jnp.float32, jnp.bfloat16
    grid.meet()
    copies = {}

    def half(i, core):
        m, row, col = chunks[i]
        return parts[m].at[:, core, :, :, pl.ds(row, rows), pl.ds(col, width)]

    def reuse(i, stage):
        if i >= RING:
            for copy in copies[i - RING, stage]:
                copy.wait_send()

    def load(i):
        copies[i, "own"] = pltpu.make_async_copy(half(i, c), own.at[i % RING], local.at[i % RING])
        copies[i, "own"].start()

    def stage0(i):
        copies[i, 0] = [
            started(half(i, 1 - c), got0.at[i], s0.at[i], r0.at[i], grid.partner())
        ]

    def stage1(i):
        s = i % RING
        reuse(i, 1)
        copies[i, "own"].wait()
        copies[i, 0][0].wait_recv()

        def add(dst, a, b):
            yy, xx = grid.place(a, b)

            def body(zz, carry):
                total_ = own[s, yy, zz, xx].astype(f32) + got0[i, yy, zz, xx].astype(f32)
                dst[zz] = total_.astype(bf16)
                return carry

            lax.fori_loop(0, depth, body, 0)

        copies[i, 1] = []
        for a in range(1, n):
            for b in range(n):
                add(send1.at[s, a - 1, b], a, b)
            copies[i, 1].append(
                started(
                    send1.at[s, a - 1],
                    got1.at[i, a - 1],
                    s1.at[s, a - 1],
                    r1.at[i, a - 1],
                    grid.step_plane(a, 0),
                )
            )
        for b in range(n):
            add(keep1.at[s, b], 0, b)
        if i + RING < total:
            load(i + RING)

    def stage2(i):
        s = i % RING
        reuse(i, 2)
        for copy in copies[i, 1]:
            copy.wait_recv()
        copies[i, 2] = []
        for b in list(range(1, n)) + [0]:
            dst = send2.at[s, b - 1] if b else keep2.at[s]

            def body(zz, carry):
                total_ = keep1[s, b, zz].astype(f32)
                for a in range(1, n):
                    total_ = total_ + got1[i, a - 1, b, zz].astype(f32)
                dst[zz] = total_.astype(bf16)
                return carry

            lax.fori_loop(0, depth, body, 0)
            if b:
                copies[i, 2].append(
                    started(
                        send2.at[s, b - 1],
                        got2.at[i, b - 1],
                        s2.at[s, b - 1],
                        r2.at[i, b - 1],
                        grid.step_plane(b, 1),
                    )
                )

    def stage3(i):
        s = i % RING
        reuse(i, 3)
        for copy in copies[i, 2]:
            copy.wait_recv()

        def body(zz, carry):
            total_ = keep2[s, zz].astype(f32)
            for b in range(1, n):
                total_ = total_ + got2[i, b - 1, zz].astype(f32)
            line[s, zz] = total_.astype(bf16)
            return carry

        lax.fori_loop(0, depth, body, 0)
        copies[i, 3] = [
            started(
                line.at[s, lax.rem(z + k, depth)],
                got3.at[i, k - 1],
                s3.at[s, k - 1],
                r3.at[i, k - 1],
                grid.step_z(k),
            )
            for k in range(1, depth)
        ]

    def stage4(i):
        m, row, col = chunks[i]
        for copy in copies[i, 3]:
            copy.wait_recv()
        total_ = line[i % RING, z].astype(f32)
        for k in range(1, depth):
            total_ = total_ + got3[i, k - 1].astype(f32)
        outs[m][pl.ds(row, rows), pl.ds(col, width)] = total_

    moves = [
        [grid.partner()],
        [grid.step_plane(a, 0) for a in range(1, n)],
        [grid.step_plane(a, 1) for a in range(1, n)],
        [grid.step_z(k) for k in range(1, depth)],
        [],
    ]
    first = [0, 1, n, 2 * n - 1, 2 * n + depth - 2]

    def gain_step(h):
        total_ = gain_in[...]
        if h:
            total_ = gain_sum[h - 1]
            for j, copy in enumerate(copies["gain", h - 1]):
                copy.wait_recv()
                total_ = total_ + gain_got[first[h - 1] + j]
        if h == len(moves) - 1:
            gain_out[...] = total_
        else:
            gain_sum[h] = total_
        copies["gain", h] = [
            started(
                gain_sum.at[h],
                gain_got.at[first[h] + j],
                gs.at[first[h] + j],
                gr.at[first[h] + j],
                device,
            )
            for j, device in enumerate(moves[h])
        ]

    plan = Plan()
    for i in range(total):
        plan.add(i - 2, 0, stage0, i)
        plan.add(i, 1, stage1, i)
        plan.add(i + 1, 2, stage2, i)
        plan.add(i + 2, 3, stage3, i)
        plan.add(i + 3, 4, stage4, i)
    for h in range(len(moves)):
        plan.add(total - 4 + h, 5, gain_step, h)
    for i in range(min(RING, total)):
        load(i)
    plan.run()
    for i in range(total):
        copies[i, 0][0].wait_send()
        if i >= total - RING:
            for stage in (1, 2, 3):
                for copy in copies[i, stage]:
                    copy.wait_send()
    for h in range(len(moves)):
        for copy in copies["gain", h]:
            copy.wait_send()


def reduce_all(parts, gains):
    dp, fsdp = lax.axis_size("dp"), lax.axis_size("fsdp")
    n = dp // CORES
    depth = fsdp // n
    devices = dp * fsdp
    rows = WIDTH // devices
    chunks = []
    for m, part in enumerate(parts):
        for row in range(0, part.shape[0] // devices, rows):
            for col in range(0, part.shape[1], WIDTH):
                chunks.append((m, row, col))
    t = len(chunks)
    dma = pltpu.SemaphoreType.DMA
    hops = 2 * n + depth - 2

    def scratch(*lead):
        return pltpu.VMEM(lead + (rows, WIDTH), jnp.bfloat16)

    views = [p.reshape(n, CORES, depth, n, p.shape[0] // devices, p.shape[1]) for p in parts]
    return pl.pallas_call(
        functools.partial(reduce_kernel, chunks, len(parts)),
        out_shape=[
            jax.ShapeDtypeStruct((p.shape[0] // devices, p.shape[1]), jnp.float32) for p in parts
        ]
        + [jax.ShapeDtypeStruct(gains.shape, jnp.float32)],
        in_specs=[pl.BlockSpec(memory_space=pltpu.HBM)] * len(parts)
        + [pl.BlockSpec(memory_space=pltpu.VMEM)],
        out_specs=[pl.BlockSpec(memory_space=pltpu.VMEM)] * (len(parts) + 1),
        scratch_shapes=[
            scratch(RING, n, depth, n),
            scratch(t, n, depth, n),
            scratch(RING, n - 1, n, depth),
            scratch(t, n - 1, n, depth),
            scratch(RING, n, depth),
            scratch(RING, n - 1, depth),
            scratch(t, n - 1, depth),
            scratch(RING, depth),
            scratch(RING, depth),
            scratch(t, depth - 1),
            pltpu.VMEM((4,) + gains.shape, jnp.float32),
            pltpu.VMEM((hops,) + gains.shape, jnp.float32),
            dma((RING,)),
            dma((t,)),
            dma((t,)),
            dma((RING, n - 1)),
            dma((t, n - 1)),
            dma((RING, n - 1)),
            dma((t, n - 1)),
            dma((RING, depth - 1)),
            dma((t, depth - 1)),
            dma((hops,)),
            dma((hops,)),
        ],
        compiler_params=pltpu.CompilerParams(
            collective_id=1, has_side_effects=True, vmem_limit_bytes=60 << 20
        ),
    )(*views, gains)


def outer(left, grad):
    total = lax.dot_general(left, grad, (((0,), (0,)), ((), ())), preferred_element_type=jnp.float32)
    return total.astype(jnp.bfloat16)


def split_heads(value):
    return value.reshape(value.shape[0], value.shape[1], -1, HD)


def project(left, weight):
    return jnp.einsum("bld,de->ble", left, weight, preferred_element_type=jnp.float32)


def project_back(grad, weight):
    return jnp.einsum("ble,de->bld", grad, weight, preferred_element_type=jnp.float32)


def normalize(value, gain):
    centred = value - jnp.mean(value, axis=-1, keepdims=True)
    spread = jnp.mean(centred * centred, axis=-1, keepdims=True)
    scale_row = lax.rsqrt(spread + EPS)
    unit = centred * scale_row
    return (unit * gain, unit, scale_row)


def normalize_back(grad, unit, scale_row, gain):
    grad_unit = grad * gain
    grad_gain = jnp.sum(grad * unit, axis=(0, 1))
    centred = grad_unit - jnp.mean(grad_unit, axis=-1, keepdims=True)
    grad_input = scale_row * (centred - unit * jnp.mean(grad_unit * unit, axis=-1, keepdims=True))
    return (grad_input, grad_gain)


def masked_scores(queries, keys, allowed):
    scores = jnp.einsum(
        "bqhd,bkhd->bhqk",
        split_heads(queries),
        split_heads(keys),
        preferred_element_type=jnp.float32,
    ) * HD ** (-0.5)
    return jnp.where(allowed[:, None], scores, -1000000000.0)


def attend(queries, keys, values, allowed):
    scores = masked_scores(queries, keys, allowed)
    top = jnp.max(scores, axis=-1, keepdims=True)
    expos = jnp.exp(scores - top)
    total = jnp.sum(expos, axis=-1, keepdims=True)
    probs = (expos / total).astype(jnp.bfloat16)
    context = jnp.einsum(
        "bhqk,bkhd->bqhd", probs, split_heads(values), preferred_element_type=jnp.float32
    )
    return (context.reshape(queries.shape).astype(jnp.bfloat16), top + jnp.log(total))


def attend_back(queries, keys, values, allowed, logsum, grad_context):
    probs = jnp.exp(masked_scores(queries, keys, allowed) - logsum)
    grad_heads = split_heads(grad_context)
    grad_values = jnp.einsum(
        "bhqk,bqhd->bkhd",
        probs.astype(jnp.bfloat16),
        grad_heads,
        preferred_element_type=jnp.float32,
    )
    grad_probs = jnp.einsum(
        "bqhd,bkhd->bhqk", grad_heads, split_heads(values), preferred_element_type=jnp.float32
    )
    inner = jnp.sum(probs * grad_probs, axis=-1, keepdims=True)
    grad_scores = (probs * (grad_probs - inner)).astype(jnp.bfloat16)
    scale = HD ** (-0.5)
    grad_queries = (
        jnp.einsum(
            "bhqk,bkhd->bqhd", grad_scores, split_heads(keys), preferred_element_type=jnp.float32
        )
        * scale
    )
    grad_keys = (
        jnp.einsum(
            "bhqk,bqhd->bkhd", grad_scores, split_heads(queries), preferred_element_type=jnp.float32
        )
        * scale
    )
    return (
        grad_queries.reshape(queries.shape).astype(jnp.bfloat16),
        grad_keys.reshape(keys.shape).astype(jnp.bfloat16),
        grad_values.reshape(values.shape).astype(jnp.bfloat16),
    )


def per_device(
    hidden_in,
    memory,
    cotangent,
    lengths,
    memory_count,
    causal_gain,
    causal_query,
    causal_key,
    causal_value,
    causal_output,
    source_gain,
    source_query,
    source_key,
    source_value,
    source_output,
    dense_gain,
    dense_expand,
    dense_reduce,
):
    inputs = hidden_in[:, 0].astype(jnp.float32)
    source = memory[:, 0]
    page_length = lengths[:, 0]
    page_count = memory_count[:, 0]
    pages, rows, width = inputs.shape
    slots = source.shape[1]
    places = jnp.arange(rows)
    causal_mask = (places[None, None, :] <= places[None, :, None]) & (
        places[None, None, :] < page_length[:, None, None]
    )
    source_mask = jnp.arange(slots)[None, None, :] < page_count[:, None, None]

    def flat(value):
        return value.reshape(pages * value.shape[1], value.shape[2])

    gains = jnp.stack([causal_gain, source_gain, dense_gain], axis=1)
    gains = jnp.pad(gains, ((0, 0), (0, 125)))
    kv_weight, self_weight, qo_weight, expand_weight, reduce_weight = gather_all(
        [
            jnp.concatenate([source_key, source_value], axis=1),
            jnp.concatenate([causal_query, causal_key, causal_value, causal_output, gains], axis=1),
            jnp.concatenate([source_query, source_output], axis=1),
            dense_expand,
            dense_reduce,
        ],
        (1, 5, 9),
    )
    gain_rows = self_weight[:, 4 * width : 4 * width + 3].T.astype(jnp.float32)
    gain_one, gain_two, gain_three = gain_rows[0], gain_rows[1], gain_rows[2]
    qkv_weight = self_weight[:, : 3 * width]
    out_weight = self_weight[:, 3 * width : 4 * width]
    source_query_weight, source_out_weight = qo_weight[:, :width], qo_weight[:, width:]

    memory_both = project(source, kv_weight).astype(jnp.bfloat16)
    memory_keys, memory_values = memory_both[..., :width], memory_both[..., width:]
    normed, unit_one, scale_one = normalize(inputs, gain_one)
    first = normed.astype(jnp.bfloat16)
    qkv = project(first, qkv_weight).astype(jnp.bfloat16)
    queries, keys, values = (qkv[..., i * width : (i + 1) * width] for i in range(3))
    context, logsum_self = attend(queries, keys, values, causal_mask)
    after_self = inputs + project(context, out_weight)
    normed, unit_two, scale_two = normalize(after_self, gain_two)
    second = normed.astype(jnp.bfloat16)
    cross_queries = project(second, source_query_weight).astype(jnp.bfloat16)
    cross_context, logsum_cross = attend(cross_queries, memory_keys, memory_values, source_mask)
    after_cross = after_self + project(cross_context, source_out_weight)
    normed, unit_three, scale_three = normalize(after_cross, gain_three)
    third = normed.astype(jnp.bfloat16)
    hidden_pre = project(third, expand_weight)
    hidden = jax.nn.gelu(hidden_pre, approximate=False).astype(jnp.bfloat16)
    result = after_cross + project(hidden, reduce_weight)

    grad_out = cotangent[:, 0].astype(jnp.float32)
    grad_branch = grad_out.astype(jnp.bfloat16)
    grad_reduce = outer(flat(hidden), flat(grad_branch))
    grad_hidden = project_back(grad_branch, reduce_weight)
    _, gelu_pull = jax.vjp(lambda v: jax.nn.gelu(v, approximate=False), hidden_pre)
    grad_pre = gelu_pull(grad_hidden)[0].astype(jnp.bfloat16)
    grad_expand = outer(flat(third), flat(grad_pre))
    grad_norm, grad_gain_three = normalize_back(
        project_back(grad_pre, expand_weight), unit_three, scale_three, gain_three
    )
    grad_cross = grad_out + grad_norm

    grad_branch = grad_cross.astype(jnp.bfloat16)
    grad_source_output = outer(flat(cross_context), flat(grad_branch))
    grad_context = project_back(grad_branch, source_out_weight).astype(jnp.bfloat16)
    grad_cq, grad_mk, grad_mv = attend_back(
        cross_queries, memory_keys, memory_values, source_mask, logsum_cross, grad_context
    )
    grad_both = jnp.concatenate([grad_mk, grad_mv], axis=-1)
    grad_source_query = outer(flat(second), flat(grad_cq))
    grad_source_both = outer(flat(source), flat(grad_both))
    grad_memory = project_back(grad_both, kv_weight)
    grad_norm, grad_gain_two = normalize_back(
        project_back(grad_cq, source_query_weight), unit_two, scale_two, gain_two
    )
    grad_self = grad_cross + grad_norm

    grad_branch = grad_self.astype(jnp.bfloat16)
    grad_causal_output = outer(flat(context), flat(grad_branch))
    grad_context = project_back(grad_branch, out_weight).astype(jnp.bfloat16)
    grad_q, grad_k, grad_v = attend_back(
        queries, keys, values, causal_mask, logsum_self, grad_context
    )
    grad_qkv = jnp.concatenate([grad_q, grad_k, grad_v], axis=-1)
    grad_causal = outer(flat(first), flat(grad_qkv))
    grad_norm, grad_gain_one = normalize_back(
        project_back(grad_qkv, qkv_weight), unit_one, scale_one, gain_one
    )
    grad_inputs = grad_self + grad_norm
    gain_sums = jnp.stack([grad_gain_one, grad_gain_two, grad_gain_three])
    gain_sums = jnp.pad(gain_sums, ((0, 5), (0, 0)))
    (
        grad_reduce,
        grad_expand,
        grad_source_output,
        grad_source_query,
        grad_source_both,
        grad_causal_output,
        grad_causal,
        grad_gains,
    ) = reduce_all(
        [
            grad_reduce,
            grad_expand,
            grad_source_output,
            grad_source_query,
            grad_source_both,
            grad_causal_output,
            grad_causal,
        ],
        gain_sums,
    )
    entries = causal_gain.shape[0]
    me = lax.axis_index("dp") * lax.axis_size("fsdp") + lax.axis_index("fsdp")
    grad_gains = lax.dynamic_slice_in_dim(grad_gains, me * entries, entries, axis=1)
    return (
        result.astype(jnp.bfloat16)[:, None],
        grad_inputs[:, None],
        grad_memory[:, None],
        grad_gains[0],
        grad_causal[:, :width],
        grad_causal[:, width : 2 * width],
        grad_causal[:, 2 * width :],
        grad_causal_output,
        grad_gains[1],
        grad_source_query,
        grad_source_both[:, :width],
        grad_source_both[:, width:],
        grad_source_output,
        grad_gains[2],
        grad_expand,
        grad_reduce,
    )


def solution(mesh):
    pages = P(None, AXES, None, None)
    counts = P(None, AXES)
    gain = P(AXES)
    weight = P(AXES, None)
    return jax.shard_map(
        per_device,
        mesh=mesh,
        in_specs=(pages, pages, pages, counts, counts)
        + (gain, weight, weight, weight, weight)
        + (gain, weight, weight, weight, weight)
        + (gain, weight, weight),
        out_specs=(pages, pages, pages)
        + (gain, weight, weight, weight, weight)
        + (gain, weight, weight, weight, weight)
        + (gain, weight, weight),
        check_vma=False,
    )
```

time: 701 us -> 572 us (0.82)
  Pallas kernels: 0 us -> 299 us
  waiting for transfers between devices: 205 us -> 0 us
  starting transfers between devices: 136 us -> 0 us
  local copies, waits for them, and re-layouts: 186 us -> 97 us
  matrix products: 126 us -> 140 us
  other arithmetic: 37.8 us -> 26 us
    pallas_call x0 -> x2, Pallas kernels: none -> 299 us  [the longest x1 155 us: reduce_all(): pl.pallas_call(functools.partial(reduce_kernel, chunks, len(parts)), out_...]
    ppermute x105 -> x0, waiting for transfers between devices: 205 us -> none  [send(): return lax.ppermute(value, AXES, pairs)]
    ppermute x105 -> x0, starting transfers between devices: 136 us -> none  [send(): return lax.ppermute(value, AXES, pairs)]
    dynamic_update_slice x42 -> x0, local copies, waits for them, and re-layouts: 65.3 us -> none  [gather(): lax.dynamic_update_slice(out, part[None, None, :, None], (yy, c, 0, xx, 0...]
    unnamed x258 -> x123, local copies, waits for them, and re-layouts: 42.6 us -> 30.3 us
    dot_general x7, matrix products: 24.5 us -> 32.3 us  [project(): jnp.einsum('bld,de->ble', left, weight, preferred_element_type=jnp.float32)]
    dynamic_slice x5 -> x1, local copies, waits for them, and re-layouts: 7.99 us -> 0.74 us  [per_device(): lax.dynamic_slice_in_dim(grad_gains, me * entries, entries, axis=1)]
    convert_element_type x5 -> x4, local copies, waits for them, and re-layouts: 16.2 us -> 18.6 us  [attend_back(): grad_values.reshape(values.shape).astype(jnp.bfloat16)]
  transfers between devices with their start and end apart: 105 -> 0, of which waited for: 35 -> 0; matrix products, arithmetic and copies ran while one was open for 33% -> 0% of each run, Pallas kernels for 0% -> 0%
where the time goes in v2:
time: 572 us; the launch traced here: 563 us
  Pallas kernels  299 us (52%)
  matrix products  140 us (24%)
  local copies, waits for them, and re-layouts  97 us (17%)
  other arithmetic  26 us (5%)
    pallas_call x1, Pallas kernels, reduce_all(): pl.pallas_call(functools.partial(reduce_kernel, chunks, len(parts)), out_...  155 us
    pallas_call x1, Pallas kernels, gather_all(): pl.pallas_call(functools.partial(gather_kernel, chunks, len(shards)), out...  143 us
    dot_general x7, matrix products, outer(): lax.dot_general(left, grad, (((0,), (0,)), ((), ())), preferred_element_t...  33.6 us
    dot_general x7, matrix products, project(): jnp.einsum('bld,de->ble', left, weight, preferred_element_type=jnp.float32)  32.3 us
    dot_general x7, matrix products, project_back(): jnp.einsum('ble,de->bld', grad, weight, preferred_element_type=jnp.float32)  32 us
    unnamed x123, local copies, waits for them, and re-layouts  30.3 us
    convert_element_type x4, local copies, waits for them, and re-layouts, attend_back(): grad_values.reshape(values.shape).astype(jnp.bfloat16)  18.6 us
    convert_element_type x4, local copies, waits for them, and re-layouts, attend_back(): grad_keys.reshape(keys.shape).astype(jnp.bfloat16)  15.5 us

profile of v2, /device:TPU:0, one launch (start us, length us, event | category | flops | bytes accessed | tf_op | source)
XLA Modules:
  0.0 563.1 jit_solution(8517639187604050639)
XLA Ops:
  7.3 143.2 %shard_map.297 = (bf16[2,2,4,2,32,2048]{5,4,3,2,1,0:T(8,128)(2,1)}, bf16[2,2,4,2,32,4224]{5,4,3,2,1,0:T(8,128)(2,1)}, bf16[2,2,4,2,32,2048]{5,4,3,2,1,0:T(8,128)...) custom-call(bf16[32,2048]{1,0:T(8,128)(2,1)} %get-tuple-element.135.refs_0_, ...), custom_call_target="tpu_custom_call" | custom-call | tf_op jit(solution)/shard_map/pallas_call | solution.py:289
  152.7 4.7 fusion.23
  170.4 8.2 %convert_bitcast_fusion = bf16[2,588,2048]{2,1,0:T(8,128)(2,1)S(1)} fusion(bf16[1024,2048,1]{1,0,2:T(8,128)(2,1)} %bitcast.290, bf16[2,588,1024]{2,0,1:T(2,128)(2,1)} %bitcast.255), kind=kOutput, calls=%fused_computation.25 | convolution fusion | flops 4934909952 | bytes 11419648 | tf_op jit(solution)/shard_map/bld,de->ble/dot_general | solution.py:558
  181.3 4.4 copy.121
  185.8 4.5 fusion.22
  194.0 4.5 copy.119
  198.5 7.7 %fusion.52 = bf16[2,16,64,128]{3,2,1,0:T(8,128)(2,1)S(1)} fusion(bf16[2,588,16,64]{1,3,2,0:T(8,128)(2,1)} %bitcast.238, f32[2,16,128]{2,1,0:T(8,128)S(1)} %fusion, f32[2,16,128]{2,1,0:T(8,128)S(1)} %get-tuple-element.123, f32[2,16,128,588]{2,3,1,0:T(8,128)} %copy-done, pred[2,588]{1,0:T(4,128)(4,1)S(1)} %iota_compare_fusion.2), kind=kOutput, calls=%fused_computation.94 | convolution fusion | flops 320585728 | bytes 12600472 | tf_op jit(solution)/shard_map/bhqk,bkhd->bqhd/dot_general | solution.py:597
  207.3 7.8 %fusion.71 = (u8[128,4096]{1,0:T(8,128)(4,1)S(1)}, u8[128,4096]{1,0:T(8,128)(4,1)S(1)}, f32[2,128,4096]{2,1,0:T(8,128)S(1)}) fusion(bf16[1024,4096,1]{1,0,2:T(8,128)(2,1)} %bitcast.288, f32[2,128,1024]{2,1,0:T(8,128)S(1)} %get-tuple-element.126, f32[1024]{0:T(1024)S(1)} %get-tuple-element.101, f32[2,128]{1,0:T(2,128)S(1)} %add_rsqrt_fusion, ...), kind=kOutput, calls=%fused_computation.122 | convolution fusion | flops 2161115136 | bytes 14686208 | tf_op jit(solution)/shard_map/bld,de->ble/dot_general | solution.py:558
  215.1 10.5 %multiply_convert_fusion.2 = (bf16[2,128,4096]{2,1,0:T(8,128)(2,1)}, f32[2,128,4096]{2,1,0:T(8,128)S(1)}) fusion(f32[2,128,4096]{2,1,0:T(8,128)S(1)} %get-tuple-element.127, u8[128,4096]{1,0:T(8,128)(4,1)S(1)} %get-tuple-element.91, u8[128,4096]{1,0:T(8,128)(4,1)S(1)} %get-tuple-element.90), kind=kLoop, calls=%fused_computation.39 | loop fusion | flops 73400320 | bytes 11534336 | tf_op jit(solution)/shard_map/convert_element_type | solution.py:706
  225.6 3.7 add_convert_fusion
  229.3 6.8 %multiply_reduce_fusion.2 = (f32[1024]{0:T(1024)S(1)}, f32[2,128]{1,0:T(2,128)S(1)}, f32[2,128]{1,0:T(2,128)S(1)}, f32[2,128,1024]{2,1,0:T(8,128)S(1)}) fusion(f32[2,128,1024]{2,1,0:T(8,128)S(1)} %get-tuple-element.126, f32[2,128]{1,0:T(2,128)S(1)} %add_rsqrt_fusion, f32[2,128]{1,0:T(2,128)S(1)} %broadcast_multiply_fusion.6, ...), kind=kOutput, calls=%fused_computation.110 | convolution fusion | flops 2149579264 | bytes 12595200 | tf_op jit(solution)/shard_map/ble,de->bld/dot_general | solution.py:562
  241.2 8.4 %multiply_reduce_fusion = (f32[2,16,128]{2,1,0:T(8,128)S(1)}, f32[2,16,128,588]{2,3,1,0:T(8,128)S(1)}) fusion(f32[2,16,128]{2,1,0:T(8,128)S(1)} %log_add_fusion.1, f32[2,16,128,588]{2,3,1,0:T(8,128)} %copy-done, pred[2,588]{1,0:T(4,128)(4,1)S(1)} %iota_compare_fusion.2, bf16[2,128,16,64]{1,3,2,0:T(8,128)(2,1)} %bitcast.244, ...), kind=kOutput, calls=%fused_computation.3 | convolution fusion | flops 320319488 | bytes 22234264 | tf_op jit(solution)/shard_map/bqhd,bkhd->bhqk/dot_general | solution.py:612
  249.6 3.3 multiply_convert_fusion
  259.4 3.2 fusion.51
  280.5 6.4 %fusion.66 = (f32[1024]{0:T(1024)S(1)}, f32[2,128]{1,0:T(2,128)S(1)}, f32[2,128]{1,0:T(2,128)S(1)}, f32[2,128,1024]{2,1,0:T(8,128)}) fusion(bf16[2,1,128,1024]{3,2,1,0:T(8,128)(2,1)} %param.18, f32[2,128]{1,0:T(2,128)S(1)} %add_rsqrt_fusion.2, f32[2,128]{1,0:T(2,128)S(1)} %broadcast_multiply_fusion.8, f32[1024]{0:T(1024)S(1)} %get-tuple-element.103, ...), kind=kOutput, calls=%fused_computation.108 | convolution fusion | flops 1617689088 | bytes 9449472 | tf_op jit(solution)/shard_map/ble,de->bld/dot_general | solution.py:562
  287.5 5.7 %bitcast_convert_fusion.1 = bf16[1024,3072]{1,0:T(8,128)(2,1)} fusion(bf16[2,128,1024]{2,1,0:T(8,128)(2,1)} %copy-done.42, bf16[2,128,1024]{2,1,0:T(8,128)(2,1)S(1)} %copy-done.41, bf16[2,128,1024]{2,1,0:T(8,128)(2,1)S(1)} %copy-done.40, bf16[2,1,128,1024]{3,2,1,0:T(8,128)(2,1)S(1)} %copy-done.18, f32[1024]{0:T(1024)S(1)} %get-tuple-element.103, ...), kind=kOutput, calls=%fused_computation.1 | convolution fusion | flops 1619787776 | bytes 8394752 | tf_op jit(solution)/shard_map/dot_general | solution.py:549
  296.5 4.4 copy.138
  300.8 6.5 %convert_element_type.239 = bf16[1176,1024]{0,1:T(8,128)(2,1)} reshape(bf16[2,588,16,64]{1,0,3,2:T(2,128)(2,1)} %copy.138) | data formatting | bytes 4816896 | tf_op jit(solution)/shard_map/convert_element_type | solution.py:632
  307.3 7.8 %fusion.31 = bf16[2,16,64,588]{3,2,1,0:T(8,128)(2,1)} fusion(bf16[2,128,16,64]{1,3,2,0:T(8,128)(2,1)S(1)} %bitcast.245, f32[2,16,128]{2,1,0:T(8,128)S(1)} %log_add_fusion.1, f32[2,16,128,588]{2,3,1,0:T(8,128)} %copy-done, pred[2,588]{1,0:T(4,128)(4,1)S(1)} %iota_compare_fusion.2), kind=kOutput, calls=%fused_computation.66 | convolution fusion | flops 319119360 | bytes 12584088 | tf_op jit(solution)/shard_map/bhqk,bqhd->bkhd/dot_general | solution.py:606
  315.1 5.9 %copy.139 = bf16[2,588,16,64]{1,0,3,2:T(2,128)(2,1)} copy(bf16[2,588,16,64]{1,3,2,0:T(8,128)(2,1)} %bitcast.52) | data formatting | bytes 4816896 | tf_op jit(solution)/shard_map/convert_element_type | solution.py:633
  321.0 6.9 %convert_element_type.240 = bf16[1176,1024]{0,1:T(8,128)(2,1)} reshape(bf16[2,588,16,64]{1,0,3,2:T(2,128)(2,1)} %copy.139) | data formatting | bytes 4816896 | tf_op jit(solution)/shard_map/convert_element_type | solution.py:633
  327.9 3.8 copy.140
  331.8 3.6 reshape_squeeze.3
  335.3 10.2 %fusion.24 = bf16[2048,1024]{0,1:T(8,128)(2,1)} fusion(bf16[1176,1024]{1,0:T(8,128)(2,1)} %reshape_squeeze.3, bf16[1176,1024]{0,1:T(8,128)(2,1)} %convert_element_type.240, bf16[1176,1024]{0,1:T(8,128)(2,1)} %convert_element_type.239), kind=kOutput, calls=%fused_computation.54 | convolution fusion | flops 4944232448 | bytes 11419648 | tf_op jit(solution)/shard_map/dot_general | solution.py:549
  349.9 5.8 %bitcast_convert_fusion = bf16[1024,4096]{1,0:T(8,128)(2,1)} fusion(bf16[2,128,4096]{2,1,0:T(8,128)(2,1)S(1)} %copy-done.28, f32[2,128,1024]{2,1,0:T(8,128)S(1)} %copy-done.6, f32[1024]{0:T(1024)S(1)} %get-tuple-element.101, f32[2,128]{1,0:T(2,128)S(1)} %add_rsqrt_fusion, f32[2,128]{1,0:T(2,128)S(1)} %broadcast_multiply_fusion.6), kind=kOutput, calls=%fused_computation | convolution fusion | flops 2152726528 | bytes 11540480 | tf_op jit(solution)/shard_map/dot_general | solution.py:549
  357.7 5.6 convolution_convert_fusion
  363.3 155.4 %shard_map.298 = (f32[128,1024]{1,0:T(8,128)}, f32[32,4096]{1,0:T(8,128)}, f32[32,1024]{1,0:T(8,128)}, f32[32,1024]{1,0:T(8,128)}, f32[32,2048]{1,0:T(8,128)}, /...) custom-call(bf16[2,2,4,2,128,1024]{5,4,3,2,1,0:T(8,128)(2,1)} %bitcast.229, ...), custom_call_target="tpu_custom_call" | custom-call | tf_op jit(solution)/shard_map/pallas_call | solution.py:508
  526.0 4.5 copy.134
  530.5 9.4 %fusion.28 = f32[2,1,588,1024]{3,2,0,1:T(8,128)} fusion(bf16[1024,2048,1]{1,0,2:T(8,128)(2,1)} %bitcast.291, bf16[2,588,1024]{2,1,0:T(8,128)(2,1)} %copy.134, bf16[2,588,1024]{2,1,0:T(8,128)(2,1)S(1)} %copy-done.24), kind=kOutput, calls=%fused_computation.56 | convolution fusion | flops 4942135296 | bytes 13828096 | tf_op jit(solution)/shard_map/ble,de->bld/dot_general | solution.py:562
  539.9 9.7 %copy.144 = f32[2,1,588,1024]{3,1,2,0:T(1,128)} copy(f32[2,1,588,1024]{3,2,0,1:T(8,128)} %fusion.28) | data formatting | bytes 9633792
  549.6 3.0 fusion.65
  552.7 6.6 %fusion.59 = bf16[2,1,128,1024]{3,2,1,0:T(8,128)(2,1)} fusion(f32[2,128,1024]{2,1,0:T(8,128)S(1)} %copy-done.7, bf16[2,128,4096]{2,1,0:T(8,128)(2,1)S(1)} %copy-done.9, bf16[4096,1024,1]{1,0,2:T(8,128)(2,1)} %bitcast.284), kind=kOutput, calls=%fused_computation.101 | convolution fusion | flops 2148007936 | bytes 12058624 | tf_op jit(solution)/shard_map/bld,de->ble/dot_general | solution.py:558
  (190 shorter events, 79.7 us)
Async XLA Ops:
  0.6 151.6 %copy-start.16 = (bf16[2,1,128,1024]{3,2,1,0:T(8,128)(2,1)S(1)}, bf16[2,1,128,1024]{3,2,1,0:T(8,128)(2,1)}, u32[]{:S(2)}) copy-start(bf16[2,1,128,1024]{3,2,1,0:T(8,128)(2,1)} %param.18) | copy-start | bytes 1572868
  198.5 7.7 %copy-start.36 = (bf16[2,2,4,2,32,2048]{5,4,3,2,1,0:T(8,128)(2,1)S(1)}, bf16[2,2,4,2,32,2048]{5,4,3,2,1,0:T(8,128)(2,1)}, u32[]{:S(2)}) copy-start(bf16[2,2,4,2,32,2048]{5,4,3,2,1,0:T(8,128)(2,1)} %get-tuple-element.31) | copy-start | bytes 12582916
  206.2 19.4 %slice-start.5 = ((s8[8388608]{0:T(1024)(128)(4,1)}), s8[4194304]{0:T(1024)(128)(4,1)S(1)}, s32[]{:S(2)}) async-start(s8[8388608]{0:T(1024)(128)(4,1)} %bitcast.285), calls=%async_computation.5 | async-start | bytes 8388608
  207.0 29.1 %copy-start.5 = (f32[2,128,1024]{2,1,0:T(8,128)}, f32[2,128,1024]{2,1,0:T(8,128)S(1)}, u32[]{:S(2)}) copy-start(f32[2,128,1024]{2,1,0:T(8,128)S(1)} %get-tuple-element.126) | copy-start | bytes 3145732
  207.3 18.3 %slice-start.6 = ((s8[8388608]{0:T(1024)(128)(4,1)}), s8[4194304]{0:T(1024)(128)(4,1)S(1)}, s32[]{:S(2)}) async-start(s8[8388608]{0:T(1024)(128)(4,1)} %bitcast.285), calls=%async_computation.6 | async-start | bytes 8388608
  215.1 10.5 %copy-start.25 = (bf16[2,1,128,1024]{3,2,1,0:T(8,128)(2,1)S(1)}, bf16[2,1,128,1024]{3,2,1,0:T(8,128)(2,1)}, u32[]{:S(2)}) copy-start(bf16[2,1,128,1024]{3,2,1,0:T(8,128)(2,1)} %param.20) | copy-start | bytes 1572868
  229.3 6.8 %copy-start.27 = (bf16[2,128,4096]{2,1,0:T(8,128)(2,1)}, bf16[2,128,4096]{2,1,0:T(8,128)(2,1)S(1)}, u32[]{:S(2)}) copy-start(bf16[2,128,4096]{2,1,0:T(8,128)(2,1)S(1)} %add_convert_fusion) | copy-start | bytes 6291460
  241.1 8.4 %slice-start = ((s8[9699328]{0:T(1024)(128)(4,1)}), s8[4194304]{0:T(1024)(128)(4,1)S(1)}, s32[]{:S(2)}) async-start(s8[9699328]{0:T(1024)(128)(4,1)} %bitcast.227), calls=%async_computation | async-start | bytes 8388608
  241.1 8.4 %slice-start.1 = ((s8[9699328]{0:T(1024)(128)(4,1)}), s8[4194304]{0:T(1024)(128)(4,1)S(1)}, s32[]{:S(2)}) async-start(s8[9699328]{0:T(1024)(128)(4,1)} %bitcast.227), calls=%async_computation.1 | async-start | bytes 8388608
  241.1 8.4 %slice-start.2 = ((s8[9699328]{0:T(1024)(128)(4,1)}), s8[1310720]{0:T(1024)(128)(4,1)S(1)}, s32[]{:S(2)}) async-start(s8[9699328]{0:T(1024)(128)(4,1)} %bitcast.227), calls=%async_computation.2 | async-start | bytes 2621440
  252.9 5.2 copy-start.1
  279.1 14.1 %slice-start.3 = ((s8[4849664]{0:T(1024)(128)(4,1)}), s8[655360]{0:T(1024)(128)(4,1)S(1)}, s32[]{:S(2)}) async-start(s8[4849664]{0:T(1024)(128)(4,1)} %bitcast.230), calls=%async_computation.3 | async-start | bytes 1310720
  280.4 6.4 %copy-start.42 = (bf16[2,128,1024]{2,1,0:T(8,128)(2,1)}, bf16[2,128,1024]{2,1,0:T(8,128)(2,1)S(1)}, u32[]{:S(2)}) copy-start(bf16[2,128,1024]{2,1,0:T(8,128)(2,1)S(1)} %copy.132) | copy-start | bytes 1572868
  280.4 7.1 %copy-start.18 = (bf16[2,1,128,1024]{3,2,1,0:T(8,128)(2,1)S(1)}, bf16[2,1,128,1024]{3,2,1,0:T(8,128)(2,1)}, u32[]{:S(2)}) copy-start(bf16[2,1,128,1024]{3,2,1,0:T(8,128)(2,1)} %param.18) | copy-start | bytes 1572868
  280.4 7.1 %copy-start.40 = (bf16[2,128,1024]{2,1,0:T(8,128)(2,1)S(1)}, bf16[2,128,1024]{2,1,0:T(8,128)(2,1)}, u32[]{:S(2)}) copy-start(bf16[2,128,1024]{2,1,0:T(8,128)(2,1)} %copy.130) | copy-start | bytes 1572868
  280.5 7.0 %copy-start.41 = (bf16[2,128,1024]{2,1,0:T(8,128)(2,1)S(1)}, bf16[2,128,1024]{2,1,0:T(8,128)(2,1)}, u32[]{:S(2)}) copy-start(bf16[2,128,1024]{2,1,0:T(8,128)(2,1)} %copy.131) | copy-start | bytes 1572868
  280.5 12.8 %slice-start.4 = ((s8[4849664]{0:T(1024)(128)(4,1)}), s8[4194304]{0:T(1024)(128)(4,1)S(1)}, s32[]{:S(2)}) async-start(s8[4849664]{0:T(1024)(128)(4,1)} %bitcast.230), calls=%async_computation.4 | async-start | bytes 8388608
  287.5 5.7 %copy-start.23 = (bf16[2,128,1024]{1,2,0:T(8,128)(2,1)S(1)}, bf16[2,128,1024]{1,2,0:T(8,128)(2,1)}, u32[]{:S(2)}) copy-start(bf16[2,128,1024]{1,2,0:T(8,128)(2,1)} %copy.120) | copy-start | bytes 1572868
  296.5 10.9 %copy-start.19 = (bf16[2,128,1024]{1,2,0:T(8,128)(2,1)S(1)}, bf16[2,128,1024]{1,2,0:T(8,128)(2,1)}, u32[]{:S(2)}) copy-start(bf16[2,128,1024]{1,2,0:T(8,128)(2,1)} %copy.124) | copy-start | bytes 1572868
  335.3 10.2 %copy-start.34 = (bf16[2,16,64,128]{3,2,1,0:T(8,128)(2,1)S(1)}, bf16[2,16,64,128]{3,2,1,0:T(8,128)(2,1)}, u32[]{:S(2)}) copy-start(bf16[2,16,64,128]{3,2,1,0:T(8,128)(2,1)} %copy-done.33) | copy-start | bytes 1572868
  335.3 12.5 %copy-start.32 = (bf16[2,16,64,128]{3,2,1,0:T(8,128)(2,1)S(1)}, bf16[2,16,64,128]{3,2,1,0:T(8,128)(2,1)}, u32[]{:S(2)}) copy-start(bf16[2,16,64,128]{3,2,1,0:T(8,128)(2,1)} %copy-done.31) | copy-start | bytes 1572868
  349.9 5.8 %copy-start.11 = (f32[2,128,1024]{2,1,0:T(8,128)S(1)}, f32[2,128,1024]{2,1,0:T(8,128)}, u32[]{:S(2)}) copy-start(f32[2,128,1024]{2,1,0:T(8,128)} %copy-done.10) | copy-start | bytes 3145732
  349.9 5.8 %copy-start.30 = (bf16[2,16,64,128]{3,2,1,0:T(8,128)(2,1)S(1)}, bf16[2,16,64,128]{3,2,1,0:T(8,128)(2,1)}, u32[]{:S(2)}) copy-start(bf16[2,16,64,128]{3,2,1,0:T(8,128)(2,1)} %copy-done.29) | copy-start | bytes 1572868
  349.9 7.8 %copy-start.26 = (bf16[2,1,128,1024]{3,2,1,0:T(8,128)(2,1)S(1)}, bf16[2,1,128,1024]{3,2,1,0:T(8,128)(2,1)}, u32[]{:S(2)}) copy-start(bf16[2,1,128,1024]{3,2,1,0:T(8,128)(2,1)} %param.20) | copy-start | bytes 1572868
  363.3 160.2 %copy-start.3 = (bf16[2,16,64,588]{3,2,1,0:T(8,128)(2,1)S(1)}, bf16[2,16,64,588]{3,2,1,0:T(8,128)(2,1)}, u32[]{:S(2)}) copy-start(bf16[2,16,64,588]{3,2,1,0:T(8,128)(2,1)} %copy-done.2) | copy-start | bytes 7225348
  539.9 12.7 %copy-start.7 = (f32[2,128,1024]{2,1,0:T(8,128)S(1)}, f32[2,128,1024]{2,1,0:T(8,128)}, u32[]{:S(2)}) copy-start(f32[2,128,1024]{2,1,0:T(8,128)} %copy-done.5) | copy-start | bytes 3145732
  539.9 12.7 %copy-start.9 = (bf16[2,128,4096]{2,1,0:T(8,128)(2,1)S(1)}, bf16[2,128,4096]{2,1,0:T(8,128)(2,1)}, u32[]{:S(2)}) copy-start(bf16[2,128,4096]{2,1,0:T(8,128)(2,1)} %get-tuple-element.104) | copy-start | bytes 6291460
  552.7 6.7 %copy-start.46 = (f32[32,1024]{1,0:T(8,128)S(1)}, f32[32,1024]{1,0:T(8,128)}, u32[]{:S(2)}) copy-start(f32[32,1024]{1,0:T(8,128)} %get-tuple-element.160) | copy-start | bytes 393220
  552.7 7.3 %copy-start.45 = (f32[32,1024]{1,0:T(8,128)S(1)}, f32[32,1024]{1,0:T(8,128)}, u32[]{:S(2)}) copy-start(f32[32,1024]{1,0:T(8,128)} %get-tuple-element.162) | copy-start | bytes 393220
  552.7 8.0 %copy-start.44 = (f32[32,1024]{1,0:T(8,128)S(1)}, f32[32,1024]{1,0:T(8,128)}, u32[]{:S(2)}) copy-start(f32[32,1024]{1,0:T(8,128)} %get-tuple-element.165) | copy-start | bytes 393220
  552.7 8.6 %copy-start.39 = (f32[32,4096]{1,0:T(8,128)S(1)}, f32[32,4096]{1,0:T(8,128)}, u32[]{:S(2)}) copy-start(f32[32,4096]{1,0:T(8,128)} %get-tuple-element.167) | copy-start | bytes 1572868
  552.7 9.4 %copy-start.38 = (f32[128,1024]{1,0:T(8,128)S(1)}, f32[128,1024]{1,0:T(8,128)}, u32[]{:S(2)}) copy-start(f32[128,1024]{1,0:T(8,128)} %get-tuple-element.168) | copy-start | bytes 1572868
  (24 other events, 69.9 us)

commit v3 on v2

--- a/solution.py
+++ b/solution.py
@@ -300,97 +300,167 @@
 
 
 RING = 4
-
-
-def reduce_kernel(chunks, count, *refs):
+BLOCK = 256
+SPARE = 3
+
+
+def back_kernel(dims, *refs):
+    pages, length, slots = dims
+    it = iter(refs)
+
+    def take(k):
+        return [next(it) for _ in range(k)]
+
+    (hidden_in, pre_in, third_in, out_in, cross_in, cctx_in, second_in, cq_in, kv_in, memory_in,
+     self_in, ctx_in, first_in, qkv_in, x_in, wqo_in, wkv_in, wself_in) = take(18)
+    counts, lengths, gains, gain_three, lse_cross, lse_self = take(6)
+    grad_outs = take(7)
+    gain_out, input_out, memory_out = take(3)
+    (hidden, pre, third, out_grad, cross, cctx, second, cq, kv, memory, after_self, ctx, first, qkv, x_bf,
+     w_a, w_b, branch, g_ctx, stage) = take(20)
+    send0, got0, parts, got1, halves, got2, line, got3, gain_sum, gain_got = take(10)
+    local, s0, r0, s1, r1, s2, r2, s3, r3, gs, gr, free = take(12)
+
     grid = Grid()
     n, depth = grid.n, grid.depth
     y, c, z, x = grid.at
-    parts, gain_in = refs[:count], refs[count]
-    outs, gain_out = refs[count + 1 : 2 * count + 1], refs[2 * count + 1]
-    (own, got0, send1, got1, keep1, send2, got2, keep2, line, got3, gain_sum, gain_got) = refs[
-        2 * count + 2 : 2 * count + 14
-    ]
-    local, s0, r0, s1, r1, s2, r2, s3, r3, gs, gr = refs[2 * count + 14 :]
-    rows, width = own.shape[-2:]
+    rows, width = send0.shape[-2:]
+    f32, bf16 = jnp.float32, jnp.bfloat16
+    copies, loads = {}, {}
+
+    def fetch(name, src, dst, slot):
+        loads[name] = pltpu.make_async_copy(src, dst, local.at[slot])
+        loads[name].start()
+
+    def need(*names):
+        for name in names:
+            copy = loads.pop(name, None)
+            if copy is not None:
+                copy.wait()
+
+    D = x_bf.shape[1]
+    fetch("hidden", hidden_in, hidden, 0)
+    fetch("out", out_in, out_grad, 1)
+    fetch("pre", pre_in, pre, 2)
+    fetch("third", third_in, third, 3)
+    fetch("cross", cross_in, cross, 4)
+    fetch("wqo", wqo_in, w_a, 15)
+    grid.meet()
+    fetch("cctx", cctx_in, cctx, 5)
+    fetch("cq", cq_in, cq, 7)
+    fetch("kv", kv_in, kv, 8)
+    fetch("second", second_in, second, 6)
+    fetch("memory", memory_in, memory, 9)
+    fetch("self", self_in, after_self, 10)
+    fetch("ctx", ctx_in, ctx, 11)
+    fetch("first", first_in, first, 12)
+    fetch("qkv", qkv_in, qkv, 13)
+    fetch("x", x_in, x_bf, 14)
+    fetch("wo", wself_in.at[:, pl.ds(3 * D, D)], w_b.at[:, pl.ds(0, D)], 16)
+    fetch("wq", wself_in.at[:, pl.ds(0, D)], w_b.at[:, pl.ds(D, D)], 17)
+
+    chunks = []
+    wide = hidden.shape[1] // grid.devices
+    for col in range(0, D, width * rows // wide):
+        chunks.append((0, hidden, out_grad, col, ("hidden", "out")))
+    for col in range(0, pre.shape[1], width):
+        chunks.append((1, third, pre, col, ("third", "pre")))
+    chunks.append((2, cctx, branch, 0, ("cctx",)))
+    chunks.append((3, second, cq, 0, ("second",)))
+    chunks.append((4, memory, kv, 0, ("memory",)))
+    chunks.append((4, memory, kv, D, ()))
+    chunks.append((5, ctx, branch, 0, ("ctx",)))
+    for col in range(0, 3 * D, width):
+        chunks.append((6, first, qkv, col, ("first",)))
     total = len(chunks)
-    f32, bf16 = jnp.float32, jnp.bfloat16
-    grid.meet()
-    copies = {}
-
-    def half(i, core):
-        m, row, col = chunks[i]
-        return parts[m].at[:, core, :, :, pl.ds(row, rows), pl.ds(col, width)]
-
-    def reuse(i, stage):
+
+    def products(i, core, emit):
+        _, left, right, col, names = chunks[i]
+        need(*names)
+        own = left.shape[1] // grid.devices
+        span = left.shape[1] // (n * CORES)
+        lanes = width * rows // own
+
+        def body(yy, carry):
+            at = pl.multiple_of((yy * CORES + core) * span, min(span, BLOCK))
+            value = lax.dot_general(
+                left[:, pl.ds(at, span)],
+                right[:, pl.ds(col, lanes)],
+                (((0,), (0,)), ((), ())),
+                preferred_element_type=f32,
+            )
+            for k in range(depth * n):
+                for part in range(own // rows):
+                    top = k * own + part * rows
+                    emit(yy, k // n, k % n, part * lanes, lanes, value[top : top + rows])
+            return carry
+
+        lax.fori_loop(0, n, body, 0)
+
+    def reuse(i, stage, ring):
+        if i >= ring:
+            for copy in copies[i - ring, stage]:
+                copy.wait_send()
+
+    def stage0(i):
+        s = i % SPARE
+        reuse(i, 0, SPARE)
+
+        def emit(yy, zz, xx, lane, lanes, value):
+            send0[s, yy, zz, xx, :, pl.ds(lane, lanes)] = value.astype(bf16)
+
+        products(i, 1 - c, emit)
         if i >= RING:
-            for copy in copies[i - RING, stage]:
-                copy.wait_send()
-
-    def load(i):
-        copies[i, "own"] = pltpu.make_async_copy(half(i, c), own.at[i % RING], local.at[i % RING])
-        copies[i, "own"].start()
-
-    def stage0(i):
-        copies[i, 0] = [
-            started(half(i, 1 - c), got0.at[i], s0.at[i], r0.at[i], grid.partner())
-        ]
+            pl.semaphore_wait(free, 1)
+        copies[i, 0] = [started(send0.at[s], got0.at[i % RING], s0.at[s], r0.at[i % RING], grid.partner())]
 
     def stage1(i):
         s = i % RING
-        reuse(i, 1)
-        copies[i, "own"].wait()
+        reuse(i, 1, RING)
         copies[i, 0][0].wait_recv()
 
-        def add(dst, a, b):
-            yy, xx = grid.place(a, b)
-
-            def body(zz, carry):
-                total_ = own[s, yy, zz, xx].astype(f32) + got0[i, yy, zz, xx].astype(f32)
-                dst[zz] = total_.astype(bf16)
-                return carry
-
-            lax.fori_loop(0, depth, body, 0)
-
-        copies[i, 1] = []
-        for a in range(1, n):
-            for b in range(n):
-                add(send1.at[s, a - 1, b], a, b)
-            copies[i, 1].append(
-                started(
-                    send1.at[s, a - 1],
-                    got1.at[i, a - 1],
-                    s1.at[s, a - 1],
-                    r1.at[i, a - 1],
-                    grid.step_plane(a, 0),
-                )
+        def emit(yy, zz, xx, lane, lanes, value):
+            value = value + got0[s, yy, zz, xx, :, pl.ds(lane, lanes)].astype(f32)
+            to_y = lax.rem(yy - y + n, n)
+            to_x = lax.rem(xx - x + n, n)
+            a = to_x * (1 - c) + to_y * c
+            b = to_y * (1 - c) + to_x * c
+            parts[s, a, b, zz, :, pl.ds(lane, lanes)] = value.astype(bf16)
+
+        products(i, c, emit)
+        if i + RING < total:
+            pl.semaphore_signal(free, inc=1, device_id=grid.partner(), device_id_type=MESH)
+        copies[i, 1] = [
+            started(
+                parts.at[s, a],
+                got1.at[i, a - 1],
+                s1.at[s, a - 1],
+                r1.at[i, a - 1],
+                grid.step_plane(a, 0),
             )
-        for b in range(n):
-            add(keep1.at[s, b], 0, b)
-        if i + RING < total:
-            load(i + RING)
+            for a in range(1, n)
+        ]
 
     def stage2(i):
         s = i % RING
-        reuse(i, 2)
+        reuse(i, 2, RING)
         for copy in copies[i, 1]:
             copy.wait_recv()
         copies[i, 2] = []
         for b in list(range(1, n)) + [0]:
-            dst = send2.at[s, b - 1] if b else keep2.at[s]
 
             def body(zz, carry):
-                total_ = keep1[s, b, zz].astype(f32)
+                value = parts[s, 0, b, zz].astype(f32)
                 for a in range(1, n):
-                    total_ = total_ + got1[i, a - 1, b, zz].astype(f32)
-                dst[zz] = total_.astype(bf16)
+                    value = value + got1[i, a - 1, b, zz].astype(f32)
+                halves[s, b, zz] = value.astype(bf16)
                 return carry
 
             lax.fori_loop(0, depth, body, 0)
             if b:
                 copies[i, 2].append(
                     started(
-                        send2.at[s, b - 1],
+                        halves.at[s, b],
                         got2.at[i, b - 1],
                         s2.at[s, b - 1],
                         r2.at[i, b - 1],
@@ -400,15 +470,15 @@
 
     def stage3(i):
         s = i % RING
-        reuse(i, 3)
+        reuse(i, 3, RING)
         for copy in copies[i, 2]:
             copy.wait_recv()
 
         def body(zz, carry):
-            total_ = keep2[s, zz].astype(f32)
+            value = halves[s, 0, zz].astype(f32)
             for b in range(1, n):
-                total_ = total_ + got2[i, b - 1, zz].astype(f32)
-            line[s, zz] = total_.astype(bf16)
+                value = value + got2[i, b - 1, zz].astype(f32)
+            line[s, zz] = value.astype(bf16)
             return carry
 
         lax.fori_loop(0, depth, body, 0)
@@ -424,13 +494,20 @@
         ]
 
     def stage4(i):
-        m, row, col = chunks[i]
+        m, left, _, col, _ = chunks[i]
         for copy in copies[i, 3]:
             copy.wait_recv()
-        total_ = line[i % RING, z].astype(f32)
+        value = line[i % RING, z].astype(f32)
         for k in range(1, depth):
-            total_ = total_ + got3[i, k - 1].astype(f32)
-        outs[m][pl.ds(row, rows), pl.ds(col, width)] = total_
+            value = value + got3[i, k - 1].astype(f32)
+        own = left.shape[1] // grid.devices
+        if own == rows:
+            grad_outs[m][:, pl.ds(col, width)] = value
+        else:
+            for part in range(own // rows):
+                grad_outs[m][pl.ds(part * rows, rows), pl.ds(col, BLOCK)] = value[
+                    :, part * BLOCK : (part + 1) * BLOCK
+                ]
 
     moves = [
         [grid.partner()],
@@ -439,30 +516,196 @@
         [grid.step_z(k) for k in range(1, depth)],
         [],
     ]
-    first = [0, 1, n, 2 * n - 1, 2 * n + depth - 2]
+    start = [0, 1, n, 2 * n - 1, 2 * n + depth - 2]
 
     def gain_step(h):
-        total_ = gain_in[...]
+        value = gain_sum[min(h, 3)]
         if h:
-            total_ = gain_sum[h - 1]
             for j, copy in enumerate(copies["gain", h - 1]):
                 copy.wait_recv()
-                total_ = total_ + gain_got[first[h - 1] + j]
+                value = value + gain_got[start[h - 1] + j]
         if h == len(moves) - 1:
-            gain_out[...] = total_
-        else:
-            gain_sum[h] = total_
+            gain_out[...] = value
+        elif h:
+            gain_sum[h] = value
+        if h < len(moves) - 2:
+            gain_sum[h + 1] = value
         copies["gain", h] = [
             started(
                 gain_sum.at[h],
-                gain_got.at[first[h] + j],
-                gs.at[first[h] + j],
-                gr.at[first[h] + j],
+                gain_got.at[start[h] + j],
+                gs.at[start[h] + j],
+                gr.at[start[h] + j],
                 device,
             )
             for j, device in enumerate(moves[h])
         ]
 
+    def times_transposed(left, right):
+        return lax.dot_general(left, right, (((1,), (1,)), ((), ())), preferred_element_type=f32)
+
+    def round_branch():
+        need("cross")
+
+        def body(k, carry):
+            at = pl.ds(k * 32, 32)
+            branch[at] = cross[at].astype(bf16)
+            return carry
+
+        lax.fori_loop(0, cross.shape[0] // 32, body, 0)
+
+    def context_grad(weight, col):
+        def body(k, carry):
+            at = pl.multiple_of(k * BLOCK, BLOCK)
+            g_ctx[:, pl.ds(at, BLOCK)] = times_transposed(
+                branch[...], weight[pl.ds(at, BLOCK), pl.ds(col, D)]
+            ).astype(bf16)
+            return carry
+
+        lax.fori_loop(0, D // BLOCK, body, 0)
+
+    lane = lax.broadcasted_iota(jnp.int32, (length, 2 * HD), 1)
+    scale = HD ** (-0.5)
+
+    def attention(page, pair, q_ref, q_col, k_ref, k_row, k_rows, k_col, v_col, lse, allowed):
+        def lanes(col):
+            return pl.ds(pl.multiple_of(col + pair * 2 * HD, 2 * HD), 2 * HD)
+
+        q_at = pl.ds(page * length, length)
+        k_at = pl.ds(k_row, k_rows)
+        queries, grads = q_ref[q_at, lanes(q_col)], g_ctx[q_at, lanes(0)]
+        keys, values = k_ref[k_at, lanes(k_col)], k_ref[k_at, lanes(v_col)]
+        g_keys = g_values = None
+        g_queries = []
+        for h in range(2):
+            mine = (lane // HD) == h
+            q = jnp.where(mine, queries, jnp.zeros_like(queries))
+            g = jnp.where(mine, grads, jnp.zeros_like(grads))
+            scores = times_transposed(keys, q) * scale
+            scores = jnp.where(allowed, scores, -1000000000.0)
+            row = page * (D // HD) + pair * 2 + h
+            probs = jnp.exp(scores - lse[pl.ds(row, 1), :])
+            g_probs = times_transposed(values, g)
+            inner = jnp.sum(probs * g_probs, axis=0, keepdims=True)
+            g_scores = (probs * (g_probs - inner)).astype(bf16)
+            g_v = jnp.dot(probs.astype(bf16), g, preferred_element_type=f32)
+            g_k = jnp.dot(g_scores, q, preferred_element_type=f32)
+            g_queries.append(
+                lax.dot_general(
+                    g_scores, keys, (((0,), (0,)), ((), ())), preferred_element_type=f32
+                )
+            )
+            g_keys = g_k if g_keys is None else g_keys + g_k
+            g_values = g_v if g_values is None else g_values + g_v
+        g_q = jnp.where(lane < HD, g_queries[0], g_queries[1]) * scale
+        q_ref[q_at, lanes(q_col)] = g_q.astype(bf16)
+        k_ref[k_at, lanes(k_col)] = (g_keys * scale).astype(bf16)
+        k_ref[k_at, lanes(v_col)] = g_values.astype(bf16)
+
+    def cross_attention(page):
+        need("cq", "kv")
+        place = lax.broadcasted_iota(jnp.int32, (slots, length), 0)
+        allowed = place < counts[page]
+
+        def body(pair, carry):
+            attention(page, pair, cq, 0, kv, page * slots, slots, 0, D, lse_cross, allowed)
+            return carry
+
+        lax.fori_loop(0, D // (2 * HD), body, 0)
+
+    def self_attention(page):
+        need("qkv")
+        key = lax.broadcasted_iota(jnp.int32, (length, length), 0)
+        query = lax.broadcasted_iota(jnp.int32, (length, length), 1)
+        allowed = (key <= query) & (key < lengths[page])
+
+        def body(pair, carry):
+            attention(page, pair, qkv, 0, qkv, page * length, length, D, 2 * D, lse_self, allowed)
+            return carry
+
+        lax.fori_loop(0, D // (2 * HD), body, 0)
+
+    def norm_back(value_ref, gain_row, grad_of, put):
+        gain = gains[pl.ds(gain_row, 1), :]
+
+        def body(k, total_):
+            at = pl.ds(k * 32, 32)
+            value = value_ref[at].astype(f32)
+            centred = value - jnp.mean(value, axis=-1, keepdims=True)
+            spread = jnp.mean(centred * centred, axis=-1, keepdims=True)
+            row_scale = lax.rsqrt(spread + EPS)
+            unit = centred * row_scale
+            grad = grad_of(at)
+            grad_unit = grad * gain
+            inner = jnp.mean(grad_unit * unit, axis=-1, keepdims=True)
+            put(at, row_scale * (grad_unit - jnp.mean(grad_unit, axis=-1, keepdims=True) - unit * inner))
+            return total_ + jnp.sum(grad * unit, axis=0, keepdims=True)
+
+        summed = lax.fori_loop(0, value_ref.shape[0] // 32, body, jnp.zeros((1, D), f32))
+        gain_sum[0, pl.ds(gain_row, 1), :] = summed
+
+    def second_norm():
+        need("self")
+
+        def grad_of(at):
+            return times_transposed(cq[at], w_a[:, pl.ds(0, D)])
+
+        def put(at, value):
+            value = cross[at] + value
+            cross[at] = value
+            branch[at] = value.astype(bf16)
+
+        norm_back(after_self, 1, grad_of, put)
+        fetch("wkv2", wself_in.at[:, pl.ds(D, 2 * D)], w_a, 15)
+
+    def first_norm():
+        need("x", "wkv2")
+
+        def grad_of(at):
+            value = times_transposed(qkv[at, pl.ds(0, D)], w_b[:, pl.ds(D, D)])
+            return value + times_transposed(qkv[at, pl.ds(D, 2 * D)], w_a_cat(at))
+
+        def w_a_cat(at):
+            return w_a[...]
+
+        def grad_of(at):
+            value = times_transposed(qkv[at, pl.ds(0, D)], w_b[:, pl.ds(D, D)])
+            value = value + times_transposed(qkv[at, pl.ds(D, D)], w_a[:, pl.ds(0, D)])
+            return value + times_transposed(qkv[at, pl.ds(2 * D, D)], w_a[:, pl.ds(D, D)])
+
+        def put(at, value):
+            input_out[at] = cross[at] + value
+
+        norm_back(x_bf, 0, grad_of, put)
+        fetch("wkv", wkv_in, w_b, 16)
+
+    def memory_grad(page, part):
+        need("wkv")
+        slot = part % 2
+        need(("stage", slot))
+        top = part * span
+        height = min(slots - top, span)
+        live = min(memory_rows - top, height)
+        at = pl.ds(page * slots + top, height)
+
+        def body(k, carry):
+            col = pl.multiple_of(k * BLOCK, BLOCK)
+            value = times_transposed(kv[at, :], w_b[pl.ds(col, BLOCK), :])
+            for j in range(BLOCK // 128):
+                stage[slot, pl.ds(k * (BLOCK // 128) + j, live, 8), :] = value[:live, j * 128 : j * 128 + 128]
+            return carry
+
+        lax.fori_loop(0, D // BLOCK, body, 0)
+        fetch(
+            ("stage", slot),
+            stage.at[slot, pl.ds(0, live * 8)],
+            memory_out.at[pl.ds((page * memory_rows + top) * 8, live * 8)],
+            18 + slot,
+        )
+
+    span = -(-slots // 32) * 16
+    memory_rows = memory_out.shape[0] // 8 // pages
+    gain_sum[0] = gain_three[...]
     plan = Plan()
     for i in range(total):
         plan.add(i - 2, 0, stage0, i)
@@ -470,13 +713,32 @@
         plan.add(i + 1, 2, stage2, i)
         plan.add(i + 2, 3, stage3, i)
         plan.add(i + 3, 4, stage4, i)
+
+    def cross_in_grad():
+        need("wqo")
+        context_grad(w_a, D)
+
+    def self_in_grad():
+        need("wo", "wq")
+        context_grad(w_b, 0)
+
+    plan.add(0, 9, round_branch)
+    plan.add(0, 9, cross_in_grad)
+    for page in range(pages):
+        plan.add(1 + page, 9, cross_attention, page)
+        plan.add(8 + page, 11, self_attention, page)
+    plan.add(8, 9, second_norm)
+    plan.add(8, 9, self_in_grad)
+    plan.add(9 + pages, 9, first_norm)
+    for page in range(pages):
+        for part in range(2):
+            plan.add(12 + 2 * part, 9, memory_grad, page, part)
     for h in range(len(moves)):
         plan.add(total - 4 + h, 5, gain_step, h)
-    for i in range(min(RING, total)):
-        load(i)
     plan.run()
     for i in range(total):
-        copies[i, 0][0].wait_send()
+        if i >= total - SPARE:
+            copies[i, 0][0].wait_send()
         if i >= total - RING:
             for stage in (1, 2, 3):
                 for copy in copies[i, stage]:
@@ -484,52 +746,61 @@
     for h in range(len(moves)):
         for copy in copies["gain", h]:
             copy.wait_send()
-
-
-def reduce_all(parts, gains):
+    need(*list(loads))
+
+
+def backward(big, small, shapes):
     dp, fsdp = lax.axis_size("dp"), lax.axis_size("fsdp")
     n = dp // CORES
     depth = fsdp // n
     devices = dp * fsdp
     rows = WIDTH // devices
-    chunks = []
-    for m, part in enumerate(parts):
-        for row in range(0, part.shape[0] // devices, rows):
-            for col in range(0, part.shape[1], WIDTH):
-                chunks.append((m, row, col))
-    t = len(chunks)
+    pages, length, slots, live = shapes
+    tokens = pages * length
+    D = WIDTH
+    t = sum(k * m for k, m in ((big[0].shape[1], D), (D, big[1].shape[1]), (D, 8 * D))) // (D * D)
     dma = pltpu.SemaphoreType.DMA
     hops = 2 * n + depth - 2
+    outs = [(big[0].shape[1], D), (D, big[1].shape[1]), (D, D), (D, D), (D, 2 * D), (D, D), (D, 3 * D)]
+    f32 = jnp.float32
 
     def scratch(*lead):
         return pltpu.VMEM(lead + (rows, WIDTH), jnp.bfloat16)
 
-    views = [p.reshape(n, CORES, depth, n, p.shape[0] // devices, p.shape[1]) for p in parts]
+    def like(value):
+        return pltpu.VMEM(value.shape, value.dtype)
+
+    hbm = pl.BlockSpec(memory_space=pltpu.HBM)
+    vmem = pl.BlockSpec(memory_space=pltpu.VMEM)
+    smem = pl.BlockSpec(memory_space=pltpu.SMEM)
     return pl.pallas_call(
-        functools.partial(reduce_kernel, chunks, len(parts)),
-        out_shape=[
-            jax.ShapeDtypeStruct((p.shape[0] // devices, p.shape[1]), jnp.float32) for p in parts
-        ]
-        + [jax.ShapeDtypeStruct(gains.shape, jnp.float32)],
-        in_specs=[pl.BlockSpec(memory_space=pltpu.HBM)] * len(parts)
-        + [pl.BlockSpec(memory_space=pltpu.VMEM)],
-        out_specs=[pl.BlockSpec(memory_space=pltpu.VMEM)] * (len(parts) + 1),
-        scratch_shapes=[
+        functools.partial(back_kernel, (pages, length, slots)),
+        out_shape=[jax.ShapeDtypeStruct((k // devices, m), f32) for k, m in outs]
+        + [
+            jax.ShapeDtypeStruct((8, D), f32),
+            jax.ShapeDtypeStruct((tokens, D), f32),
+            jax.ShapeDtypeStruct((pages * live * D // 128, 128), f32),
+        ],
+        in_specs=[hbm] * len(big) + [smem, smem] + [vmem] * 4,
+        out_specs=[vmem] * (len(outs) + 2) + [hbm],
+        scratch_shapes=[like(v) for v in big[:15]]
+        + [pltpu.VMEM((D, 2 * D), jnp.bfloat16)] * 2
+        + [pltpu.VMEM((tokens, D), jnp.bfloat16)] * 2
+        + [
+            pltpu.VMEM((2, -(-slots // 32) * 16 * 8, 128), f32),
+            scratch(SPARE, n, depth, n),
             scratch(RING, n, depth, n),
-            scratch(t, n, depth, n),
-            scratch(RING, n - 1, n, depth),
+            scratch(RING, n, n, depth),
             scratch(t, n - 1, n, depth),
             scratch(RING, n, depth),
-            scratch(RING, n - 1, depth),
             scratch(t, n - 1, depth),
             scratch(RING, depth),
-            scratch(RING, depth),
             scratch(t, depth - 1),
-            pltpu.VMEM((4,) + gains.shape, jnp.float32),
-            pltpu.VMEM((hops,) + gains.shape, jnp.float32),
+            pltpu.VMEM((4, 8, D), f32),
+            pltpu.VMEM((hops, 8, D), f32),
+            dma((20,)),
+            dma((SPARE,)),
             dma((RING,)),
-            dma((t,)),
-            dma((t,)),
             dma((RING, n - 1)),
             dma((t, n - 1)),
             dma((RING, n - 1)),
@@ -538,16 +809,12 @@
             dma((t, depth - 1)),
             dma((hops,)),
             dma((hops,)),
+            pltpu.SemaphoreType.REGULAR,
         ],
         compiler_params=pltpu.CompilerParams(
-            collective_id=1, has_side_effects=True, vmem_limit_bytes=60 << 20
+            collective_id=1, has_side_effects=True, vmem_limit_bytes=67043328
         ),
-    )(*views, gains)
-
-
-def outer(left, grad):
-    total = lax.dot_general(left, grad, (((0,), (0,)), ((), ())), preferred_element_type=jnp.float32)
-    return total.astype(jnp.bfloat16)
+    )(*big, *small)
 
 
 def split_heads(value):
@@ -598,40 +865,6 @@
         "bhqk,bkhd->bqhd", probs, split_heads(values), preferred_element_type=jnp.float32
     )
     return (context.reshape(queries.shape).astype(jnp.bfloat16), top + jnp.log(total))
-
-
-def attend_back(queries, keys, values, allowed, logsum, grad_context):
-    probs = jnp.exp(masked_scores(queries, keys, allowed) - logsum)
-    grad_heads = split_heads(grad_context)
-    grad_values = jnp.einsum(
-        "bhqk,bqhd->bkhd",
-        probs.astype(jnp.bfloat16),
-        grad_heads,
-        preferred_element_type=jnp.float32,
-    )
-    grad_probs = jnp.einsum(
-        "bqhd,bkhd->bhqk", grad_heads, split_heads(values), preferred_element_type=jnp.float32
-    )
-    inner = jnp.sum(probs * grad_probs, axis=-1, keepdims=True)
-    grad_scores = (probs * (grad_probs - inner)).astype(jnp.bfloat16)
-    scale = HD ** (-0.5)
-    grad_queries = (
-        jnp.einsum(
-            "bhqk,bkhd->bqhd", grad_scores, split_heads(keys), preferred_element_type=jnp.float32
-        )
-        * scale
-    )
-    grad_keys = (
-        jnp.einsum(
-            "bhqk,bqhd->bkhd", grad_scores, split_heads(queries), preferred_element_type=jnp.float32
-        )
-        * scale
-    )
-    return (
-        grad_queries.reshape(queries.shape).astype(jnp.bfloat16),
-        grad_keys.reshape(keys.shape).astype(jnp.bfloat16),
-        grad_values.reshape(values.shape).astype(jnp.bfloat16),
-    )
 
 
 def per_device(
@@ -708,45 +941,44 @@
 
     grad_out = cotangent[:, 0].astype(jnp.float32)
     grad_branch = grad_out.astype(jnp.bfloat16)
-    grad_reduce = outer(flat(hidden), flat(grad_branch))
     grad_hidden = project_back(grad_branch, reduce_weight)
     _, gelu_pull = jax.vjp(lambda v: jax.nn.gelu(v, approximate=False), hidden_pre)
     grad_pre = gelu_pull(grad_hidden)[0].astype(jnp.bfloat16)
-    grad_expand = outer(flat(third), flat(grad_pre))
     grad_norm, grad_gain_three = normalize_back(
         project_back(grad_pre, expand_weight), unit_three, scale_three, gain_three
     )
     grad_cross = grad_out + grad_norm
 
-    grad_branch = grad_cross.astype(jnp.bfloat16)
-    grad_source_output = outer(flat(cross_context), flat(grad_branch))
-    grad_context = project_back(grad_branch, source_out_weight).astype(jnp.bfloat16)
-    grad_cq, grad_mk, grad_mv = attend_back(
-        cross_queries, memory_keys, memory_values, source_mask, logsum_cross, grad_context
-    )
-    grad_both = jnp.concatenate([grad_mk, grad_mv], axis=-1)
-    grad_source_query = outer(flat(second), flat(grad_cq))
-    grad_source_both = outer(flat(source), flat(grad_both))
-    grad_memory = project_back(grad_both, kv_weight)
-    grad_norm, grad_gain_two = normalize_back(
-        project_back(grad_cq, source_query_weight), unit_two, scale_two, gain_two
-    )
-    grad_self = grad_cross + grad_norm
-
-    grad_branch = grad_self.astype(jnp.bfloat16)
-    grad_causal_output = outer(flat(context), flat(grad_branch))
-    grad_context = project_back(grad_branch, out_weight).astype(jnp.bfloat16)
-    grad_q, grad_k, grad_v = attend_back(
-        queries, keys, values, causal_mask, logsum_self, grad_context
-    )
-    grad_qkv = jnp.concatenate([grad_q, grad_k, grad_v], axis=-1)
-    grad_causal = outer(flat(first), flat(grad_qkv))
-    grad_norm, grad_gain_one = normalize_back(
-        project_back(grad_qkv, qkv_weight), unit_one, scale_one, gain_one
-    )
-    grad_inputs = grad_self + grad_norm
-    gain_sums = jnp.stack([grad_gain_one, grad_gain_two, grad_gain_three])
-    gain_sums = jnp.pad(gain_sums, ((0, 5), (0, 0)))
+    pad = -slots % 16
+    both = jnp.pad(memory_both, ((0, 0), (0, pad), (0, 0)))
+    big = [
+        flat(hidden),
+        flat(grad_pre),
+        flat(third),
+        flat(grad_branch),
+        flat(grad_cross),
+        flat(cross_context),
+        flat(second),
+        flat(cross_queries),
+        flat(both),
+        flat(jnp.pad(source, ((0, 0), (0, pad), (0, 0)))),
+        flat(after_self),
+        flat(context),
+        flat(first),
+        flat(qkv),
+        flat(hidden_in[:, 0]),
+        qo_weight,
+        kv_weight,
+        self_weight,
+    ]
+    small = [
+        page_count,
+        page_length,
+        jnp.pad(gain_rows, ((0, 5), (0, 0))),
+        jnp.pad(grad_gain_three[None], ((2, 5), (0, 0))),
+        logsum_cross.reshape(-1, rows),
+        logsum_self.reshape(-1, rows),
+    ]
     (
         grad_reduce,
         grad_expand,
@@ -756,25 +988,16 @@
         grad_causal_output,
         grad_causal,
         grad_gains,
-    ) = reduce_all(
-        [
-            grad_reduce,
-            grad_expand,
-            grad_source_output,
-            grad_source_query,
-            grad_source_both,
-            grad_causal_output,
-            grad_causal,
-        ],
-        gain_sums,
-    )
+        grad_inputs,
+        grad_memory,
+    ) = backward(big, small, (pages, rows, slots + pad, slots))
     entries = causal_gain.shape[0]
     me = lax.axis_index("dp") * lax.axis_size("fsdp") + lax.axis_index("fsdp")
     grad_gains = lax.dynamic_slice_in_dim(grad_gains, me * entries, entries, axis=1)
     return (
         result.astype(jnp.bfloat16)[:, None],
-        grad_inputs[:, None],
-        grad_memory[:, None],
+        grad_inputs.reshape(pages, 1, rows, width),
+        grad_memory.reshape(memory.shape),
         grad_gains[0],
         grad_causal[:, :width],
         grad_causal[:, width : 2 * width],

time: 572 us -> 475 us (0.83)
  matrix products: 140 us -> 57 us
  local copies, waits for them, and re-layouts: 97 us -> 55.6 us
  Pallas kernels: 299 us -> 330 us
    dot_general x15 -> x0, matrix products: 61.4 us -> none  [the longest x7 33.6 us: outer(): lax.dot_general(left, grad, (((0,), (0,)), ((), ())), preferred_element_t...]
    convert_element_type x11 -> x4, local copies, waits for them, and re-layouts: 40.2 us -> 4.64 us  [attend(): context.reshape(queries.shape).astype(jnp.bfloat16)]
    pallas_call x1, Pallas kernels: 155 us -> 187 us  [backward(): pl.pallas_call(functools.partial(back_kernel, (pages, length, slots)), ou...]
    dot_general x7 -> x2, matrix products: 32 us -> 10.5 us  [project_back(): jnp.einsum('ble,de->bld', grad, weight, preferred_element_type=jnp.float32)]
    unnamed x123 -> x68, local copies, waits for them, and re-layouts: 30.3 us -> 20.3 us
    pad x0 -> x4, local copies, waits for them, and re-layouts: none -> 8.46 us  [the longest x1 5.54 us: per_device(): both = jnp.pad(memory_both, ((0, 0), (0, pad), (0, 0)))]
where the time goes in v3:
time: 475 us; the launch traced here: 467 us
  Pallas kernels  330 us (69%)
  matrix products  57 us (12%)
  local copies, waits for them, and re-layouts  55.6 us (12%)
  other arithmetic  22.8 us (5%)
    pallas_call x1, Pallas kernels, backward(): pl.pallas_call(functools.partial(back_kernel, (pages, length, slots)), ou...  187 us
    pallas_call x1, Pallas kernels, gather_all(): pl.pallas_call(functools.partial(gather_kernel, chunks, len(shards)), out...  143 us
    dot_general x7, matrix products, project(): jnp.einsum('bld,de->ble', left, weight, preferred_element_type=jnp.float32)  32.1 us
    unnamed x68, local copies, waits for them, and re-layouts  20.3 us
    dot_general x2, matrix products, project_back(): jnp.einsum('ble,de->bld', grad, weight, preferred_element_type=jnp.float32)  10.5 us
    convert_element_type x1, other arithmetic, per_device(): hidden = jax.nn.gelu(hidden_pre, approximate=False).astype(jnp.bfloat16)  10.4 us
    dot_general x2, matrix products, attend(): jnp.einsum('bhqk,bkhd->bqhd', probs, split_heads(values), preferred_eleme...  9.98 us

profile of v3, /device:TPU:0, one launch (start us, length us, event | category | flops | bytes accessed | tf_op | source)
XLA Modules:
  0.0 466.8 jit_solution(11305889455141722126)
XLA Ops:
  0.7 1.7 pad_maximum_fusion
  7.3 143.2 %shard_map.297 = (bf16[2,2,4,2,32,2048]{5,4,3,2,1,0:T(8,128)(2,1)}, bf16[2,2,4,2,32,4224]{5,4,3,2,1,0:T(8,128)(2,1)}, bf16[2,2,4,2,32,2048]{5,4,3,2,1,0:T(8,128)...) custom-call(bf16[32,2048]{1,0:T(8,128)(2,1)} %get-tuple-element.131.refs_0_, ...), custom_call_target="tpu_custom_call" | custom-call | tf_op jit(solution)/shard_map/pallas_call | solution.py:289
  151.7 1.2 convert_reduce_fusion
  153.2 4.7 %fusion.10 = bf16[2,128,3072]{2,1,0:T(8,128)(2,1)S(1)} fusion(bf16[1024,4224]{1,0:T(8,128)(2,1)} %bitcast.150, bf16[2,1,128,1024]{3,2,1,0:T(8,128)(2,1)S(1)} %copy-done.4, f32[1024]{0:T(1024)S(1)} %bitcast.189, f32[2,128]{1,0:T(2,128)S(1)} %get-tuple-element.120, f32[2,128]{1,0:T(2,128)S(1)} %get-tuple-element.118), kind=kOutput, calls=%fused_computation.31 | convolution fusion | flops 1612709888 | bytes 8394752 | tf_op jit(solution)/shard_map/bld,de->ble/dot_general | solution.py:825
  157.9 1.3 fusion.46
  159.4 1.3 copy.86
  161.5 1.3 copy-done.7
  163.3 1.3 copy.84
  164.7 2.3 convolution_convert_fusion
  167.0 2.6 fusion.50
  171.2 8.0 %convert_bitcast_fusion = bf16[2,588,2048]{2,1,0:T(8,128)(2,1)S(1)} fusion(bf16[1024,2048,1]{1,0,2:T(8,128)(2,1)} %bitcast.162, bf16[2,588,1024]{2,0,1:T(2,128)(2,1)} %bitcast.166), kind=kOutput, calls=%fused_computation.9 | convolution fusion | flops 4934909952 | bytes 11419648 | tf_op jit(solution)/shard_map/bld,de->ble/dot_general | solution.py:825
  179.2 3.1 fusion.45
  182.9 4.3 copy.92
  187.3 3.9 fusion
  191.2 2.1 fusion.1
  193.4 1.6 copy-done
  195.6 4.7 %copy.90 = bf16[2,588,1024]{1,2,0:T(8,128)(2,1)} copy(bf16[2,588,1024]{2,1,0:T(8,128)(2,1)} %get-tuple-element.102) | data formatting | bytes 4816896 | tf_op jit(solution)/shard_map/slice | solution.py:924
  200.3 7.6 %fusion.21 = bf16[2,16,64,128]{3,2,1,0:T(8,128)(2,1)S(1)} fusion(bf16[2,588,16,64]{1,3,2,0:T(8,128)(2,1)} %bitcast.165, f32[2,16,128,588]{2,3,1,0:T(8,128)} %copy-done, f32[2,16,128]{2,1,0:T(8,128)S(1)} %fusion.1, f32[2,16,128]{2,1,0:T(8,128)S(1)} %get-tuple-element.125, pred[2,588]{1,0:T(4,128)(4,1)S(1)} %iota_compare_fusion.1), kind=kOutput, calls=%fused_computation.52 | convolution fusion | flops 320585728 | bytes 12600472 | tf_op jit(solution)/shard_map/bhqk,bkhd->bqhd/dot_general | solution.py:864
  209.4 7.8 %fusion.29 = (u8[128,4096]{1,0:T(8,128)(4,1)S(1)}, u8[128,4096]{1,0:T(8,128)(4,1)S(1)}, f32[2,128,4096]{2,1,0:T(8,128)S(1)}) fusion(bf16[2,128,1024]{2,1,0:T(8,128)(2,1)S(1)} %multiply_convert_fusion.2, bf16[1024,4096,1]{1,0,2:T(8,128)(2,1)} %bitcast.204), kind=kOutput, calls=%fused_computation.68 | convolution fusion | flops 2160066560 | bytes 14155776 | tf_op jit(solution)/shard_map/bld,de->ble/dot_general | solution.py:825
  217.2 10.4 %multiply_convert_fusion = (bf16[2,128,4096]{2,1,0:T(8,128)(2,1)}, f32[2,128,4096]{2,1,0:T(8,128)S(1)}) fusion(f32[2,128,4096]{2,1,0:T(8,128)S(1)} %get-tuple-element.129, u8[128,4096]{1,0:T(8,128)(4,1)S(1)} %get-tuple-element.95, u8[128,4096]{1,0:T(8,128)(4,1)S(1)} %get-tuple-element.94), kind=kLoop, calls=%fused_computation.18 | loop fusion | flops 73400320 | bytes 11534336 | tf_op jit(solution)/shard_map/convert_element_type | solution.py:939
  227.6 3.7 add_convert_fusion
  231.4 6.8 %multiply_reduce_fusion = (f32[1024]{0:T(1024)S(1)}, f32[2,128]{1,0:T(2,128)S(1)}, f32[2,128]{1,0:T(2,128)S(1)}, f32[2,128,1024]{2,1,0:T(8,128)S(1)}) fusion(f32[2,128,1024]{2,1,0:T(8,128)S(1)} %get-tuple-element.128, f32[2,128]{1,0:T(2,128)S(1)} %add_rsqrt_fusion, f32[2,128]{1,0:T(2,128)S(1)} %broadcast_multiply_fusion.2, f32[1024]{0:T(1024)S(1)} %bitcast.187, ...), kind=kOutput, calls=%fused_computation.59 | convolution fusion | flops 2149579264 | bytes 12595200 | tf_op jit(solution)/shard_map/ble,de->bld/dot_general | solution.py:829
  238.2 1.4 multiply_add_fusion
  241.0 1.5 reshape.290.refs_5_
  243.3 1.5 reshape.291.refs_11_
  247.2 5.5 %pad.21 = bf16[2,592,2048]{2,1,0:T(8,128)(2,1)} pad(bf16[2,588,2048]{2,1,0:T(8,128)(2,1)} %copy-done.2, bf16[]{:T(256)} %constant.14.clone.1), padding=0_0x0_4x0_0 | pad | bytes 9666562 | tf_op jit(solution)/shard_map/jit(_pad)/pad | solution.py:953
  253.4 1.7 pad.22.clone
  255.1 186.6 %shard_map.298 = (f32[128,1024]{1,0:T(8,128)}, f32[32,4096]{1,0:T(8,128)}, f32[32,1024]{1,0:T(8,128)}, f32[32,1024]{1,0:T(8,128)}, f32[32,2048]{1,0:T(8,128)}, /...) custom-call(bf16[256,4096]{1,0:T(8,128)(2,1)} %bitcast.159, ...), custom_call_target="tpu_custom_call" | custom-call | tf_op jit(solution)/shard_map/pallas_call | solution.py:776
  441.7 1.8 fusion.47
  443.4 1.7 fusion.48
  446.4 7.4 %fusion.24 = bf16[2,1,128,1024]{3,2,1,0:T(8,128)(2,1)} fusion(f32[2,128,1024]{2,1,0:T(8,128)} %copy-done.3, bf16[2,128,4096]{2,1,0:T(8,128)(2,1)} %get-tuple-element.99, bf16[4096,1024,1]{1,0,2:T(8,128)(2,1)} %bitcast.200), kind=kOutput, calls=%fused_computation.55 | convolution fusion | flops 2148007936 | bytes 12058624 | tf_op jit(solution)/shard_map/bld,de->ble/dot_general | solution.py:825
  454.8 8.0 %copy.126 = f32[2,1,588,1024]{3,1,2,0:T(1,128)} copy(f32[2,1,588,1024]{3,1,2,0:T(1,128)} %bitcast.161) | data formatting | bytes 9633792
  (104 shorter events, 23.1 us)
Async XLA Ops:
  0.6 152.2 %copy-start.4 = (bf16[2,1,128,1024]{3,2,1,0:T(8,128)(2,1)S(1)}, bf16[2,1,128,1024]{3,2,1,0:T(8,128)(2,1)}, u32[]{:S(2)}) copy-start(bf16[2,1,128,1024]{3,2,1,0:T(8,128)(2,1)} %param.18) | copy-start | bytes 1572868
  6.6 0.7 copy-start.20
  157.9 3.7 copy-start.8
  157.9 2.9 copy-start.25
  161.5 1.3 copy-start.7
  167.0 3.2 copy-start.15
  167.0 3.2 copy-start.5
  169.7 38.3 %copy-start.1 = (f32[2,128,1024]{2,1,0:T(8,128)}, f32[2,128,1024]{2,1,0:T(8,128)S(1)}, u32[]{:S(2)}) copy-start(f32[2,128,1024]{2,1,0:T(8,128)S(1)} %get-tuple-element.124) | copy-start | bytes 3145732
  170.2 9.0 %copy-start.11 = (bf16[2,128,1024]{2,1,0:T(8,128)(2,1)}, bf16[2,128,1024]{2,1,0:T(8,128)(2,1)S(1)}, u32[]{:S(2)}) copy-start(bf16[2,128,1024]{2,1,0:T(8,128)(2,1)S(1)} %multiply_convert_fusion.3) | copy-start | bytes 1572868
  170.9 8.3 %copy-start.12 = (bf16[2,128,1024]{2,1,0:T(8,128)(2,1)}, bf16[2,128,1024]{2,1,0:T(8,128)(2,1)S(1)}, u32[]{:S(2)}) copy-start(bf16[2,128,1024]{2,1,0:T(8,128)(2,1)S(1)} %fusion.20) | copy-start | bytes 1572868
  179.2 3.7 copy-start.2
  182.9 4.4 copy-start.24
  191.2 3.7 copy-start
  200.3 7.7 %copy-start.6 = (bf16[2,2,4,2,32,2048]{5,4,3,2,1,0:T(8,128)(2,1)S(1)}, bf16[2,2,4,2,32,2048]{5,4,3,2,1,0:T(8,128)(2,1)}, u32[]{:S(2)}) copy-start(bf16[2,2,4,2,32,2048]{5,4,3,2,1,0:T(8,128)(2,1)} %get-tuple-element.33) | copy-start | bytes 12582916
  208.8 29.4 %copy-start.3 = (f32[2,128,1024]{2,1,0:T(8,128)}, f32[2,128,1024]{2,1,0:T(8,128)S(1)}, u32[]{:S(2)}) copy-start(f32[2,128,1024]{2,1,0:T(8,128)S(1)} %get-tuple-element.128) | copy-start | bytes 3145732
  208.8 18.8 %slice-start = ((s8[8388608]{0:T(1024)(128)(4,1)}), s8[4194304]{0:T(1024)(128)(4,1)S(1)}, s32[]{:S(2)}) async-start(s8[8388608]{0:T(1024)(128)(4,1)} %bitcast.201), calls=%async_computation | async-start | bytes 8388608
  209.3 7.8 %copy-start.13 = (bf16[2,128,1024]{2,1,0:T(8,128)(2,1)}, bf16[2,128,1024]{2,1,0:T(8,128)(2,1)S(1)}, u32[]{:S(2)}) copy-start(bf16[2,128,1024]{2,1,0:T(8,128)(2,1)S(1)} %multiply_convert_fusion.2) | copy-start | bytes 1572868
  209.3 18.3 %slice-start.1 = ((s8[8388608]{0:T(1024)(128)(4,1)}), s8[4194304]{0:T(1024)(128)(4,1)S(1)}, s32[]{:S(2)}) async-start(s8[8388608]{0:T(1024)(128)(4,1)} %bitcast.201), calls=%async_computation.1 | async-start | bytes 8388608
  217.2 10.4 %copy-start.10 = (bf16[2,1,128,1024]{3,2,1,0:T(8,128)(2,1)S(1)}, bf16[2,1,128,1024]{3,2,1,0:T(8,128)(2,1)}, u32[]{:S(2)}) copy-start(bf16[2,1,128,1024]{3,2,1,0:T(8,128)(2,1)} %param.20) | copy-start | bytes 1572868
  231.3 6.8 %copy-start.14 = (bf16[2,128,4096]{2,1,0:T(8,128)(2,1)}, bf16[2,128,4096]{2,1,0:T(8,128)(2,1)S(1)}, u32[]{:S(2)}) copy-start(bf16[2,128,4096]{2,1,0:T(8,128)(2,1)S(1)} %add_convert_fusion) | copy-start | bytes 6291460
  238.1 4.4 copy-start.16
  247.2 5.5 %copy-start.9 = (bf16[2,1,588,1024]{3,0,2,1:T(2,128)(2,1)S(1)}, bf16[2,1,588,1024]{3,0,2,1:T(2,128)(2,1)}, u32[]{:S(2)}) copy-start(bf16[2,1,588,1024]{3,0,2,1:T(2,128)(2,1)} %param.19) | copy-start | bytes 7225348
  446.4 7.4 %copy-start.17 = (f32[256,1024]{1,0:T(8,128)S(1)}, f32[256,1024]{1,0:T(8,128)}, u32[]{:S(2)}) copy-start(f32[256,1024]{1,0:T(8,128)} %get-tuple-element.36) | copy-start | bytes 3145732
  454.8 8.0 %copy-start.23 = (f32[32,1024]{1,0:T(8,128)S(1)}, f32[32,1024]{1,0:T(8,128)}, u32[]{:S(2)}) copy-start(f32[32,1024]{1,0:T(8,128)} %get-tuple-element.156) | copy-start | bytes 393220
  454.8 8.7 %copy-start.22 = (f32[32,1024]{1,0:T(8,128)S(1)}, f32[32,1024]{1,0:T(8,128)}, u32[]{:S(2)}) copy-start(f32[32,1024]{1,0:T(8,128)} %get-tuple-element.158) | copy-start | bytes 393220
  454.8 9.3 %copy-start.21 = (f32[32,1024]{1,0:T(8,128)S(1)}, f32[32,1024]{1,0:T(8,128)}, u32[]{:S(2)}) copy-start(f32[32,1024]{1,0:T(8,128)} %get-tuple-element.161) | copy-start | bytes 393220
  454.8 10.0 %copy-start.19 = (f32[32,4096]{1,0:T(8,128)S(1)}, f32[32,4096]{1,0:T(8,128)}, u32[]{:S(2)}) copy-start(f32[32,4096]{1,0:T(8,128)} %get-tuple-element.163) | copy-start | bytes 1572868
  454.8 10.8 %copy-start.18 = (f32[128,1024]{1,0:T(8,128)S(1)}, f32[128,1024]{1,0:T(8,128)}, u32[]{:S(2)}) copy-start(f32[128,1024]{1,0:T(8,128)} %get-tuple-element.164) | copy-start | bytes 1572868

commit v4 on v3

--- a/solution.py
+++ b/solution.py
@@ -12,6 +12,7 @@
 AXES = ("dp", "fsdp")
 CORES = 2
 WIDTH = 1024
+BLOCK = 256
 MESH = pl.DeviceIdType.MESH
 
 
@@ -91,12 +92,87 @@
                 call(*args)
 
 
-def gather_kernel(chunks, count, *refs):
+def times(left, right):
+    return jnp.dot(left, right, preferred_element_type=jnp.float32)
+
+
+def times_transposed(left, right):
+    return lax.dot_general(left, right, (((1,), (1,)), ((), ())), preferred_element_type=jnp.float32)
+
+
+def transposed_times(left, right):
+    return lax.dot_general(left, right, (((0,), (0,)), ((), ())), preferred_element_type=jnp.float32)
+
+
+def standardize(value):
+    centred = value - jnp.mean(value, axis=-1, keepdims=True)
+    spread = jnp.mean(centred * centred, axis=-1, keepdims=True)
+    row_scale = lax.rsqrt(spread + EPS)
+    return centred * row_scale, row_scale
+
+
+def standardize_back(grad, unit, row_scale, gain):
+    grad_unit = grad * gain
+    inner = jnp.mean(grad_unit * unit, axis=-1, keepdims=True)
+    return row_scale * (grad_unit - jnp.mean(grad_unit, axis=-1, keepdims=True) - unit * inner)
+
+
+def lane_window(col, pair):
+    return pl.ds(pl.multiple_of(col + pair * 2 * HD, 2 * HD), 2 * HD)
+
+
+STRIP = 32
+
+
+def strips(count, body, carry=None):
+    def one(k, carry):
+        return body(pl.ds(pl.multiple_of(k * STRIP, STRIP), STRIP), carry)
+
+    return lax.fori_loop(0, count // STRIP, one, carry)
+
+
+FLAT_AHEAD = 2
+TALL_GAP = 2
+ARRIVED = 5
+
+
+def front_kernel(dims, chunks, counts_, *refs):
+    pages, length, slots = dims
+    n_src, n_out = counts_
+    it = iter(refs)
+
+    def take(k):
+        return [next(it) for _ in range(k)]
+
+    shards = take(n_src)
+    x_in, cot_in, memory_in, counts, lengths = take(5)
+    outs = take(n_out)
+    saved_out = take(13)
+    gains, gain_three, lse_cross, lse_self = take(4)
+    saved = take(13)
+    (result, hidden, pre, third, cross_grad, cctx, second, cq, kv, after_self, ctx, first, qkv) = saved
+    x_bf, cot, memory, w_a, w_b, w_d, w_gain, after_cross, slope, g_hidden = take(10)
+    local, zs, zr, ps, pr, qs, qr, cs, cr, us, ur, ds, dr, loads_sem, stores_sem = take(15)
+    f32, bf16 = jnp.float32, jnp.bfloat16
     grid = Grid()
     n, depth = grid.n, grid.depth
-    shards, outs = refs[:count], refs[count : 2 * count]
-    local, zs, zr, ps, pr, qs, qr, cs, cr, us, ur, ds, dr = refs[2 * count :]
     y, c, z, x = grid.at
+    tokens, D = x_bf.shape
+    loads = {}
+
+    def fetch(name, src, dst, slot):
+        loads[name] = pltpu.make_async_copy(src, dst, loads_sem.at[slot])
+        loads[name].start()
+
+    def need(*names):
+        for name in names:
+            copy = loads.pop(name, None)
+            if copy is not None:
+                copy.wait()
+
+    fetch("x", x_in, x_bf, 0)
+    fetch("cot", cot_in, cot, 1)
+    fetch("memory", memory_in, memory, 2)
     grid.meet()
     pending = []
 
@@ -106,21 +182,25 @@
         return made
 
     def window(i):
-        _, r0, nr, c0, nc, _ = chunks[i]
-        return pl.ds(r0, nr), pl.ds(c0, nc)
+        _, r0, nr, c0, nc, _, o0, _ = chunks[i]
+        return pl.ds(r0, nr), pl.ds(o0, nc)
+
+    def out(i):
+        return outs[chunks[i][5]]
 
     def shard(i):
-        return shards[chunks[i][0]].at[window(i)]
+        m, r0, nr, c0, nc, _, _, _ = chunks[i]
+        return shards[m].at[pl.ds(r0, nr), pl.ds(c0, nc)]
 
     def block(i, yy, zz, xx):
-        return outs[chunks[i][0]].at[(yy, c, zz, xx) + window(i)]
+        return out(i).at[(yy, c, zz, xx) + window(i)]
 
     def back(a, b):
         return grid.place((n - a) % n, (n - b) % n)
 
     def column(i, a, b):
         yy, xx = back(a, b)
-        return outs[chunks[i][0]].at[(yy, c, slice(None), xx) + window(i)]
+        return out(i).at[(yy, c, slice(None), xx) + window(i)]
 
     def share(i, a, b):
         piece = column(i, a, b)
@@ -197,7 +277,7 @@
 
     def layer(i, k, j):
         zz = lax.rem(z + (depth - j if k == 0 else j), depth)
-        return outs[chunks[i][0]].at[(slice(None), c, zz, slice(None)) + window(i)]
+        return out(i).at[(slice(None), c, zz, slice(None)) + window(i)]
 
     def hop(i, k, j):
         piece = layer(i, k, j)
@@ -232,76 +312,391 @@
                 def _():
                     hop(i, k, j).start()
 
-    def finish_tall(i):
-        share_layer(i, 0, 0).wait()
+    def each_layer(i, call, hops):
+        call(share_layer(i, 0, 0))
         for k in (0, 1):
             for j in range(depth - 1):
-
-                @pl.when((level(k) >= j) & (level(k) < depth - 1))
-                def _():
-                    hop(i, k, j).wait_send()
+                if hops:
+
+                    @pl.when((level(k) >= j) & (level(k) < depth - 1))
+                    def _():
+                        call(hop(i, k, j))
 
                 @pl.when(level(k) >= j + 1)
                 def _():
-                    share_layer(i, k, j + 1).wait()
+                    call(share_layer(i, k, j + 1))
+
+    there = set()
+
+    def arrive(*ids):
+        for i in ids:
+            if i in there:
+                continue
+            there.add(i)
+            if chunks[i][7]:
+                each_layer(i, lambda copy: copy.wait_recv(), False)
+            else:
+                for copy in cc[i]:
+                    copy.wait_recv()
+
+    def pull(i, dst, dst_row, slot):
+        _, _, nr, _, nc, o, o0, _ = chunks[i]
+        arrive(i)
+        loads[i] = pltpu.make_async_copy(
+            out(i).at[:, :, :, :, :, pl.ds(o0, nc)], dst, loads_sem.at[slot]
+        )
+        loads[i].start()
+
+    def store(name, slot):
+        src = saved[name]
+        made = pltpu.make_async_copy(src, saved_out[name], stores_sem.at[slot])
+        made.start()
+        stores.append(made)
+
+    stores = []
+    lane = lax.broadcasted_iota(jnp.int32, (length, 2 * HD), 1)
+
+    def attention(page, pair, q_ref, k_ref, k_row, k_rows, k_col, v_col, allowed, to, lse):
+        q_at, k_at = pl.ds(page * length, length), pl.ds(k_row, k_rows)
+        queries = q_ref[q_at, lane_window(0, pair)]
+        keys = k_ref[k_at, lane_window(k_col, pair)]
+        values = k_ref[k_at, lane_window(v_col, pair)]
+        found = []
+        for h in range(2):
+            q = jnp.where((lane // HD) == h, queries, jnp.zeros_like(queries))
+            scores = times_transposed(keys, q) * HD ** (-0.5)
+            scores = jnp.where(allowed, scores, -1000000000.0)
+            top = jnp.max(scores, axis=0, keepdims=True)
+            expos = jnp.exp(scores - top)
+            sum_ = jnp.sum(expos, axis=0, keepdims=True)
+            probs = (expos * (1.0 / sum_)).astype(bf16)
+            lse[pl.ds(page * (D // HD) + pair * 2 + h, 1), :] = top + jnp.log(sum_)
+            found.append(transposed_times(probs, values))
+        to[q_at, lane_window(0, pair)] = jnp.where(lane < HD, found[0], found[1]).astype(bf16)
+
+    def read_gains():
+        arrive(GAIN)
+        piece = outs[GAIN_OUT]
+        copy = pltpu.make_async_copy(piece, w_gain, loads_sem.at[3])
+        copy.start()
+        copy.wait()
+        columns = w_gain.reshape(D, 128)[...].astype(f32)
+        gains[...] = columns.T[:8]
+
+    def project(left, weight, col, count, to, to_col):
+        def body(k, carry):
+            at = pl.multiple_of(k * BLOCK, BLOCK)
+            to[:, pl.ds(to_col + at, BLOCK)] = times(
+                left[...], weight[:, pl.ds(col + at, BLOCK)]
+            ).astype(to.dtype)
+            return carry
+
+        lax.fori_loop(0, count // BLOCK, body, 0)
+
+    def first_norm():
+        need("x")
+        gain = gains[pl.ds(0, 1), :]
+
+        def body(at, carry):
+            unit, _ = standardize(x_bf[at].astype(f32))
+            first[at] = (unit * gain).astype(bf16)
+            return carry
+
+        strips(tokens, body, 0)
+
+    def self_project(k):
+        need(SELF[k])
+        project(first, flat_b, k * D, D, qkv, k * D)
+
+    def self_attention(page):
+        key = lax.broadcasted_iota(jnp.int32, (length, length), 0)
+        query = lax.broadcasted_iota(jnp.int32, (length, length), 1)
+        allowed = (key <= query) & (key < lengths[page])
+
+        def body(pair, carry):
+            attention(page, pair, qkv, qkv, page * length, length, D, 2 * D, allowed, ctx, lse_self)
+            return carry
+
+        lax.fori_loop(0, D // (2 * HD), body, 0)
+
+    def residual(left, weight, col, base, to):
+        def body(k, carry):
+            at = pl.ds(pl.multiple_of(k * BLOCK, BLOCK), BLOCK)
+            w_at = pl.ds(pl.multiple_of(col + k * BLOCK, BLOCK), BLOCK)
+            to[:, at] = base[:, at].astype(f32) + times(left[...], weight[:, w_at])
+            return carry
+
+        lax.fori_loop(0, D // BLOCK, body, 0)
+
+    def self_out():
+        need(SELF[3])
+        residual(ctx, flat_b, 3 * D, x_bf, after_self)
+        gain = gains[pl.ds(1, 1), :]
+
+        def body(at, carry):
+            unit, _ = standardize(after_self[at])
+            second[at] = (unit * gain).astype(bf16)
+            return carry
+
+        strips(tokens, body, 0)
+
+    def memory_project(page, part):
+        need("memory", KV[0], KV[1])
+        span = -(-slots // 32) * 16
+        at = pl.ds(page * slots + part * span, min(span, slots - part * span))
+
+        def body(k, carry):
+            col = pl.ds(pl.multiple_of(k * 2 * BLOCK, BLOCK), 2 * BLOCK)
+            kv[at, col] = times(memory[at, :], flat_a[:, col]).astype(bf16)
+            return carry
+
+        lax.fori_loop(0, D // BLOCK, body, 0)
+
+    def cross_query():
+        need(QO[0])
+        project(second, flat_a, 0, D, cq, 0)
+
+    def cross_attention(page):
+        allowed = lax.broadcasted_iota(jnp.int32, (slots, length), 0) < counts[page]
+
+        def body(pair, carry):
+            attention(page, pair, cq, kv, page * slots, slots, 0, D, allowed, cctx, lse_cross)
+            return carry
+
+        lax.fori_loop(0, D // (2 * HD), body, 0)
+
+    def cross_out():
+        need(QO[1])
+        residual(cctx, flat_a, D, after_self, after_cross)
+        gain = gains[pl.ds(2, 1), :]
+
+        def body(at, carry):
+            unit, _ = standardize(after_cross[at])
+            third[at] = (unit * gain).astype(bf16)
+            return carry
+
+        strips(tokens, body, 0)
+
+    def expand(k):
+        need(EXPAND[k])
+
+        def body(j, carry):
+            at = pl.ds(pl.multiple_of(k * D + j * BLOCK, BLOCK), BLOCK)
+            value = times(third[...], flat_b[:, at])
+            below = 0.5 + 0.5 * lax.erf(value * 0.5**0.5)
+            hidden[:, at] = (value * below).astype(bf16)
+            density = jnp.exp(-0.5 * value * value) * 0.3989422804014327
+            slope[:, at] = below + value * density
+            return carry
+
+        lax.fori_loop(0, D // BLOCK, body, 0)
+
+    def hidden_grad(k):
+        need("cot", REDUCE[k])
+        col = pl.ds(k * BLOCK, BLOCK)
+
+        def body(j, carry):
+            at = pl.ds(pl.multiple_of(j * 2 * BLOCK, BLOCK), 2 * BLOCK)
+            value = times_transposed(cot[:, col], flat_d[at, col])
+            g_hidden[:, at] = value if k == 0 else g_hidden[:, at] + value
+            return carry
+
+        lax.fori_loop(0, hidden.shape[1] // (2 * BLOCK), body, 0)
+
+    def reduce_out(k):
+        col = pl.ds(k * BLOCK, BLOCK)
+        result[:, col] = (after_cross[:, col] + times(hidden[...], flat_d[:, col])).astype(bf16)
+
+    def last_part():
+        def body(j, carry):
+            at = pl.ds(pl.multiple_of(j * BLOCK, BLOCK), BLOCK)
+            pre[:, at] = (g_hidden[:, at] * slope[:, at]).astype(bf16)
+            return carry
+
+        lax.fori_loop(0, hidden.shape[1] // BLOCK, body, 0)
+        store(2, 2)
+
+        def dot_body(j, carry):
+            at = pl.ds(pl.multiple_of(j * BLOCK, BLOCK), BLOCK)
+            g_hidden[:, at] = times_transposed(pre[...], flat_b[at, :])
+            return carry
+
+        lax.fori_loop(0, D // BLOCK, dot_body, 0)
+        gain = gains[pl.ds(2, 1), :]
+
+        def body(at, total_):
+            unit, row_scale = standardize(after_cross[at])
+            grad = g_hidden[at, pl.ds(0, D)]
+            cross_grad[at] = cot[at].astype(f32) + standardize_back(grad, unit, row_scale, gain)
+            return total_ + jnp.sum(grad * unit, axis=0, keepdims=True)
+
+        summed = strips(tokens, body, jnp.zeros((1, D), f32))
+        gain_three[...] = jnp.zeros_like(gain_three)
+        gain_three[pl.ds(2, 1), :] = summed
+
+    flat_a, flat_b, flat_d = w_a.reshape(D, 2 * D), w_b.reshape(D, 4 * D), w_d.reshape(4 * D, D)
+
+    ids = {}
+    for i, chunk in enumerate(chunks):
+        ids.setdefault(chunk[5], []).append(i)
+    SELF, KV, QO, EXPAND, REDUCE = (sorted(ids[o], key=lambda i: chunks[i][6]) for o in range(5))
+    GAIN, GAIN_OUT = ids[5][0], 5
 
     plan = Plan()
-    flat = [i for i, chunk in enumerate(chunks) if not chunk[5]]
-    tall = [i for i, chunk in enumerate(chunks) if chunk[5]]
+    flat = [i for i, chunk in enumerate(chunks) if not chunk[7]]
+    tall = [i for i, chunk in enumerate(chunks) if chunk[7]]
+    tick = {}
     for t, i in enumerate(flat):
-        plan.add(t - 2, 0, stage_z, i)
+        plan.add(t - FLAT_AHEAD, 0, stage_z, i)
         plan.add(t, 2, stage_p, i)
         plan.add(t + 1, 4, stage_q, i)
         plan.add(t + 2, 6, stage_c, i)
+        tick[i] = t + 3
     for t, i in enumerate(tall):
-        t = 3 * t - 1
+        t = TALL_GAP * t - 1
         plan.add(t, 1, tall_p, i)
         plan.add(t + 2, 3, tall_q, i)
         for h in range(depth):
             plan.add(t + 4 + 2 * h, 5, climb, i, h)
+        tick[i] = t + 4 + 2 * (depth - 1) + 1
+
+    def part(buffer, k, width):
+        return buffer.at[:, :, :, :, :, pl.ds(k * width, width)]
+
+    now = max(tick[GAIN], tick[SELF[0]])
+    plan.add(tick[GAIN], 8, read_gains)
+    plan.add(tick[GAIN], 9, first_norm)
+    for k in range(4):
+        plan.add(tick[SELF[k]], 8, pull, SELF[k], part(w_b, k, D), 0, 4 + k)
+        now = max(now, tick[SELF[k]])
+        if k < 3:
+            plan.add(tick[SELF[k]] + 1, 9, self_project, k)
+    t = tick[SELF[2]] + 1
+    for page in range(pages):
+        plan.add(t + page, 10, self_attention, page)
+    t = max(t + pages, tick[SELF[3]] + 1)
+    plan.add(t, 11, self_out)
+    done_self = t
+    for k in range(2):
+        plan.add(tick[KV[k]], 8, pull, KV[k], part(w_a, k, D), 0, 8 + k)
+    t = max(tick[KV[1]] + 1, done_self)
+    for page in range(pages):
+        for half in range(2):
+            plan.add(t, 12, memory_project, page, half)
+    t = max(t + 1, tick[QO[1]])
+    for k in range(2):
+        plan.add(t, 8, pull, QO[k], part(w_a, k, D), 0, 10 + k)
+    plan.add(t, 13, cross_query)
+    for page in range(pages):
+        plan.add(t + page, 14, cross_attention, page)
+    t = t + pages - 1
+    plan.add(t, 15, cross_out)
+    done_cross = t
+    for k in range(4):
+        t = max(tick[EXPAND[k]], done_self + 1)
+        plan.add(t, 8, pull, EXPAND[k], part(w_b, k, D), 0, 12 + k)
+        plan.add(max(t, done_cross), 16, expand, k)
+    last = 0
+    for k in range(4):
+        t = tick[REDUCE[k]]
+        plan.add(t, 8, pull, REDUCE[k], part(w_d, k, BLOCK), 0, 16 + k)
+        plan.add(t + 1, 17, hidden_grad, k)
+        last = max(last, t + 1)
+    last = max([last, done_cross] + [tick[i] for i in EXPAND])
+
+    def finish():
+        for name, slot in ((1, 1), (3, 3), (5, 5), (6, 6), (7, 7), (8, 8), (9, 9), (10, 10), (11, 11), (12, 12)):
+            store(name, slot)
+        for k in range(4):
+            reduce_out(k)
+        store(0, 0)
+        last_part()
+        store(4, 4)
+
+    plan.add(last + 1, 20, finish)
     plan.run()
     for i in flat:
-        for copy in cc[i]:
-            copy.wait_recv()
+        arrive(i)
     for i in tall:
-        finish_tall(i)
+        arrive(i)
+        each_layer(i, lambda copy: copy.wait_send(), True)
     for copy in pending:
         copy.wait_send()
-
-
-def gather_all(shards, tall):
+    for copy in stores:
+        copy.wait()
+
+
+def front(sources, pieces, tokens_in, shapes):
     dp, fsdp = lax.axis_size("dp"), lax.axis_size("fsdp")
     n = dp // CORES
     depth = fsdp // n
-    rows = shards[0].shape[0]
-    chunks = []
-    for m, shard in enumerate(shards):
-        r, cols = shard.shape
-        for r0 in range(0, r, rows):
-            for c0 in range(0, cols // WIDTH * WIDTH, WIDTH):
-                nc = WIDTH if c0 + 2 * WIDTH <= cols else cols - c0
-                chunks.append((m, r0, rows, c0, nc, len(chunks) in tall))
+    rows = sources[0].shape[0]
+    pages, length, slots = shapes
+    tokens, D = pages * length, WIDTH
+    chunks = [
+        (m, 0, sources[m].shape[0], c0, nc, group, o0, tall) for m, c0, nc, group, o0, tall in pieces
+    ]
+    groups = [(rows, 4 * D), (rows, 2 * D), (rows, 2 * D), (rows, 4 * D), (4 * rows, D), (rows, 128)]
     t = len(chunks)
-    slots = max(n * n, 2 * depth - 1)
-    shapes = (1, depth - 1, depth - 1, n - 1, n - 1, n * (n - 1), n * (n - 1), slots, slots)
-    shapes += (depth - 1,) * 4
+    slot_count = max(n * n, 2 * depth - 1)
+    shapes_ = (depth - 1, depth - 1, n - 1, n - 1, n * (n - 1), n * (n - 1), slot_count, slot_count)
+    shapes_ += (depth - 1,) * 4
     dma = pltpu.SemaphoreType.DMA
-    outs = pl.pallas_call(
-        functools.partial(gather_kernel, chunks, len(shards)),
-        out_shape=[
-            jax.ShapeDtypeStruct((n, CORES, depth, n) + s.shape, s.dtype) for s in shards
-        ],
-        in_specs=[pl.BlockSpec(memory_space=pltpu.VMEM)] * len(shards),
-        out_specs=[pl.BlockSpec(memory_space=pltpu.HBM)] * len(shards),
-        scratch_shapes=[dma((t,))] + [dma((t, k)) for k in shapes[1:]],
-        compiler_params=pltpu.CompilerParams(collective_id=0, has_side_effects=True),
-    )(*shards)
-    return [o.reshape(dp * fsdp * s.shape[0], s.shape[1]) for o, s in zip(outs, shards)]
+    f32, bf16 = jnp.float32, jnp.bfloat16
+    lead = (n, CORES, depth, n)
+    saved = [
+        ((tokens, D), bf16),
+        ((tokens, 4 * D), bf16),
+        ((tokens, 4 * D), bf16),
+        ((tokens, D), bf16),
+        ((tokens, D), f32),
+        ((tokens, D), bf16),
+        ((tokens, D), bf16),
+        ((tokens, D), bf16),
+        ((pages * slots, 2 * D), bf16),
+        ((tokens, D), f32),
+        ((tokens, D), bf16),
+        ((tokens, D), bf16),
+        ((tokens, 3 * D), bf16),
+    ]
+    small = [((8, D), f32), ((8, D), f32), ((pages * D // HD, length), f32), ((pages * D // HD, length), f32)]
+    hbm = pl.BlockSpec(memory_space=pltpu.HBM)
+    vmem = pl.BlockSpec(memory_space=pltpu.VMEM)
+    smem = pl.BlockSpec(memory_space=pltpu.SMEM)
+    found = pl.pallas_call(
+        functools.partial(front_kernel, shapes, chunks, (len(sources), len(groups))),
+        out_shape=[jax.ShapeDtypeStruct(lead + g, bf16) for g in groups]
+        + [jax.ShapeDtypeStruct(*s) for s in saved + small],
+        in_specs=[vmem] * len(sources) + [hbm] * 3 + [smem] * 2,
+        out_specs=[hbm] * (len(groups) + len(saved)) + [vmem] * 4,
+        scratch_shapes=[pltpu.VMEM(*s) for s in saved]
+        + [
+            pltpu.VMEM((tokens, D), bf16),
+            pltpu.VMEM((tokens, D), bf16),
+            pltpu.VMEM((pages * slots, D), bf16),
+            pltpu.VMEM(lead + groups[1], bf16),
+            pltpu.VMEM(lead + groups[0], bf16),
+            pltpu.VMEM(lead + groups[4], bf16),
+            pltpu.VMEM(lead + groups[5], bf16),
+            pltpu.VMEM((tokens, D), f32),
+            pltpu.VMEM((tokens, 4 * D), f32),
+            pltpu.VMEM((tokens, 4 * D), f32),
+            dma((t,)),
+        ]
+        + [dma((t, k)) for k in shapes_]
+        + [dma((20,)), dma((13,))],
+        compiler_params=pltpu.CompilerParams(
+            collective_id=0, has_side_effects=True, vmem_limit_bytes=67043328
+        ),
+    )(*sources, *tokens_in)
+    weights = [
+        w.reshape(dp * fsdp * g[0], g[1]) for w, g in zip(found[: len(groups)], groups)
+    ]
+    return weights, found[len(groups) : len(groups) + len(saved)], found[len(groups) + len(saved) :]
 
 
 RING = 4
-BLOCK = 256
-SPARE = 3
+SPARE = 2
 
 
 def back_kernel(dims, *refs):
@@ -317,7 +712,7 @@
     grad_outs = take(7)
     gain_out, input_out, memory_out = take(3)
     (hidden, pre, third, out_grad, cross, cctx, second, cq, kv, memory, after_self, ctx, first, qkv, x_bf,
-     w_a, w_b, branch, g_ctx, stage) = take(20)
+     w_a, w_b, branch, g_ctx, stage, g_norm) = take(21)
     send0, got0, parts, got1, halves, got2, line, got3, gain_sum, gain_got = take(10)
     local, s0, r0, s1, r1, s2, r2, s3, r3, gs, gr, free = take(12)
 
@@ -625,7 +1020,7 @@
 
         lax.fori_loop(0, D // (2 * HD), body, 0)
 
-    def norm_back(value_ref, gain_row, grad_of, put):
+    def norm_back(value_ref, gain_row, put):
         gain = gains[pl.ds(gain_row, 1), :]
 
         def body(k, total_):
@@ -635,7 +1030,7 @@
             spread = jnp.mean(centred * centred, axis=-1, keepdims=True)
             row_scale = lax.rsqrt(spread + EPS)
             unit = centred * row_scale
-            grad = grad_of(at)
+            grad = g_norm[at]
             grad_unit = grad * gain
             inner = jnp.mean(grad_unit * unit, axis=-1, keepdims=True)
             put(at, row_scale * (grad_unit - jnp.mean(grad_unit, axis=-1, keepdims=True) - unit * inner))
@@ -644,39 +1039,40 @@
         summed = lax.fori_loop(0, value_ref.shape[0] // 32, body, jnp.zeros((1, D), f32))
         gain_sum[0, pl.ds(gain_row, 1), :] = summed
 
+    def spread(terms):
+        def body(k, carry):
+            at = pl.ds(pl.multiple_of(k * BLOCK, BLOCK), BLOCK)
+            value = None
+            for left, left_col, right, right_col in terms:
+                term = times_transposed(
+                    left[:, pl.ds(left_col, D)], right[at, pl.ds(right_col, D)]
+                )
+                value = term if value is None else value + term
+            g_norm[:, at] = value
+            return carry
+
+        lax.fori_loop(0, D // BLOCK, body, 0)
+
     def second_norm():
         need("self")
-
-        def grad_of(at):
-            return times_transposed(cq[at], w_a[:, pl.ds(0, D)])
+        spread([(cq, 0, w_a, 0)])
 
         def put(at, value):
             value = cross[at] + value
             cross[at] = value
             branch[at] = value.astype(bf16)
 
-        norm_back(after_self, 1, grad_of, put)
+        norm_back(after_self, 1, put)
         fetch("wkv2", wself_in.at[:, pl.ds(D, 2 * D)], w_a, 15)
 
     def first_norm():
         need("x", "wkv2")
-
-        def grad_of(at):
-            value = times_transposed(qkv[at, pl.ds(0, D)], w_b[:, pl.ds(D, D)])
-            return value + times_transposed(qkv[at, pl.ds(D, 2 * D)], w_a_cat(at))
-
-        def w_a_cat(at):
-            return w_a[...]
-
-        def grad_of(at):
-            value = times_transposed(qkv[at, pl.ds(0, D)], w_b[:, pl.ds(D, D)])
-            value = value + times_transposed(qkv[at, pl.ds(D, D)], w_a[:, pl.ds(0, D)])
-            return value + times_transposed(qkv[at, pl.ds(2 * D, D)], w_a[:, pl.ds(D, D)])
+        spread([(qkv, 0, w_b, D), (qkv, D, w_a, 0), (qkv, 2 * D, w_a, D)])
 
         def put(at, value):
             input_out[at] = cross[at] + value
 
-        norm_back(x_bf, 0, grad_of, put)
+        norm_back(x_bf, 0, put)
         fetch("wkv", wkv_in, w_b, 16)
 
     def memory_grad(page, part):
@@ -788,6 +1184,7 @@
         + [pltpu.VMEM((tokens, D), jnp.bfloat16)] * 2
         + [
             pltpu.VMEM((2, -(-slots // 32) * 16 * 8, 128), f32),
+            pltpu.VMEM((tokens, D), f32),
             scratch(SPARE, n, depth, n),
             scratch(RING, n, depth, n),
             scratch(RING, n, n, depth),
@@ -817,56 +1214,6 @@
     )(*big, *small)
 
 
-def split_heads(value):
-    return value.reshape(value.shape[0], value.shape[1], -1, HD)
-
-
-def project(left, weight):
-    return jnp.einsum("bld,de->ble", left, weight, preferred_element_type=jnp.float32)
-
-
-def project_back(grad, weight):
-    return jnp.einsum("ble,de->bld", grad, weight, preferred_element_type=jnp.float32)
-
-
-def normalize(value, gain):
-    centred = value - jnp.mean(value, axis=-1, keepdims=True)
-    spread = jnp.mean(centred * centred, axis=-1, keepdims=True)
-    scale_row = lax.rsqrt(spread + EPS)
-    unit = centred * scale_row
-    return (unit * gain, unit, scale_row)
-
-
-def normalize_back(grad, unit, scale_row, gain):
-    grad_unit = grad * gain
-    grad_gain = jnp.sum(grad * unit, axis=(0, 1))
-    centred = grad_unit - jnp.mean(grad_unit, axis=-1, keepdims=True)
-    grad_input = scale_row * (centred - unit * jnp.mean(grad_unit * unit, axis=-1, keepdims=True))
-    return (grad_input, grad_gain)
-
-
-def masked_scores(queries, keys, allowed):
-    scores = jnp.einsum(
-        "bqhd,bkhd->bhqk",
-        split_heads(queries),
-        split_heads(keys),
-        preferred_element_type=jnp.float32,
-    ) * HD ** (-0.5)
-    return jnp.where(allowed[:, None], scores, -1000000000.0)
-
-
-def attend(queries, keys, values, allowed):
-    scores = masked_scores(queries, keys, allowed)
-    top = jnp.max(scores, axis=-1, keepdims=True)
-    expos = jnp.exp(scores - top)
-    total = jnp.sum(expos, axis=-1, keepdims=True)
-    probs = (expos / total).astype(jnp.bfloat16)
-    context = jnp.einsum(
-        "bhqk,bkhd->bqhd", probs, split_heads(values), preferred_element_type=jnp.float32
-    )
-    return (context.reshape(queries.shape).astype(jnp.bfloat16), top + jnp.log(total))
-
-
 def per_device(
     hidden_in,
     memory,
@@ -887,98 +1234,69 @@
     dense_expand,
     dense_reduce,
 ):
-    inputs = hidden_in[:, 0].astype(jnp.float32)
-    source = memory[:, 0]
-    page_length = lengths[:, 0]
-    page_count = memory_count[:, 0]
-    pages, rows, width = inputs.shape
-    slots = source.shape[1]
-    places = jnp.arange(rows)
-    causal_mask = (places[None, None, :] <= places[None, :, None]) & (
-        places[None, None, :] < page_length[:, None, None]
-    )
-    source_mask = jnp.arange(slots)[None, None, :] < page_count[:, None, None]
+    pages, _, rows, width = hidden_in.shape
+    slots = memory.shape[2]
+    pad = -slots % 16
+    source = jnp.pad(memory[:, 0], ((0, 0), (0, pad), (0, 0)))
 
     def flat(value):
         return value.reshape(pages * value.shape[1], value.shape[2])
 
     gains = jnp.stack([causal_gain, source_gain, dense_gain], axis=1)
     gains = jnp.pad(gains, ((0, 0), (0, 125)))
-    kv_weight, self_weight, qo_weight, expand_weight, reduce_weight = gather_all(
-        [
-            jnp.concatenate([source_key, source_value], axis=1),
-            jnp.concatenate([causal_query, causal_key, causal_value, causal_output, gains], axis=1),
-            jnp.concatenate([source_query, source_output], axis=1),
-            dense_expand,
-            dense_reduce,
-        ],
-        (1, 5, 9),
+    sources = [
+        causal_query,
+        causal_key,
+        causal_value,
+        causal_output,
+        source_key,
+        source_value,
+        source_query,
+        source_output,
+        dense_expand,
+        dense_reduce,
+        gains,
+    ]
+    pieces = [(10, 0, 128, 5, 0, False)]
+    pieces += [(k, 0, width, 0, k * width, False) for k in range(4)]
+    pieces += [(4 + k, 0, width, 1, k * width, False) for k in range(2)]
+    pieces += [(6 + k, 0, width, 2, k * width, False) for k in range(2)]
+    pieces += [(8, k * width, width, 3, k * width, k < 3) for k in range(4)]
+    pieces += [(9, k * BLOCK, BLOCK, 4, k * BLOCK, False) for k in range(4)]
+    tokens = flat(hidden_in[:, 0])
+    branch = flat(cotangent[:, 0])
+    memory_rows = flat(source)
+    page_length, page_count = lengths[:, 0], memory_count[:, 0]
+    weights, saved, small = front(
+        sources,
+        pieces,
+        [tokens, branch, memory_rows, page_count, page_length],
+        (pages, rows, slots + pad),
     )
-    gain_rows = self_weight[:, 4 * width : 4 * width + 3].T.astype(jnp.float32)
-    gain_one, gain_two, gain_three = gain_rows[0], gain_rows[1], gain_rows[2]
-    qkv_weight = self_weight[:, : 3 * width]
-    out_weight = self_weight[:, 3 * width : 4 * width]
-    source_query_weight, source_out_weight = qo_weight[:, :width], qo_weight[:, width:]
-
-    memory_both = project(source, kv_weight).astype(jnp.bfloat16)
-    memory_keys, memory_values = memory_both[..., :width], memory_both[..., width:]
-    normed, unit_one, scale_one = normalize(inputs, gain_one)
-    first = normed.astype(jnp.bfloat16)
-    qkv = project(first, qkv_weight).astype(jnp.bfloat16)
-    queries, keys, values = (qkv[..., i * width : (i + 1) * width] for i in range(3))
-    context, logsum_self = attend(queries, keys, values, causal_mask)
-    after_self = inputs + project(context, out_weight)
-    normed, unit_two, scale_two = normalize(after_self, gain_two)
-    second = normed.astype(jnp.bfloat16)
-    cross_queries = project(second, source_query_weight).astype(jnp.bfloat16)
-    cross_context, logsum_cross = attend(cross_queries, memory_keys, memory_values, source_mask)
-    after_cross = after_self + project(cross_context, source_out_weight)
-    normed, unit_three, scale_three = normalize(after_cross, gain_three)
-    third = normed.astype(jnp.bfloat16)
-    hidden_pre = project(third, expand_weight)
-    hidden = jax.nn.gelu(hidden_pre, approximate=False).astype(jnp.bfloat16)
-    result = after_cross + project(hidden, reduce_weight)
-
-    grad_out = cotangent[:, 0].astype(jnp.float32)
-    grad_branch = grad_out.astype(jnp.bfloat16)
-    grad_hidden = project_back(grad_branch, reduce_weight)
-    _, gelu_pull = jax.vjp(lambda v: jax.nn.gelu(v, approximate=False), hidden_pre)
-    grad_pre = gelu_pull(grad_hidden)[0].astype(jnp.bfloat16)
-    grad_norm, grad_gain_three = normalize_back(
-        project_back(grad_pre, expand_weight), unit_three, scale_three, gain_three
-    )
-    grad_cross = grad_out + grad_norm
-
-    pad = -slots % 16
-    both = jnp.pad(memory_both, ((0, 0), (0, pad), (0, 0)))
+    self_weight, kv_weight, qo_weight, _, _, _ = weights
+    result, hidden, pre, third, cross_grad, cctx, second, cq, kv, after_self, ctx, first, qkv = saved
+    gain_rows, gain_three, lse_cross, lse_self = small
     big = [
-        flat(hidden),
-        flat(grad_pre),
-        flat(third),
-        flat(grad_branch),
-        flat(grad_cross),
-        flat(cross_context),
-        flat(second),
-        flat(cross_queries),
-        flat(both),
-        flat(jnp.pad(source, ((0, 0), (0, pad), (0, 0)))),
-        flat(after_self),
-        flat(context),
-        flat(first),
-        flat(qkv),
-        flat(hidden_in[:, 0]),
+        hidden,
+        pre,
+        third,
+        branch,
+        cross_grad,
+        cctx,
+        second,
+        cq,
+        kv,
+        memory_rows,
+        after_self,
+        ctx,
+        first,
+        qkv,
+        tokens,
         qo_weight,
         kv_weight,
         self_weight,
     ]
-    small = [
-        page_count,
-        page_length,
-        jnp.pad(gain_rows, ((0, 5), (0, 0))),
-        jnp.pad(grad_gain_three[None], ((2, 5), (0, 0))),
-        logsum_cross.reshape(-1, rows),
-        logsum_self.reshape(-1, rows),
-    ]
+    small = [page_count, page_length, gain_rows, gain_three, lse_cross, lse_self]
     (
         grad_reduce,
         grad_expand,
@@ -995,7 +1313,7 @@
     me = lax.axis_index("dp") * lax.axis_size("fsdp") + lax.axis_index("fsdp")
     grad_gains = lax.dynamic_slice_in_dim(grad_gains, me * entries, entries, axis=1)
     return (
-        result.astype(jnp.bfloat16)[:, None],
+        result.reshape(hidden_in.shape),
         grad_inputs.reshape(pages, 1, rows, width),
         grad_memory.reshape(memory.shape),
         grad_gains[0],

time: 475 us -> 384 us (0.81); the launches traced: 467 us -> 384 us
  matrix products: 57 us -> 0 us
  local copies, waits for them, and re-layouts: 55.6 us -> 23.8 us
  Pallas kernels: 330 us -> 359 us
  other arithmetic: 22.8 us -> 0.01 us
    dot_general x13 -> x0, matrix products: 57 us -> none  [the longest x7 32.1 us: project(): jnp.einsum('bld,de->ble', left, weight, preferred_element_type=jnp.float32)]
    pallas_call x1, Pallas kernels: 143 us -> 185 us  [front(): pl.pallas_call(functools.partial(front_kernel, shapes, chunks, (len(sourc...]
    slice x9 -> x0, local copies, waits for them, and re-layouts: 18 us -> none  [the longest x2 7.45 us: per_device(): memory_both[..., :width]]
    convert_element_type x5 -> x0, other arithmetic: 12.9 us -> none  [the longest x1 10.4 us: per_device(): hidden = jax.nn.gelu(hidden_pre, approximate=False).astype(jnp.bfloat16)]
    pallas_call x1, Pallas kernels: 187 us -> 174 us  [backward(): pl.pallas_call(functools.partial(back_kernel, (pages, length, slots)), ou...]
    pad x4 -> x2, local copies, waits for them, and re-layouts: 8.46 us -> 2.29 us  [the longest x1 1.68 us: per_device(): source = jnp.pad(memory[:, 0], ((0, 0), (0, pad), (0, 0)))]
    convert_element_type x5 -> x0, local copies, waits for them, and re-layouts: 4.91 us -> none  [the longest x4 4.64 us: attend(): context.reshape(queries.shape).astype(jnp.bfloat16)]
    unnamed x68 -> x25, local copies, waits for them, and re-layouts: 20.3 us -> 18.2 us
where the time goes in v4:
time: 384 us
  Pallas kernels  359 us (93%)
  local copies, waits for them, and re-layouts  23.8 us (6%)
    pallas_call x1, Pallas kernels, front(): pl.pallas_call(functools.partial(front_kernel, shapes, chunks, (len(sourc...  185 us
    pallas_call x1, Pallas kernels, backward(): pl.pallas_call(functools.partial(back_kernel, (pages, length, slots)), ou...  174 us
    unnamed x25, local copies, waits for them, and re-layouts  18.2 us

profile of v4, /device:TPU:0, one launch (start us, length us, event | category | flops | bytes accessed | tf_op | source)
XLA Modules:
  0.0 383.8 jit_solution(16061364980644647722)
XLA Ops:
  0.6 0.0 copy-start.5
  0.7 0.0 copy-start.6
  0.7 0.0 copy-start.7
  0.7 2.4 copy.53
  3.1 1.7 pad.9.clone
  4.8 0.0 copy-done.5
  4.8 0.0 copy-done.6
  4.8 0.0 copy-done.7
  4.8 0.1 copy.48
  4.9 0.6 pad.8.refs_10_
  5.5 185.1 %shard_map.297 = (bf16[2,2,4,2,32,4096]{5,4,3,2,1,0:T(8,128)(2,1)}, bf16[2,2,4,2,32,2048]{5,4,3,2,1,0:T(8,128)(2,1)}, bf16[2,2,4,2,32,2048]{5,4,3,2,1,0:T(8,128)...) custom-call(bf16[32,1024]{1,0:T(8,128)(2,1)} %refs_0_.1, ...), custom_call_target="tpu_custom_call" | custom-call | tf_op jit(solution)/shard_map/pallas_call | solution.py:666
  190.6 174.1 %shard_map.298 = (f32[128,1024]{1,0:T(8,128)}, f32[32,4096]{1,0:T(8,128)}, f32[32,1024]{1,0:T(8,128)}, f32[32,1024]{1,0:T(8,128)}, f32[32,2048]{1,0:T(8,128)}, /...) custom-call(bf16[256,4096]{1,0:T(8,128)(2,1)} %get-tuple-element.47., ...), custom_call_target="tpu_custom_call" | custom-call | tf_op jit(solution)/shard_map/pallas_call | solution.py:1172
  364.7 2.0 fusion
  366.7 0.8 constant_dynamic-slice_fusion
  367.5 0.5 slice_bitcast_fusion
  368.0 1.9 copy.62
  369.9 2.3 copy.63
  372.2 0.0 copy-start.4
  372.2 0.0 copy-start.3
  372.2 0.0 copy-start.2
  372.2 0.0 copy-start
  372.2 8.0 %copy.64 = f32[2,1,588,1024]{3,1,2,0:T(1,128)} copy(f32[2,1,588,1024]{3,1,2,0:T(1,128)} %bitcast.28) | data formatting | bytes 9633792
  380.2 0.0 copy-done.4
  380.2 0.7 copy.65
  380.9 0.0 copy-done.3
  380.9 0.7 copy.66
  381.5 0.0 copy-done.2
  381.5 0.7 copy.67
  382.2 0.0 copy-done.1
  382.2 0.8 copy.68
  383.0 0.0 copy-done
  383.0 0.8 copy.69
  (2 shorter events, 0.0 us)
Async XLA Ops:
  0.6 4.1 %copy-start.5 = (bf16[32]{0:T(256)(128)(2,1)S(1)}, bf16[32]{0:T(256)(128)(2,1)}, u32[]{:S(2)}) copy-start(bf16[32]{0:T(256)(128)(2,1)} %param.33) | copy-start | bytes 196
  0.7 4.1 %copy-start.6 = (bf16[32]{0:T(256)(128)(2,1)S(1)}, bf16[32]{0:T(256)(128)(2,1)}, u32[]{:S(2)}) copy-start(bf16[32]{0:T(256)(128)(2,1)} %param.28) | copy-start | bytes 196
  0.7 4.1 %copy-start.7 = (bf16[32]{0:T(256)(128)(2,1)S(1)}, bf16[32]{0:T(256)(128)(2,1)}, u32[]{:S(2)}) copy-start(bf16[32]{0:T(256)(128)(2,1)} %param.23) | copy-start | bytes 196
  372.2 8.0 %copy-start.4 = (f32[32,1024]{1,0:T(8,128)S(1)}, f32[32,1024]{1,0:T(8,128)}, u32[]{:S(2)}) copy-start(f32[32,1024]{1,0:T(8,128)} %get-tuple-element.157) | copy-start | bytes 393220
  372.2 8.7 %copy-start.3 = (f32[32,1024]{1,0:T(8,128)S(1)}, f32[32,1024]{1,0:T(8,128)}, u32[]{:S(2)}) copy-start(f32[32,1024]{1,0:T(8,128)} %get-tuple-element.159) | copy-start | bytes 393220
  372.2 9.3 %copy-start.2 = (f32[32,1024]{1,0:T(8,128)S(1)}, f32[32,1024]{1,0:T(8,128)}, u32[]{:S(2)}) copy-start(f32[32,1024]{1,0:T(8,128)} %get-tuple-element.162) | copy-start | bytes 393220
  372.2 10.0 %copy-start.1 = (f32[32,4096]{1,0:T(8,128)S(1)}, f32[32,4096]{1,0:T(8,128)}, u32[]{:S(2)}) copy-start(f32[32,4096]{1,0:T(8,128)} %get-tuple-element.164) | copy-start | bytes 1572868
  372.2 10.8 %copy-start = (f32[128,1024]{1,0:T(8,128)S(1)}, f32[128,1024]{1,0:T(8,128)}, u32[]{:S(2)}) copy-start(f32[128,1024]{1,0:T(8,128)} %get-tuple-element.165) | copy-start | bytes 1572868
